TPU v7x, 32 devices: a whole 2x2x4 slice. The times are simulated.
32 devices in a mesh: chan: 8 (over y, x, core), band: 4 (over z).
Axes of the slice: x: 2, y: 2, z: 4, core: 2. Of those that a mesh axis runs over, the one named last changes fastest.
Arguments:
- spectra: bfloat16 [96, 2048, 384], P('band', 'chan')
- half_width: int32 [2048], P('chan'), may hold values from 4 to 12
- partner: int32 [2, 8], replicated, may hold values from 0 to 7, as said below
Outputs:
- cross: bfloat16 [3, 96, 2048, 512], P(None, 'band', 'chan')
Inputs may be any that keep to these rules, and one draw needn't show every extreme that they name: Each row pairs the blocks: partner[r, partner[r, a]] = a and partner[r, a] != a; no two rows pair the same two blocks.
All inputs are finite; a program needn't handle non-finite values.
Results may differ from a plain program's by a relative error of at most 0.0056.
Values may be sent and summed in bfloat16 or wider, within the bound.
No kernel may reach another device: no remote copies, remote signals or barrier semaphores. Data moves between devices by JAX's collectives and lax.ppermute only.
A program may use at most 128 MiB of HBM per device.

v0:
```python
import jax
import jax.numpy as jnp
from jax import lax
from jax.sharding import PartitionSpec as P

HMAX = 12
ROUNDS = 2


def padded_2(cells, sides, width):
    for axis, dim in sides:
        count = lax.axis_size(axis)
        ends = count - 1
        head = lax.slice_in_dim(cells, 0, width, axis=dim)
        tail = lax.slice_in_dim(cells, cells.shape[dim] - width, cells.shape[dim], axis=dim)
        cells = jnp.concatenate(
            [
                lax.ppermute(tail, axis, [(i, (i + 1) % count) for i in range(ends)]),
                cells,
                lax.ppermute(head, axis, [((i + 1) % count, i) for i in range(ends)]),
            ],
            axis=dim,
        )
    return cells


def pair_block(own, other, windows):
    turned = jnp.concatenate([-other[:, :, windows:], other[:, :, :windows]], axis=2)
    right = jnp.concatenate([other, turned], axis=1)
    product = jnp.einsum("fcw,fdw->fcd", own, right, preferred_element_type=jnp.float32)
    return (product * (1.0 / windows)).astype(jnp.bfloat16)


def body(spectra, half_width, partner):
    bins, chans, columns = spectra.shape
    windows = columns // 2
    raw = spectra.astype(jnp.float32)
    power = jnp.sum(raw * raw, axis=2)
    padded = padded_2(power, (("band", 0),), HMAX)
    first = lax.axis_index("band") * bins - HMAX
    position = first + jnp.arange(bins + 2 * HMAX, dtype=jnp.int32)
    present = ((position >= 0) & (position < bins * lax.axis_size("band"))).astype(jnp.float32)[
        :, None
    ]
    total = jnp.zeros((bins, chans), jnp.float32)
    count = jnp.zeros((bins, chans), jnp.float32)
    for offset in range(-HMAX, HMAX + 1):
        inside = (abs(offset) <= half_width).astype(jnp.float32)[None, :]
        total = total + padded[HMAX + offset : HMAX + offset + bins] * inside
        count = count + present[HMAX + offset : HMAX + offset + bins] * inside
    scale = lax.rsqrt(total / (2.0 * windows * count) + 1e-06)
    white = (raw * scale[:, :, None]).astype(jnp.bfloat16)
    blocks = lax.axis_size("chan")
    piece = chans // blocks
    sectioned = white.reshape(bins, blocks, piece, columns)
    results = [pair_block(white, white, windows)]
    for step in range(ROUNDS):
        held = lax.all_to_all(sectioned, "chan", split_axis=1, concat_axis=1, tiled=True)
        chosen = jnp.take(held, partner[step], axis=1)
        other = lax.all_to_all(chosen, "chan", split_axis=1, concat_axis=1, tiled=True)
        results.append(pair_block(white, other.reshape(bins, chans, columns), windows))
    return jnp.stack(results)


def solution(mesh):
    placed = (P("band", "chan", None), P("chan"), P())
    return jax.shard_map(
        body, mesh=mesh, in_specs=placed, out_specs=P(None, "band", "chan", None), check_vma=False
    )
```

profile of v0, /device:TPU:0, one launch (start us, length us, event | category | flops | bytes accessed | tf_op | source)
XLA Modules:
  0.0 252.5 jit_solution(4837852159365645081)
XLA Ops:
  0.0 0.0 copy-start.3
  0.0 3.4 %fusion = f32[24,256]{1,0:T(8,128)S(1)} fusion(bf16[24,256,384]{2,1,0:T(8,128)(2,1)} %param.5), kind=kLoop, calls=%fused_computation.8 | loop fusion | flops 7071744 | bytes 4743168 | tf_op jit(solution)/shard_map/reduce_sum | solution.py:38
  3.4 5.0 %collective-permute-start = (f32[12,256]{1,0:T(8,128)S(1)}, f32[12,256]{1,0:T(8,128)S(1)}, u32[]{:S(2)}, u32[]{:S(2)}) collective-permute-start(f32[12,256]{1,0:T(8,128)S(1)} %get-tuple-element.16), channel_id=1, source_target_pairs={{0,1},{1,2},{2,3},{4,5},{5,6},{6,7},{8,9},{9,10},{10,11},{12,13},{... | collective-permute-start | bytes 36872 | tf_op jit(solution)/shard_map/ppermute | solution.py:18
  8.3 1.3 collective-permute-start.1
  9.7 0.1 fusion.106
  9.7 0.0 copy-done.3
  9.8 0.1 fusion.107
  9.8 0.0 collective-permute-done
  9.8 4.1 %collective-permute-done.1 = f32[12,256]{1,0:T(8,128)S(1)} collective-permute-done((f32[12,256]{1,0:T(8,128)S(1)}, f32[12,256]{1,0:T(8,128)S(1)}, u32[]{:S(2)}, u32[]{:S(2)}) %collective-permute-start.1) | collective-permute-done | bytes 12320 | tf_op jit(solution)/shard_map/ppermute | solution.py:20
  14.0 0.2 fusion.101
  14.2 2.9 %fusion.1 = bf16[24,256,384]{2,1,0:T(8,128)(2,1)S(1)} fusion(bf16[24,256,384]{2,1,0:T(8,128)(2,1)} %param.5, f32[24,256]{1,0:T(8,128)S(1)} %fusion.101), kind=kLoop, calls=%fused_computation.9 | loop fusion | flops 7077888 | bytes 9461760 | tf_op jit(solution)/shard_map/convert_element_type | solution.py:52
  17.1 0.0 copy-start
  17.1 2.2 copy-done
  19.3 2.7 %copy.6 = bf16[24,8,32,384]{3,2,0,1:T(8,128)(2,1)} copy(bf16[24,8,32,384]{3,2,1,0:T(8,128)(2,1)S(1)} %bitcast.22) | data formatting | bytes 9437184 | tf_op jit(solution)/shard_map/reshape | solution.py:55
  22.0 0.0 copy-start.4
  22.0 4.7 %all-to-all-start = ((bf16[24,8,32,384]{3,2,0,1:T(8,128)(2,1)}), bf16[24,8,32,384]{3,2,0,1:T(8,128)(2,1)}, u32[]{:S(2)}, u32[]{:S(2)}) async-start(bf16[24,8,32,384]{3,2,0,1:T(8,128)(2,1)} %copy.6), calls=%async_computation | async-start | bytes 9437184 | tf_op jit(solution)/shard_map/all_to_all | solution.py:58
  26.7 0.0 copy-done.4
  26.8 54.7 %all-to-all-done = bf16[24,8,32,384]{3,2,0,1:T(8,128)(2,1)} async-done(((bf16[24,8,32,384]{3,2,0,1:T(8,128)(2,1)}), bf16[24,8,32,384]{3,2,0,1:T(8,128)(2,1)}, u32[]{:S(2)}, u32[]{:S(2)}) %all-to-all-start) | async-done | bytes 4718624 | tf_op jit(solution)/shard_map/all_to_all | solution.py:58
  81.4 5.7 %gather_fusion = bf16[8,24,32,384]{3,2,1,0:T(8,128)(2,1)} fusion(bf16[24,8,32,384]{3,2,0,1:T(8,128)(2,1)} %all-to-all-done, s32[1024]{0:T(1024)S(1)} %pad_clamp_fusion.1), kind=kCustom, calls=%fused_computation.clone | custom fusion | bytes 9437216 | tf_op jit(solution)/shard_map/jit(_take)/gather | solution.py:59
  87.1 5.1 %select_bitcast_fusion.1 = bf16[24,8,32,384]{3,2,0,1:T(8,128)(2,1)} fusion(bf16[8,24,32,384]{3,2,1,0:T(8,128)(2,1)} %gather_fusion, pred[8]{0:T(512)(128)(4,1)S(1)} %get-tuple-element.6), kind=kLoop, calls=%fused_computation.32 | loop fusion | flops 2359296 | bytes 9437192 | tf_op jit(solution)/shard_map/jit(_take)/select_n | solution.py:59
  92.2 4.6 %all-to-all-start.1 = ((bf16[24,8,32,384]{3,2,0,1:T(8,128)(2,1)}), bf16[24,8,32,384]{3,2,0,1:T(8,128)(2,1)}, u32[]{:S(2)}, u32[]{:S(2)}) async-start(bf16[24,8,32,384]{3,2,0,1:T(8,128)(2,1)} %select_bitcast_fusion.1), calls=%async_computation.1 | async-start | bytes 9437184 | tf_op jit(solution)/shard_map/all_to_all | solution.py:60
  96.8 5.8 %gather_fusion.1 = bf16[8,24,32,384]{3,2,1,0:T(8,128)(2,1)} fusion(bf16[24,8,32,384]{3,2,0,1:T(8,128)(2,1)} %all-to-all-done, s32[1024]{0:T(1024)S(1)} %pad_clamp_fusion), kind=kCustom, calls=%fused_computation.1.clone | custom fusion | bytes 9437216 | tf_op jit(solution)/shard_map/jit(_take)/gather | solution.py:59
  102.6 5.2 %select_bitcast_fusion = bf16[24,8,32,384]{3,2,0,1:T(8,128)(2,1)} fusion(bf16[8,24,32,384]{3,2,1,0:T(8,128)(2,1)} %gather_fusion.1, pred[8]{0:T(512)(128)(4,1)S(1)} %get-tuple-element.18), kind=kLoop, calls=%fused_computation.31 | loop fusion | flops 2359296 | bytes 9437192 | tf_op jit(solution)/shard_map/jit(_take)/select_n | solution.py:59
  107.8 43.7 %all-to-all-done.1 = bf16[24,8,32,384]{3,2,0,1:T(8,128)(2,1)} async-done(((bf16[24,8,32,384]{3,2,0,1:T(8,128)(2,1)}), bf16[24,8,32,384]{3,2,0,1:T(8,128)(2,1)}, u32[]{:S(2)}, u32[]{:S(2)}) %all-to-all-start.1) | async-done | bytes 4718624 | tf_op jit(solution)/shard_map/all_to_all | solution.py:60
  151.5 0.0 slice-start
  151.5 4.9 %all-to-all-start.2 = ((bf16[24,8,32,384]{3,2,0,1:T(8,128)(2,1)}), bf16[24,8,32,384]{3,2,0,1:T(8,128)(2,1)}, u32[]{:S(2)}, u32[]{:S(2)}) async-start(bf16[24,8,32,384]{3,2,0,1:T(8,128)(2,1)} %select_bitcast_fusion), calls=%async_computation.2 | async-start | bytes 9437184 | tf_op jit(solution)/shard_map/all_to_all | solution.py:60
  156.5 0.0 slice-start.1
  156.5 6.6 %slice_negate_fusion.2 = (bf16[24,256,192]{2,1,0:T(8,128)(2,1)}, bf16[24,256,192]{2,1,0:T(8,128)(2,1)}) fusion(bf16[24,256,384]{2,1,0:T(8,128)(2,1)} %copy-done), kind=kLoop, calls=%fused_computation.35 | loop fusion | flops 1179648 | bytes 9437184 | tf_op jit(solution)/shard_map/neg | solution.py:28
  163.1 0.0 slice-done
  163.1 0.0 slice-done.1
  163.1 8.0 %fusion.20 = bf16[1,24,256,512]{3,2,1,0:T(8,128)(2,1)} fusion(bf16[24,256,384]{2,1,0:T(8,128)(2,1)S(1)} %bitcast.24, bf16[24,256,192]{2,1,0:T(8,128)(2,1)} %get-tuple-element.11, bf16[24,256,192]{2,1,0:T(8,128)(2,1)} %get-tuple-element.10), kind=kOutput, calls=%fused_computation.28 | convolution fusion | flops 2450522112 | bytes 15728640 | tf_op jit(solution)/shard_map/fcw,fdw->fcd/dot_general | solution.py:30
  171.2 3.2 %copy.7 = bf16[24,8,32,384]{3,2,1,0:T(8,128)(2,1)S(1)} copy(bf16[24,8,32,384]{3,2,0,1:T(8,128)(2,1)} %all-to-all-done.1) | data formatting | bytes 9437184 | tf_op jit(solution)/shard_map/all_to_all | solution.py:60
  174.4 0.0 copy-start.1
  174.4 2.2 copy-done.1
  176.5 3.7 %slice_negate_fusion.1 = (bf16[24,256,192]{2,1,0:T(8,128)(2,1)}, bf16[24,256,192]{2,1,0:T(8,128)(2,1)}) fusion(bf16[24,256,384]{2,1,0:T(8,128)(2,1)S(1)} %bitcast.27), kind=kLoop, calls=%fused_computation.34 | loop fusion | flops 1179648 | bytes 9437184 | tf_op jit(solution)/shard_map/neg | solution.py:28
  180.3 30.7 %all-to-all-done.2 = bf16[24,8,32,384]{3,2,0,1:T(8,128)(2,1)} async-done(((bf16[24,8,32,384]{3,2,0,1:T(8,128)(2,1)}), bf16[24,8,32,384]{3,2,0,1:T(8,128)(2,1)}, u32[]{:S(2)}, u32[]{:S(2)}) %all-to-all-start.2) | async-done | bytes 4718624 | tf_op jit(solution)/shard_map/all_to_all | solution.py:60
  211.0 0.0 slice-start.2
  211.0 3.3 %copy.8 = bf16[24,8,32,384]{3,2,1,0:T(8,128)(2,1)S(1)} copy(bf16[24,8,32,384]{3,2,0,1:T(8,128)(2,1)} %all-to-all-done.2) | data formatting | bytes 9437184 | tf_op jit(solution)/shard_map/all_to_all | solution.py:60
  214.3 0.0 copy-start.2
  214.4 0.0 slice-start.3
  214.4 4.0 %slice_negate_fusion = (bf16[24,256,192]{2,1,0:T(8,128)(2,1)}, bf16[24,256,192]{2,1,0:T(8,128)(2,1)}) fusion(bf16[24,256,384]{2,1,0:T(8,128)(2,1)S(1)} %bitcast.29), kind=kLoop, calls=%fused_computation.33 | loop fusion | flops 1179648 | bytes 9437184 | tf_op jit(solution)/shard_map/neg | solution.py:28
  218.4 0.0 copy-done.2
  218.4 0.0 slice-done.2
  218.4 0.0 slice-done.3
  218.4 8.8 %fusion.21 = bf16[1,24,256,512]{3,2,1,0:T(8,128)(2,1)} fusion(bf16[24,256,384]{2,1,0:T(8,128)(2,1)S(1)} %bitcast.26, bf16[24,256,192]{2,1,0:T(8,128)(2,1)} %get-tuple-element.13, bf16[24,256,192]{2,1,0:T(8,128)(2,1)} %get-tuple-element.12, bf16[24,256,384]{2,1,0:T(8,128)(2,1)} %bitcast.28), kind=kOutput, calls=%fused_computation.29 | convolution fusion | flops 2450522112 | bytes 20447232 | tf_op jit(solution)/shard_map/fcw,fdw->fcd/dot_general | solution.py:30
  227.2 8.8 %fusion.22 = bf16[1,24,256,512]{3,2,1,0:T(8,128)(2,1)} fusion(bf16[24,256,384]{2,1,0:T(8,128)(2,1)S(1)} %bitcast.26, bf16[24,256,192]{2,1,0:T(8,128)(2,1)} %get-tuple-element.15, bf16[24,256,192]{2,1,0:T(8,128)(2,1)} %get-tuple-element.14, bf16[24,256,384]{2,1,0:T(8,128)(2,1)} %bitcast.30), kind=kOutput, calls=%fused_computation.30 | convolution fusion | flops 2450522112 | bytes 20447232 | tf_op jit(solution)/shard_map/fcw,fdw->fcd/dot_general | solution.py:30
  236.0 16.5 %pad_maximum_fusion = bf16[3,24,256,512]{3,2,1,0:T(8,128)(2,1)} fusion(bf16[1,24,256,512]{3,2,1,0:T(8,128)(2,1)} %fusion.22, bf16[1,24,256,512]{3,2,1,0:T(8,128)(2,1)} %fusion.21, bf16[1,24,256,512]{3,2,1,0:T(8,128)(2,1)} %fusion.20), kind=kLoop, calls=%fused_computation.2 | loop fusion | flops 18874368 | bytes 37748736 | tf_op jit(solution)/shard_map/stack | solution.py:62
  (8 shorter events, 0.0 us)
Async XLA Ops:
  0.0 9.7 %copy-start.3 = (s32[256]{0:T(256)S(1)}, s32[256]{0:T(256)}, u32[]{:S(2)}) copy-start(s32[256]{0:T(256)} %param.6) | copy-start | bytes 3076
  3.4 6.5 %collective-permute-start = (f32[12,256]{1,0:T(8,128)S(1)}, f32[12,256]{1,0:T(8,128)S(1)}, u32[]{:S(2)}, u32[]{:S(2)}) collective-permute-start(f32[12,256]{1,0:T(8,128)S(1)} %get-tuple-element.16), channel_id=1, source_target_pairs={{0,1},{1,2},{2,3},{4,5},{5,6},{6,7},{8,9},{9,10},{10,11},{12,13},{... | collective-permute-start | bytes 36872 | tf_op jit(solution)/shard_map/ppermute | solution.py:18
  8.3 5.6 %collective-permute-start.1 = (f32[12,256]{1,0:T(8,128)S(1)}, f32[12,256]{1,0:T(8,128)S(1)}, u32[]{:S(2)}, u32[]{:S(2)}) collective-permute-start(f32[12,256]{1,0:T(8,128)S(1)} %get-tuple-element.17), channel_id=1, source_target_pairs={{1,0},{2,1},{3,2},{5,4},{6,5},{7,6},{9,8},{10,9},{11,10},{13,12},{... | collective-permute-start | bytes 36872 | tf_op jit(solution)/shard_map/ppermute | solution.py:20
  17.1 2.2 copy-start
  22.0 4.8 %copy-start.4 = (s32[2,8]{1,0:T(2,128)S(1)}, s32[2,8]{1,0:T(2,128)}, u32[]{:S(2)}) copy-start(s32[2,8]{1,0:T(2,128)} %param.7) | copy-start | bytes 196
  22.0 59.5 %all-to-all-start = ((bf16[24,8,32,384]{3,2,0,1:T(8,128)(2,1)}), bf16[24,8,32,384]{3,2,0,1:T(8,128)(2,1)}, u32[]{:S(2)}, u32[]{:S(2)}) async-start(bf16[24,8,32,384]{3,2,0,1:T(8,128)(2,1)} %copy.6), calls=%async_computation | async-start | bytes 9437184 | tf_op jit(solution)/shard_map/all_to_all | solution.py:58
  92.2 59.3 %all-to-all-start.1 = ((bf16[24,8,32,384]{3,2,0,1:T(8,128)(2,1)}), bf16[24,8,32,384]{3,2,0,1:T(8,128)(2,1)}, u32[]{:S(2)}, u32[]{:S(2)}) async-start(bf16[24,8,32,384]{3,2,0,1:T(8,128)(2,1)} %select_bitcast_fusion.1), calls=%async_computation.1 | async-start | bytes 9437184 | tf_op jit(solution)/shard_map/all_to_all | solution.py:60
  151.5 11.6 %slice-start = ((s8[4718592]{0:T(1024)(128)(4,1)}), s8[524288]{0:T(1024)(128)(4,1)S(1)}, s32[]{:S(2)}) async-start(s8[4718592]{0:T(1024)(128)(4,1)} %bitcast.23), calls=%async_computation.3 | async-start | bytes 1048576
  151.5 59.5 %all-to-all-start.2 = ((bf16[24,8,32,384]{3,2,0,1:T(8,128)(2,1)}), bf16[24,8,32,384]{3,2,0,1:T(8,128)(2,1)}, u32[]{:S(2)}, u32[]{:S(2)}) async-start(bf16[24,8,32,384]{3,2,0,1:T(8,128)(2,1)} %select_bitcast_fusion), calls=%async_computation.2 | async-start | bytes 9437184 | tf_op jit(solution)/shard_map/all_to_all | solution.py:60
  156.5 6.7 %slice-start.1 = ((s8[4718592]{0:T(1024)(128)(4,1)}), s8[4194304]{0:T(1024)(128)(4,1)S(1)}, s32[]{:S(2)}) async-start(s8[4718592]{0:T(1024)(128)(4,1)} %bitcast.23), calls=%async_computation.4 | async-start | bytes 8388608
  174.4 2.2 copy-start.1
  211.0 7.4 %slice-start.2 = ((s8[4718592]{0:T(1024)(128)(4,1)}), s8[4194304]{0:T(1024)(128)(4,1)S(1)}, s32[]{:S(2)}) async-start(s8[4718592]{0:T(1024)(128)(4,1)} %bitcast.25), calls=%async_computation.5 | async-start | bytes 8388608
  214.3 4.1 %copy-start.2 = (bf16[24,8,32,384]{3,2,1,0:T(8,128)(2,1)}, bf16[24,8,32,384]{3,2,1,0:T(8,128)(2,1)S(1)}, u32[]{:S(2)}) copy-start(bf16[24,8,32,384]{3,2,1,0:T(8,128)(2,1)S(1)} %copy.8) | copy-start | bytes 14155780
  214.4 4.1 %slice-start.3 = ((s8[4718592]{0:T(1024)(128)(4,1)}), s8[524288]{0:T(1024)(128)(4,1)S(1)}, s32[]{:S(2)}) async-start(s8[4718592]{0:T(1024)(128)(4,1)} %bitcast.25), calls=%async_computation.6 | async-start | bytes 1048576
where the time goes:
time: 253 us
  waiting for transfers between devices  133 us (53%)
  other arithmetic  47.6 us (19%)
  matrix products  25.6 us (10%)
  local copies, waits for them, and re-layouts  25.3 us (10%)
  starting transfers between devices  20.5 us (8%)
    all_to_all x2, waiting for transfers between devices, body(): lax.all_to_all(chosen, 'chan', split_axis=1, concat_axis=1, tiled=True)  74.5 us
    all_to_all x1, waiting for transfers between devices, body(): lax.all_to_all(sectioned, 'chan', split_axis=1, concat_axis=1, tiled=True)  54.7 us
    dot_general x3, matrix products, pair_block(): jnp.einsum('fcw,fdw->fcd', own, right, preferred_element_type=jnp.float32)  25.6 us
    another operation x1, other arithmetic, body(): return jnp.stack(results)  16.5 us
    neg x3, other arithmetic, pair_block(): -other[:, :, windows:]  14.4 us
    gather x2, local copies, waits for them, and re-layouts, body(): chosen = jnp.take(held, partner[step], axis=1)  11.5 us
    select_n x2, other arithmetic, body(): chosen = jnp.take(held, partner[step], axis=1)  10.2 us
    all_to_all x2, starting transfers between devices, body(): lax.all_to_all(chosen, 'chan', split_axis=1, concat_axis=1, tiled=True)  9.53 us
  transfers between devices with their start and end apart: 5, of which 4 were waited for; matrix products, arithmetic and copies ran while one was open for 13% of the time, Pallas kernels for 0%

commit v1 on v0

--- a/solution.py
+++ b/solution.py
@@ -1,10 +1,18 @@
+import functools
+
 import jax
 import jax.numpy as jnp
 from jax import lax
+from jax.experimental import pallas as pl
+from jax.experimental.pallas import tpu as pltpu
 from jax.sharding import PartitionSpec as P
+
 
 HMAX = 12
 ROUNDS = 2
+CORE = 1
+AXIS_X = 2
+AXIS_Y = 4
 
 
 def padded_2(cells, sides, width):
@@ -31,7 +39,7 @@
     return (product * (1.0 / windows)).astype(jnp.bfloat16)
 
 
-def body(spectra, half_width, partner):
+def whitening_scale(spectra, half_width):
     bins, chans, columns = spectra.shape
     windows = columns // 2
     raw = spectra.astype(jnp.float32)
@@ -48,8 +56,17 @@
         inside = (abs(offset) <= half_width).astype(jnp.float32)[None, :]
         total = total + padded[HMAX + offset : HMAX + offset + bins] * inside
         count = count + present[HMAX + offset : HMAX + offset + bins] * inside
-    scale = lax.rsqrt(total / (2.0 * windows * count) + 1e-06)
-    white = (raw * scale[:, :, None]).astype(jnp.bfloat16)
+    return lax.rsqrt(total / (2.0 * windows * count) + 1e-06)
+
+
+def whitened(raw, scale):
+    return (raw.astype(jnp.float32) * scale[..., None]).astype(jnp.bfloat16)
+
+
+def general_body(spectra, half_width, partner):
+    bins, chans, columns = spectra.shape
+    windows = columns // 2
+    white = whitened(spectra, whitening_scale(spectra, half_width))
     blocks = lax.axis_size("chan")
     piece = chans // blocks
     sectioned = white.reshape(bins, blocks, piece, columns)
@@ -62,8 +79,366 @@
     return jnp.stack(results)
 
 
+def swap(values, offset):
+    return lax.ppermute(values, "chan", [(i, i ^ offset) for i in range(lax.axis_size("chan"))])
+
+
+def line_of(first):
+    return (0, CORE, first, first | CORE)
+
+
+SEND, TAKE, GIVE, ROUTE = 0, 4, 6, 8
+
+
+def route_base(first):
+    return 8 if first == AXIS_X else 8 + ROUTE
+
+
+def route_kernel(devices, device_ref, partner_ref, out_ref):
+    def needed(sender, first, second):
+        receiver = sender ^ second
+        wanted = [
+            partner_ref[r, who] for r in range(ROUNDS) for who in (receiver, receiver ^ CORE)
+        ]
+        need = []
+        for place in line_of(first):
+            hit = (sender ^ wanted[0]) == place
+            for want in wanted[1:]:
+                hit = hit | ((sender ^ want) == place)
+            need.append(hit.astype(jnp.int32))
+        return need
+
+    def slots(need):
+        slot = [jnp.int32(0)]
+        for flag in need[:-1]:
+            slot.append(slot[-1] + flag)
+        return slot
+
+    device = device_ref[0]
+    for place in range(8 + 2 * ROUTE):
+        out_ref[place] = 0
+    for which, (first, second) in enumerate(((AXIS_X, AXIS_Y), (AXIS_Y, AXIS_X))):
+        most = jnp.int32(0)
+        for chip in range(0, devices, 2):
+            need = needed(jnp.int32(chip), first, second)
+            most = jnp.maximum(most, need[0] + need[1] + need[2] + need[3])
+        out_ref[which] = most
+        base = route_base(first)
+        need = needed(device, first, second)
+        slot = slots(need)
+        for s in range(4):
+            value = jnp.int32(0)
+            for place in range(4):
+                value = value + place * need[place] * (slot[place] == s).astype(jnp.int32)
+            out_ref[base + SEND + s] = value
+        slot = slots(needed(device ^ second, first, second))
+        for r in range(ROUNDS):
+            for at, who in ((TAKE, device), (GIVE, device ^ CORE)):
+                offset = device ^ partner_ref[r, who]
+                value = jnp.int32(0)
+                for place, bits in enumerate(line_of(first)):
+                    near = (offset == bits).astype(jnp.int32)
+                    far = (offset == (bits | second)).astype(jnp.int32)
+                    value = value + near * place + far * (4 + slot[place])
+                out_ref[base + at + r] = value
+
+
+def routes(device, partner):
+    smem = pl.BlockSpec(memory_space=pltpu.SMEM)
+    return pl.pallas_call(
+        functools.partial(route_kernel, partner.shape[1]),
+        out_shape=jax.ShapeDtypeStruct((8 + 2 * ROUTE,), jnp.int32),
+        in_specs=[smem, smem],
+        out_specs=smem,
+        name="route",
+    )(device.reshape(1), partner)
+
+
+def line_kernel(base, slots, route, at, own, sister, near, far, scale, line, sent):
+    for b in range(own.shape[0]):
+        columns = jnp.transpose(scale[b])
+        for place, ref in enumerate((own, sister, near, far)):
+            raw = ref[b].astype(jnp.float32)
+            line[place, b] = (raw * columns[:, place : place + 1]).astype(jnp.bfloat16)
+    for s in range(slots):
+        sent[s] = line[route[base + SEND + s]]
+
+
+def line_blocks(first, slots, route, at, own, sister, near, far, scale):
+    part, chans, columns = far.shape
+    step = 1
+
+    def spec(place):
+        return pl.BlockSpec(
+            (pl.Element(step), pl.Element(chans), pl.Element(columns)),
+            lambda i, route, at: (at[place] + i * step, 0, 0),
+        )
+
+    return pl.pallas_call(
+        functools.partial(line_kernel, route_base(first), slots),
+        out_shape=(
+            jax.ShapeDtypeStruct((4, part, chans, columns), jnp.bfloat16),
+            jax.ShapeDtypeStruct((slots, part, chans, columns), jnp.bfloat16),
+        ),
+        grid_spec=pltpu.PrefetchScalarGridSpec(
+            num_scalar_prefetch=2,
+            grid=(part // step,),
+            in_specs=[
+                spec(0),
+                spec(2),
+                spec(1),
+                pl.BlockSpec((step, chans, columns), lambda i, route, at: (i, 0, 0)),
+                pl.BlockSpec(
+                    (pl.Element(step), pl.Element(8), pl.Element(chans)),
+                    lambda i, route, at: (at[3] + i * step, 0, 0),
+                ),
+            ],
+            out_specs=[
+                pl.BlockSpec((4, step, chans, columns), lambda i, route, at: (0, i, 0, 0)),
+                pl.BlockSpec((slots, step, chans, columns), lambda i, route, at: (0, i, 0, 0)),
+            ],
+        ),
+        cost_estimate=pl.CostEstimate(
+            flops=8 * part * chans * columns,
+            bytes_accessed=2 * part * chans * columns * (8 + slots),
+            transcendentals=0,
+        ),
+        name="line",
+    )(route, at, own, sister, near, far, scale)
+
+
+def give_kernel(base, route, line, got, out):
+    place = route[base + GIVE + pl.program_id(0)]
+
+    @pl.when(place < 4)
+    def _():
+        out[...] = line[...]
+
+    @pl.when(place >= 4)
+    def _():
+        out[...] = got[...]
+
+
+def given(first, route, line, got):
+    part, chans, columns = line.shape[1:]
+    base = route_base(first)
+    shape = (1, part, chans, columns)
+    return pl.pallas_call(
+        functools.partial(give_kernel, base),
+        out_shape=jax.ShapeDtypeStruct((ROUNDS, part, chans, columns), jnp.bfloat16),
+        grid_spec=pltpu.PrefetchScalarGridSpec(
+            num_scalar_prefetch=1,
+            grid=(ROUNDS,),
+            in_specs=[
+                pl.BlockSpec(shape, lambda r, route: (jnp.minimum(route[base + GIVE + r], 3), 0, 0, 0)),
+                pl.BlockSpec(
+                    shape, lambda r, route: (jnp.maximum(route[base + GIVE + r] - 4, 0), 0, 0, 0)
+                ),
+            ],
+            out_specs=pl.BlockSpec(shape, lambda r, route: (r, 0, 0, 0)),
+        ),
+        cost_estimate=pl.CostEstimate(
+            flops=0, bytes_accessed=12 * part * chans * columns, transcendentals=0
+        ),
+        name="give",
+    )(route, line, got)
+
+
+def multiply(own, turned, other, out_ref, at, bin_at, windows):
+    contract = (((1,), (1,)), ((), ()))
+    chans = own.shape[0]
+    re = lax.dot_general(own, other, contract, preferred_element_type=jnp.float32)
+    im = lax.dot_general(turned, other, contract, preferred_element_type=jnp.float32)
+    out_ref[at, bin_at, :, :chans] = (re * (1.0 / windows)).astype(jnp.bfloat16)
+    out_ref[at, bin_at, :, chans:] = (im * (1.0 / windows)).astype(jnp.bfloat16)
+
+
+def own_kernel(own, turned, out_ref):
+    for b in range(own.shape[0]):
+        multiply(own[b], turned[b], own[b], out_ref, 0, b, own.shape[2] // 2)
+
+
+def own_products(own, turned):
+    bins, chans, columns = own.shape
+    step = 3
+    spec = pl.BlockSpec((step, chans, columns), lambda i: (i, 0, 0))
+    return pl.pallas_call(
+        own_kernel,
+        out_shape=jax.ShapeDtypeStruct((1 + ROUNDS, bins, chans, 2 * chans), jnp.bfloat16),
+        grid=(bins // step,),
+        in_specs=[spec, spec],
+        out_specs=pl.BlockSpec((1, step, chans, 2 * chans), lambda i: (0, i, 0, 0)),
+        cost_estimate=pl.CostEstimate(
+            flops=4 * bins * chans * chans * columns,
+            bytes_accessed=4 * bins * chans * (columns + chans),
+            transcendentals=0,
+        ),
+        name="own_products",
+    )(own, turned)
+
+
+def here_kernel(base, route, at, own, turned, line0, got0, line1, got1, result, out_ref):
+    for b in range(own.shape[0]):
+        for r, (line, got) in enumerate(((line0, got0), (line1, got1))):
+            near = route[base + TAKE + r] < 4
+            other = jnp.where(near, line[0, b], got[0, b])
+            multiply(own[b], turned[b], other, out_ref, r, b, own.shape[2] // 2)
+
+
+def there_kernel(route, at, own, turned, other, result, out_ref):
+    for b in range(own.shape[0]):
+        for r in range(ROUNDS):
+            multiply(own[b], turned[b], other[r, b], out_ref, r, b, own.shape[2] // 2)
+
+
+def pair_products(kernel, route, at, own, turned, others, other_specs, part, step, result):
+    _, chans, columns = own.shape
+    own_spec = pl.BlockSpec(
+        (pl.Element(step), pl.Element(chans), pl.Element(columns)),
+        lambda i, route, at: (at[0] + i * step, 0, 0),
+    )
+    return pl.pallas_call(
+        kernel,
+        out_shape=jax.ShapeDtypeStruct(result.shape, result.dtype),
+        grid_spec=pltpu.PrefetchScalarGridSpec(
+            num_scalar_prefetch=2,
+            grid=(part // step,),
+            in_specs=[own_spec, own_spec, *other_specs, pl.BlockSpec(memory_space=pl.ANY)],
+            out_specs=pl.BlockSpec(
+                (pl.Element(ROUNDS), pl.Element(step), pl.Element(chans), pl.Element(2 * chans)),
+                lambda i, route, at: (1, at[0] + i * step, 0, 0),
+            ),
+        ),
+        input_output_aliases={4 + len(others): 0},
+        cost_estimate=pl.CostEstimate(
+            flops=8 * part * chans * chans * columns,
+            bytes_accessed=8 * part * chans * (columns + chans),
+            transcendentals=0,
+        ),
+    )(route, at, own, turned, *others, result)
+
+
+def here_products(first, route, at, own, turned, line, got, result):
+    part, chans, columns = line.shape[1:]
+    base = route_base(first)
+    step = 1
+    shape = (1, step, chans, columns)
+    specs, others = [], []
+    for r in range(ROUNDS):
+        specs.append(
+            pl.BlockSpec(
+                shape,
+                lambda i, route, at, r=r: (jnp.minimum(route[base + TAKE + r], 3), i, 0, 0),
+            )
+        )
+        specs.append(
+            pl.BlockSpec(
+                shape,
+                lambda i, route, at, r=r: (jnp.maximum(route[base + TAKE + r] - 4, 0), i, 0, 0),
+            )
+        )
+        others += [line, got]
+    kernel = functools.partial(here_kernel, base)
+    return pair_products(kernel, route, at, own, turned, others, specs, part, step, result)
+
+
+def there_products(route, at, own, turned, other, result):
+    part, chans, columns = other.shape[1:]
+    step = 1
+    specs = [pl.BlockSpec((ROUNDS, step, chans, columns), lambda i, route, at: (0, i, 0, 0))]
+    return pair_products(there_kernel, route, at, own, turned, [other], specs, part, step, result)
+
+
+def plan_of(along_x):
+    pieces = []
+    x_sizes, y_sizes = along_x
+    start_x, start_y = 0, 2 * sum(x_sizes)
+    for place in range(max(len(x_sizes), len(y_sizes))):
+        if place < len(x_sizes):
+            pieces.append((start_x, x_sizes[place], AXIS_X))
+            start_x += 2 * x_sizes[place]
+        if place < len(y_sizes):
+            pieces.append((start_y, y_sizes[place], AXIS_Y))
+            start_y += 2 * y_sizes[place]
+    return pieces
+
+
+def exchange(slots, sizes, spectra, half_width, route, device):
+    _, _, columns = spectra.shape
+    windows = columns // 2
+    core = device & CORE
+    plan = plan_of(sizes)
+    near = []
+    for start, part, first in plan:
+        near.append(swap(spectra[start : start + 2 * part], first))
+    sister = [
+        lax.dynamic_slice_in_dim(spectra, start + (1 - core) * part, part)
+        for start, part, first in plan
+    ]
+    sister = swap(jnp.concatenate(sister), CORE)
+    scale = whitening_scale(spectra, half_width)
+    pair = jnp.stack([scale, swap(scale, CORE)])
+    scales = {}
+    for first in (AXIS_X, AXIS_Y):
+        parts = jnp.concatenate([pair, swap(pair, first), jnp.zeros((4,) + scale.shape)])
+        scales[first] = jnp.swapaxes(parts, 0, 1)
+    own_white = whitened(spectra, scale)
+    turned = jnp.concatenate([own_white[:, :, windows:], -own_white[:, :, :windows]], axis=2)
+    result = own_products(own_white, turned)
+    pools = []
+    shared_at = 0
+    for n, (start, part, first) in enumerate(plan):
+        far = lax.dynamic_slice_in_dim(near[n], (1 - core) * part, part)
+        far = swap(far, CORE)
+        mine = start + core * part
+        at = jnp.stack([mine, core * part, jnp.int32(shared_at), mine])
+        shared_at += part
+        line, sent = line_blocks(
+            first, slots[first], route, at, spectra, sister, near[n], far, scales[first]
+        )
+        got = swap(sent, AXIS_X + AXIS_Y - first)
+        pools.append((line, got))
+    for pair in range(0, len(plan), 2):
+        gifts = []
+        for n in range(pair, min(pair + 2, len(plan))):
+            start, part, first = plan[n]
+            line, got = pools[n]
+            gift = given(first, route, line, got)
+            gifts.append(swap(gift, CORE))
+            at = (start + core * part).reshape(1)
+            result = here_products(first, route, at, own_white, turned, line, got, result)
+        for n in range(pair, min(pair + 2, len(plan))):
+            start, part, first = plan[n]
+            at = (start + (1 - core) * part).reshape(1)
+            result = there_products(route, at, own_white, turned, gifts[n - pair], result)
+    return result
+
+
+CASES = [
+    (2, ((4, 2), (4, 2))),
+    (3, ((4, 2), (4, 2))),
+    (4, ((4, 2), (4, 2))),
+]
+
+
+def paired_body(spectra, half_width, partner):
+    device = lax.axis_index("chan").astype(jnp.int32)
+    route = routes(device, partner)
+    most = jnp.maximum(route[0], route[1])
+    choices = [
+        functools.partial(exchange, {AXIS_X: slots, AXIS_Y: slots}, sizes)
+        for slots, sizes in CASES
+    ]
+    return lax.switch(jnp.clip(most - 2, 0, 2), choices, spectra, half_width, route, device)
+
+
 def solution(mesh):
     placed = (P("band", "chan", None), P("chan"), P())
+    paired = mesh.shape["chan"] == 8
     return jax.shard_map(
-        body, mesh=mesh, in_specs=placed, out_specs=P(None, "band", "chan", None), check_vma=False
+        paired_body if paired else general_body,
+        mesh=mesh,
+        in_specs=placed,
+        out_specs=P(None, "band", "chan", None),
+        check_vma=False,
     )

time: 253 us -> 260 us (1.028); the launches traced: 253 us -> 256 us
  Pallas kernels: 0 us -> 81.6 us
  waiting for transfers between devices: 133 us -> 98.6 us
  other arithmetic: 47.6 us -> 18.4 us
  matrix products: 25.6 us -> 0 us
  loops' own time: 0 us -> 12.3 us
  local copies, waits for them, and re-layouts: 25.3 us -> 21.6 us
    all_to_all x3 -> x0, waiting for transfers between devices: 129 us -> none  [the longest x2 74.5 us: body(): lax.all_to_all(chosen, 'chan', split_axis=1, concat_axis=1, tiled=True)]
    ppermute x0 -> x20, waiting for transfers between devices: none -> 98.6 us  [swap(): lax.ppermute(values, 'chan', [(i, i ^ offset) for i in range(lax.axis_siz...]
    pallas_call x0 -> x18, Pallas kernels: none -> 81.6 us  [the longest x8 37.5 us: pair_products(): pl.pallas_call(kernel, out_shape=jax.ShapeDtypeStruct(result.shape, resul...]
    dot_general x3 -> x0, matrix products: 25.6 us -> none  [pair_block(): jnp.einsum('fcw,fdw->fcd', own, right, preferred_element_type=jnp.float32)]
    ppermute x0 -> x20, starting transfers between devices: none -> 16.4 us  [swap(): lax.ppermute(values, 'chan', [(i, i ^ offset) for i in range(lax.axis_siz...]
    neg x3 -> x0, other arithmetic: 14.4 us -> none  [pair_block(): -other[:, :, windows:]]
    all_to_all x3 -> x0, starting transfers between devices: 14.3 us -> none  [the longest x2 9.53 us: body(): lax.all_to_all(chosen, 'chan', split_axis=1, concat_axis=1, tiled=True)]
    another operation x1 -> x5, other arithmetic: 16.5 us -> 2.47 us  [the longest x4 2.43 us: exchange(): at = jnp.stack([mine, core * part, jnp.int32(shared_at), mine])]
  transfers between devices with their start and end apart: 5 -> 22, of which waited for: 4 -> 7; matrix products, arithmetic and copies ran while one was open for 13% -> 12% of each run, Pallas kernels for 0% -> 30%
where the time goes in v1:
time: 260 us; the launch traced here: 256 us
  waiting for transfers between devices  98.6 us (38%)
  Pallas kernels  81.6 us (31%)
  local copies, waits for them, and re-layouts  21.6 us (8%)
  starting transfers between devices  21.3 us (8%)
  other arithmetic  18.4 us (7%)
  loops' own time  12.3 us (5%)
    ppermute x20, waiting for transfers between devices, swap(): lax.ppermute(values, 'chan', [(i, i ^ offset) for i in range(lax.axis_siz...  98.6 us
    pallas_call x8, Pallas kernels, pair_products(): pl.pallas_call(kernel, out_shape=jax.ShapeDtypeStruct(result.shape, resul...  37.5 us
    pallas_call x4, Pallas kernels, line_blocks(): pl.pallas_call(functools.partial(line_kernel, route_base(first), slots),...  20.9 us
    ppermute x20, starting transfers between devices, swap(): lax.ppermute(values, 'chan', [(i, i ^ offset) for i in range(lax.axis_siz...  16.4 us
    another operation x1, loops' own time, paired_body(): lax.switch(jnp.clip(most - 2, 0, 2), choices, spectra, half_width, route,...  12.3 us
    pallas_call x4, Pallas kernels, given(): pl.pallas_call(functools.partial(give_kernel, base), out_shape=jax.ShapeD...  11.6 us
    pallas_call x1, Pallas kernels, own_products(): pl.pallas_call(own_kernel, out_shape=jax.ShapeDtypeStruct((1 + ROUNDS, bi...  10 us
    slice x2, local copies, waits for them, and re-layouts, exchange(): near.append(swap(spectra[start:start + 2 * part], first))  7.42 us
  transfers between devices with their start and end apart: 22, of which 7 were waited for; matrix products, arithmetic and copies ran while one was open for 12% of the time, Pallas kernels for 30%

profile of v1, /device:TPU:0, one launch (start us, length us, event | category | flops | bytes accessed | tf_op | source)
XLA Modules:
  0.0 256.2 jit_solution(2707029649863731040)
XLA Ops:
  0.0 1.5 route.1
  1.6 0.6 fusion.252
  3.4 251.6 %conditional.1 = (bf16[3,24,256,512]{3,2,1,0:T(8,128)(2,1)}) conditional(s32[]{:T(128)} %bitcast.37, (s32[]{:T(128)}, bf16[24,256,384]{2,1,0:T(8,128)(2,1)}, s32[256]{0:T(256)}, s32[24]{0:T(128)S(1)}) %tuple.14, (s32[]{:T(128)}, bf16[24,256,384]{2,1,0:T(8,128)(2,1)}, s32[256]{0:T(256)}, s32[24]{0:T(128)S(1)}) %tuple.14, (s32[]{:T(128)}, ...), branch_computations={%region_0.2_spmd, %region_2.4_spmd, %region_4.6_spmd} | conditional | flops 7286533120 | bytes 306872224 | solution.py:432
  6.5 4.0 %fusion.240 = (bf16[8,256,384]{2,1,0:T(8,128)(2,1)}, bf16[8,256,384]{2,1,0:T(8,128)(2,1)}) fusion(bf16[24,256,384]{2,1,0:T(8,128)(2,1)} %get-tuple-element.77.own), kind=kLoop, calls=%fused_computation.480 | loop fusion | bytes 6291456 | tf_op jit(solution)/shard_map/cond/branch_1_fun/slice | solution.py:373
  10.6 3.0 %collective-permute-start.40 = (bf16[8,256,384]{2,1,0:T(8,128)(2,1)}, bf16[8,256,384]{2,1,0:T(8,128)(2,1)}, u32[]{:S(2)}, u32[]{:S(2)}) collective-permute-start(bf16[8,256,384]{2,1,0:T(8,128)(2,1)} %get-tuple-element.134), channel_id=1, source_target_pairs={{0,8},{4,12},{8,0},{12,4},{16,24},{20,28},{24,16},{28,20},{1,9},{5... | collective-permute-start | bytes 4718600 | tf_op jit(solution)/shard_map/cond/branch_1_fun/ppermute | solution.py:83
  13.5 1.5 collective-permute-start.36
  15.0 3.4 %fusion.241 = (bf16[4,256,384]{2,1,0:T(8,128)(2,1)}, bf16[4,256,384]{2,1,0:T(8,128)(2,1)}, bf16[4,256,384]{2,1,0:T(8,128)(2,1)S(1)}, bf16[4,256,384]{2,1,0:T(8,128)(2,1)S(1)}) fusion(bf16[24,256,384]{2,1,0:T(8,128)(2,1)} %get-tuple-element.77.own, s32[]{:T(128)S(6)} %select_n.49, s32[]{:T(128)S(6)} %select_n.48), kind=kLoop, calls=%fused_computation.481 | loop fusion | bytes 6291464 | tf_op jit(solution)/shard_map/cond/branch_1_fun/slice | solution.py:373
  18.4 1.3 constant_dynamic-slice_fusion.13
  19.8 1.8 pad_maximum_fusion.7
  21.6 1.0 fusion.78
  22.6 3.5 %collective-permute-start.22 = (f32[12,256]{1,0:T(8,128)S(1)}, f32[12,256]{1,0:T(8,128)S(1)}, u32[]{:S(2)}, u32[]{:S(2)}) collective-permute-start(f32[12,256]{1,0:T(8,128)S(1)} %get-tuple-element.146), channel_id=1, source_target_pairs={{0,1},{1,2},{2,3},{4,5},{5,6},{6,7},{8,9},{9,10},{10,11},{12,13},{... | collective-permute-start | bytes 36872 | tf_op jit(solution)/shard_map/cond/branch_1_fun/ppermute | solution.py:26
  26.1 1.5 collective-permute-start.23
  27.8 20.4 %collective-permute-done.40.near = bf16[8,256,384]{2,1,0:T(8,128)(2,1)} collective-permute-done((bf16[8,256,384]{2,1,0:T(8,128)(2,1)}, bf16[8,256,384]{2,1,0:T(8,128)(2,1)}, u32[]{:S(2)}, u32[]{:S(2)}) %collective-permute-start.40) | collective-permute-done | bytes 1572896 | tf_op jit(solution)/shard_map/cond/branch_1_fun/ppermute | solution.py:83
  48.2 2.1 constant_dynamic-slice_fusion.8
  50.3 2.1 constant_dynamic-slice_fusion.9
  52.4 0.5 collective-permute-start.37
  53.0 0.2 fusion.155
  53.3 0.5 copy-done.22
  53.8 1.3 collective-permute-done.27
  55.2 1.8 collective-permute-start.28
  57.0 1.5 collective-permute-start.33
  58.5 0.6 pad_add_fusion.7.at
  59.3 1.8 collective-permute-done.33
  61.1 0.9 fusion.82
  62.0 1.4 copy-done.7
  63.4 6.4 %line.19 = (bf16[4,4,256,384]{3,2,1,0:T(8,128)(2,1)}, bf16[3,4,256,384]{3,2,1,0:T(8,128)(2,1)}) custom-call(s32[24]{0:T(128)S(1)} %get-tuple-element.45.route, s32[4]{0:T(128)} %pad_add_fusion.7.at, bf16[24,256,384]{2,1,0:T(8,128)(2,1)} %get-tuple-element.77.own, bf16[12,256,384]{2,1,0:T(8,128)(2,1)} %copy-done.7, ...), custom_call_target="tpu_custom_call" | custom-call | flops 3145728 | bytes 8650752 | tf_op jit(solution)/shard_map/cond/branch_1_fun/line/pallas_call | solution.py:177
  69.9 0.3 collective-permute-start.42
  70.1 0.6 pad_add_fusion.6.at
  70.7 0.9 copy-done.14
  71.7 6.4 %line.18 = (bf16[4,4,256,384]{3,2,1,0:T(8,128)(2,1)}, bf16[3,4,256,384]{3,2,1,0:T(8,128)(2,1)}) custom-call(s32[24]{0:T(128)S(1)} %get-tuple-element.45.route, s32[4]{0:T(128)} %pad_add_fusion.6.at, bf16[24,256,384]{2,1,0:T(8,128)(2,1)} %get-tuple-element.77.own, bf16[12,256,384]{2,1,0:T(8,128)(2,1)} %copy-done.7, ...), custom_call_target="tpu_custom_call" | custom-call | flops 3145728 | bytes 8650752 | tf_op jit(solution)/shard_map/cond/branch_1_fun/line/pallas_call | solution.py:177
  78.1 1.7 collective-permute-start.38
  79.9 0.3 collective-permute-start.31
  80.1 1.8 collective-permute-start.25
  81.9 65.6 %collective-permute-done.31.near = bf16[4,256,384]{2,1,0:T(8,128)(2,1)} collective-permute-done((bf16[4,256,384]{2,1,0:T(8,128)(2,1)}, bf16[4,256,384]{2,1,0:T(8,128)(2,1)}, u32[]{:S(2)}, u32[]{:S(2)}) %collective-permute-start.31) | collective-permute-done | bytes 786464 | tf_op jit(solution)/shard_map/cond/branch_1_fun/ppermute | solution.py:83
  147.5 1.8 constant_dynamic-slice_fusion.10
  149.3 0.9 constant_dynamic-slice_fusion.11
  150.2 0.5 collective-permute-start.26
  150.7 0.6 pad_add_fusion.5.at
  151.4 0.6 pad_add_fusion.4.at
  151.9 4.0 %line.17 = (bf16[4,2,256,384]{3,2,1,0:T(8,128)(2,1)}, bf16[3,2,256,384]{3,2,1,0:T(8,128)(2,1)}) custom-call(s32[24]{0:T(128)S(1)} %get-tuple-element.45.route, s32[4]{0:T(128)} %pad_add_fusion.5.at, bf16[24,256,384]{2,1,0:T(8,128)(2,1)} %get-tuple-element.77.own, bf16[12,256,384]{2,1,0:T(8,128)(2,1)} %copy-done.7, ...), custom_call_target="tpu_custom_call" | custom-call | flops 1572864 | bytes 4325376 | tf_op jit(solution)/shard_map/cond/branch_1_fun/line/pallas_call | solution.py:177
  155.9 1.4 collective-permute-start.34
  157.3 0.7 copy-done.18
  158.0 4.1 %line.16 = (bf16[4,2,256,384]{3,2,1,0:T(8,128)(2,1)}, bf16[3,2,256,384]{3,2,1,0:T(8,128)(2,1)}) custom-call(s32[24]{0:T(128)S(1)} %get-tuple-element.45.route, s32[4]{0:T(128)} %pad_add_fusion.4.at, bf16[24,256,384]{2,1,0:T(8,128)(2,1)} %get-tuple-element.77.own, bf16[12,256,384]{2,1,0:T(8,128)(2,1)} %copy-done.7, bf16[4,256,384]{2,1,0:T(8,128)(2,1)} %copy-done.13, ...), custom_call_target="tpu_custom_call" | custom-call | flops 1572864 | bytes 4325376 | tf_op jit(solution)/shard_map/cond/branch_1_fun/line/pallas_call | solution.py:177
  162.1 1.5 collective-permute-start.29
  163.6 1.5 copy-done.10
  165.1 3.2 %give.19 = bf16[2,4,256,384]{3,2,1,0:T(8,128)(2,1)} custom-call(s32[24]{0:T(128)S(1)} %get-tuple-element.45.route, bf16[4,4,256,384]{3,2,1,0:T(8,128)(2,1)} %get-tuple-element.55.line.line0.line1, bf16[3,4,256,384]{3,2,1,0:T(8,128)(2,1)} %copy-done.10), custom_call_target="tpu_custom_call" | custom-call | bytes 4718592 | tf_op jit(solution)/shard_map/cond/branch_1_fun/give/pallas_call | solution.py:226
  168.3 3.2 %give.18 = bf16[2,4,256,384]{3,2,1,0:T(8,128)(2,1)} custom-call(s32[24]{0:T(128)S(1)} %get-tuple-element.45.route, bf16[4,4,256,384]{3,2,1,0:T(8,128)(2,1)} %get-tuple-element.53.line.line0.line1, bf16[3,4,256,384]{3,2,1,0:T(8,128)(2,1)} %collective-permute-done.38.got.got0.got1), custom_call_target="tpu_custom_call" | custom-call | bytes 4718592 | tf_op jit(solution)/shard_map/cond/branch_1_fun/give/pallas_call | solution.py:226
  171.5 0.5 collective-permute-start.39
  172.0 2.9 %fusion.79.own = bf16[24,256,384]{2,1,0:T(8,128)(2,1)S(1)} fusion(bf16[24,256,384]{2,1,0:T(8,128)(2,1)} %get-tuple-element.77.own, f32[24,256]{1,0:T(8,128)S(1)} %copy-done.23), kind=kLoop, calls=%fused_computation.161 | loop fusion | flops 7077888 | bytes 9461760 | tf_op jit(solution)/shard_map/cond/branch_1_fun/convert_element_type | solution.py:63
  174.9 3.2 %fusion.242 = (bf16[24,256,192]{2,1,0:T(8,128)(2,1)S(1)}, bf16[24,256,192]{2,1,0:T(8,128)(2,1)}) fusion(bf16[24,256,384]{2,1,0:T(8,128)(2,1)S(1)} %fusion.79.own), kind=kLoop, calls=%fused_computation.482 | loop fusion | flops 1179648 | bytes 9437184 | tf_op jit(solution)/shard_map/cond/branch_1_fun/slice | solution.py:386
  178.1 6.0 %collective-permute-done.34.got.got0.got1 = bf16[3,2,256,384]{3,2,1,0:T(8,128)(2,1)} collective-permute-done((bf16[3,2,256,384]{3,2,1,0:T(8,128)(2,1)}, bf16[3,2,256,384]{3,2,1,0:T(8,128)(2,1)}, u32[]{:S(2)}, u32[]{:S(2)}) %collective-permute-start.34) | collective-permute-done | bytes 1179680 | tf_op jit(solution)/shard_map/cond/branch_1_fun/ppermute | solution.py:83
  184.1 2.6 %give.17 = bf16[2,2,256,384]{3,2,1,0:T(8,128)(2,1)} custom-call(s32[24]{0:T(128)S(1)} %get-tuple-element.45.route, bf16[4,2,256,384]{3,2,1,0:T(8,128)(2,1)} %get-tuple-element.51.line.line0.line1, bf16[3,2,256,384]{3,2,1,0:T(8,128)(2,1)} %collective-permute-done.34.got.got0.got1), custom_call_target="tpu_custom_call" | custom-call | bytes 2359296 | tf_op jit(solution)/shard_map/cond/branch_1_fun/give/pallas_call | solution.py:226
  186.8 3.3 %collective-permute-done.29.got.got0.got1 = bf16[3,2,256,384]{3,2,1,0:T(8,128)(2,1)} collective-permute-done((bf16[3,2,256,384]{3,2,1,0:T(8,128)(2,1)}, bf16[3,2,256,384]{3,2,1,0:T(8,128)(2,1)}, u32[]{:S(2)}, u32[]{:S(2)}) %collective-permute-start.29) | collective-permute-done | bytes 1179680 | tf_op jit(solution)/shard_map/cond/branch_1_fun/ppermute | solution.py:83
  190.1 2.6 %give.16 = bf16[2,2,256,384]{3,2,1,0:T(8,128)(2,1)} custom-call(s32[24]{0:T(128)S(1)} %get-tuple-element.45.route, bf16[4,2,256,384]{3,2,1,0:T(8,128)(2,1)} %get-tuple-element.49.line.line0.line1, bf16[3,2,256,384]{3,2,1,0:T(8,128)(2,1)} %collective-permute-done.29.got.got0.got1), custom_call_target="tpu_custom_call" | custom-call | bytes 2359296 | tf_op jit(solution)/shard_map/cond/branch_1_fun/give/pallas_call | solution.py:226
  192.7 5.9 %pad_maximum_fusion.6.turned = bf16[24,256,384]{2,1,0:T(8,128)(2,1)} fusion(bf16[24,256,192]{2,1,0:T(8,128)(2,1)} %get-tuple-element.143, bf16[24,256,192]{2,1,0:T(8,128)(2,1)S(1)} %get-tuple-element.142), kind=kLoop, calls=%fused_computation.162 | loop fusion | flops 9437184 | bytes 9437184 | tf_op jit(solution)/shard_map/cond/branch_1_fun/concatenate | solution.py:386
  198.6 10.0 %own_products.4.result = bf16[3,24,256,512]{3,2,1,0:T(8,128)(2,1)} custom-call(bf16[24,256,384]{2,1,0:T(8,128)(2,1)} %copy-done.3, bf16[24,256,384]{2,1,0:T(8,128)(2,1)} %pad_maximum_fusion.6.turned), custom_call_target="tpu_custom_call" | custom-call | flops 2415919104 | bytes 15728640 | tf_op jit(solution)/shard_map/cond/branch_1_fun/own_products/pallas_call | solution.py:265
  208.6 5.9 %branch_1_fun.8.result = bf16[3,24,256,512]{3,2,1,0:T(8,128)(2,1)} custom-call(s32[24]{0:T(128)S(1)} %get-tuple-element.45.route, s32[1]{0:T(128)} %bitcast.22.at, bf16[24,256,384]{2,1,0:T(8,128)(2,1)} %copy-done.3, bf16[24,256,384]{2,1,0:T(8,128)(2,1)} %pad_maximum_fusion.6.turned, ...), custom_call_target="tpu_custom_call", output_to_operand_aliasing={{}: (8, {})} | custom-call | flops 805306368 | bytes 5242880 | tf_op jit(solution)/shard_map/cond/branch_1_fun/pallas_call | solution.py:300
  214.5 6.0 %branch_1_fun.9.result = bf16[3,24,256,512]{3,2,1,0:T(8,128)(2,1)} custom-call(s32[24]{0:T(128)S(1)} %get-tuple-element.45.route, s32[1]{0:T(128)} %bitcast.21.at, bf16[24,256,384]{2,1,0:T(8,128)(2,1)} %copy-done.3, bf16[24,256,384]{2,1,0:T(8,128)(2,1)} %pad_maximum_fusion.6.turned, ...), custom_call_target="tpu_custom_call", output_to_operand_aliasing={{}: (8, {})} | custom-call | flops 805306368 | bytes 5242880 | tf_op jit(solution)/shard_map/cond/branch_1_fun/pallas_call | solution.py:300
  220.5 5.5 %branch_1_fun.10.result = bf16[3,24,256,512]{3,2,1,0:T(8,128)(2,1)} custom-call(s32[24]{0:T(128)S(1)} %get-tuple-element.45.route, s32[1]{0:T(128)} %bitcast.23.at, bf16[24,256,384]{2,1,0:T(8,128)(2,1)} %copy-done.3, bf16[24,256,384]{2,1,0:T(8,128)(2,1)} %pad_maximum_fusion.6.turned, ...), custom_call_target="tpu_custom_call", output_to_operand_aliasing={{}: (5, {})} | custom-call | flops 805306368 | bytes 5242880 | tf_op jit(solution)/shard_map/cond/branch_1_fun/pallas_call | solution.py:300
  225.9 5.5 %branch_1_fun.11.result = bf16[3,24,256,512]{3,2,1,0:T(8,128)(2,1)} custom-call(s32[24]{0:T(128)S(1)} %get-tuple-element.45.route, s32[1]{0:T(128)} %bitcast.20.at, bf16[24,256,384]{2,1,0:T(8,128)(2,1)} %copy-done.3, bf16[24,256,384]{2,1,0:T(8,128)(2,1)} %pad_maximum_fusion.6.turned, ...), custom_call_target="tpu_custom_call", output_to_operand_aliasing={{}: (5, {})} | custom-call | flops 805306368 | bytes 5242880 | tf_op jit(solution)/shard_map/cond/branch_1_fun/pallas_call | solution.py:300
  231.4 3.8 %branch_1_fun.12.result = bf16[3,24,256,512]{3,2,1,0:T(8,128)(2,1)} custom-call(s32[24]{0:T(128)S(1)} %get-tuple-element.45.route, s32[1]{0:T(128)} %bitcast.18.at, bf16[24,256,384]{2,1,0:T(8,128)(2,1)} %copy-done.3, bf16[24,256,384]{2,1,0:T(8,128)(2,1)} %pad_maximum_fusion.6.turned, ...), custom_call_target="tpu_custom_call", output_to_operand_aliasing={{}: (8, {})} | custom-call | flops 402653184 | bytes 2621440 | tf_op jit(solution)/shard_map/cond/branch_1_fun/pallas_call | solution.py:300
  235.2 3.8 %branch_1_fun.13.result = bf16[3,24,256,512]{3,2,1,0:T(8,128)(2,1)} custom-call(s32[24]{0:T(128)S(1)} %get-tuple-element.45.route, s32[1]{0:T(128)} %bitcast.13.at, bf16[24,256,384]{2,1,0:T(8,128)(2,1)} %copy-done.3, bf16[24,256,384]{2,1,0:T(8,128)(2,1)} %pad_maximum_fusion.6.turned, ...), custom_call_target="tpu_custom_call", output_to_operand_aliasing={{}: (8, {})} | custom-call | flops 402653184 | bytes 2621440 | tf_op jit(solution)/shard_map/cond/branch_1_fun/pallas_call | solution.py:300
  239.0 3.6 %branch_1_fun.14.result = bf16[3,24,256,512]{3,2,1,0:T(8,128)(2,1)} custom-call(s32[24]{0:T(128)S(1)} %get-tuple-element.45.route, s32[1]{0:T(128)} %bitcast.17.at, bf16[24,256,384]{2,1,0:T(8,128)(2,1)} %copy-done.3, bf16[24,256,384]{2,1,0:T(8,128)(2,1)} %pad_maximum_fusion.6.turned, ...), custom_call_target="tpu_custom_call", output_to_operand_aliasing={{}: (5, {})} | custom-call | flops 402653184 | bytes 2621440 | tf_op jit(solution)/shard_map/cond/branch_1_fun/pallas_call | solution.py:300
  242.5 3.5 %branch_1_fun.15 = bf16[3,24,256,512]{3,2,1,0:T(8,128)(2,1)} custom-call(s32[24]{0:T(128)S(1)} %get-tuple-element.45.route, s32[1]{0:T(128)} %bitcast.12.at, bf16[24,256,384]{2,1,0:T(8,128)(2,1)} %copy-done.3, bf16[24,256,384]{2,1,0:T(8,128)(2,1)} %pad_maximum_fusion.6.turned, ...), custom_call_target="tpu_custom_call", output_to_operand_aliasing={{}: (5, {})} | custom-call | flops 402653184 | bytes 2621440 | tf_op jit(solution)/shard_map/cond/branch_1_fun/pallas_call | solution.py:300
  (48 shorter events, 0.7 us)
Async XLA Ops:
  10.6 37.7 %collective-permute-start.40 = (bf16[8,256,384]{2,1,0:T(8,128)(2,1)}, bf16[8,256,384]{2,1,0:T(8,128)(2,1)}, u32[]{:S(2)}, u32[]{:S(2)}) collective-permute-start(bf16[8,256,384]{2,1,0:T(8,128)(2,1)} %get-tuple-element.134), channel_id=1, source_target_pairs={{0,8},{4,12},{8,0},{12,4},{16,24},{20,28},{24,16},{28,20},{1,9},{5... | collective-permute-start | bytes 4718600 | tf_op jit(solution)/shard_map/cond/branch_1_fun/ppermute | solution.py:83
  13.5 36.8 %collective-permute-start.36 = (bf16[8,256,384]{2,1,0:T(8,128)(2,1)}, bf16[8,256,384]{2,1,0:T(8,128)(2,1)}, u32[]{:S(2)}, u32[]{:S(2)}) collective-permute-start(bf16[8,256,384]{2,1,0:T(8,128)(2,1)} %get-tuple-element.135), channel_id=1, source_target_pairs={{0,16},{4,20},{8,24},{12,28},{16,0},{20,4},{24,8},{28,12},{1,17},{... | collective-permute-start | bytes 4718600 | tf_op jit(solution)/shard_map/cond/branch_1_fun/ppermute | solution.py:83
  18.4 3.2 %copy-start.1 = (bf16[24,256,384]{2,1,0:T(8,128)(2,1)S(1)}, bf16[24,256,384]{2,1,0:T(8,128)(2,1)}, u32[]{:S(2)}) copy-start(bf16[24,256,384]{2,1,0:T(8,128)(2,1)} %get-tuple-element.77.own) | copy-start | bytes 14155780 | tf_op jit(solution)/shard_map/cond
  21.6 6.2 %copy-start.27 = (s32[256]{0:T(256)S(1)}, s32[256]{0:T(256)}, u32[]{:S(2)}) copy-start(s32[256]{0:T(256)} %get-tuple-element.80) | copy-start | bytes 3076 | tf_op jit(solution)/shard_map/cond
  21.6 40.4 %collective-permute-start.24 = (bf16[12,256,384]{2,1,0:T(8,128)(2,1)}, bf16[12,256,384]{2,1,0:T(8,128)(2,1)S(1)}, u32[]{:S(2)}, u32[]{:S(2)}) collective-permute-start(bf16[12,256,384]{2,1,0:T(8,128)(2,1)} %pad_maximum_fusion.7), channel_id=1, source_target_pairs={{0,4},{4,0},{8,12},{12,8},{16,20},{20,16},{24,28},{28,24},{1,5},{5... | collective-permute-start | bytes 7077896 | tf_op jit(solution)/shard_map/cond/branch_1_fun/ppermute | solution.py:83
  22.6 30.3 %collective-permute-start.22 = (f32[12,256]{1,0:T(8,128)S(1)}, f32[12,256]{1,0:T(8,128)S(1)}, u32[]{:S(2)}, u32[]{:S(2)}) collective-permute-start(f32[12,256]{1,0:T(8,128)S(1)} %get-tuple-element.146), channel_id=1, source_target_pairs={{0,1},{1,2},{2,3},{4,5},{5,6},{6,7},{8,9},{9,10},{10,11},{12,13},{... | collective-permute-start | bytes 36872 | tf_op jit(solution)/shard_map/cond/branch_1_fun/ppermute | solution.py:26
  26.1 26.8 %collective-permute-start.23 = (f32[12,256]{1,0:T(8,128)S(1)}, f32[12,256]{1,0:T(8,128)S(1)}, u32[]{:S(2)}, u32[]{:S(2)}) collective-permute-start(f32[12,256]{1,0:T(8,128)S(1)} %get-tuple-element.147), channel_id=1, source_target_pairs={{1,0},{2,1},{3,2},{5,4},{6,5},{7,6},{9,8},{10,9},{11,10},{13,12},{... | collective-permute-start | bytes 36872 | tf_op jit(solution)/shard_map/cond/branch_1_fun/ppermute | solution.py:28
  50.3 11.7 %collective-permute-start.41 = (bf16[4,256,384]{2,1,0:T(8,128)(2,1)}, bf16[4,256,384]{2,1,0:T(8,128)(2,1)}, u32[]{:S(2)}, u32[]{:S(2)}) collective-permute-start(bf16[4,256,384]{2,1,0:T(8,128)(2,1)} %constant_dynamic-slice_fusion.8), channel_id=1, source_target_pairs={{0,4},{4,0},{8,12},{12,8},{16,20},{20,16},{24,28},{28,24},{1,5},{5... | collective-permute-start | bytes 2359304 | tf_op jit(solution)/shard_map/cond/branch_1_fun/ppermute | solution.py:83
  52.4 18.3 %collective-permute-start.37 = (bf16[4,256,384]{2,1,0:T(8,128)(2,1)}, bf16[4,256,384]{2,1,0:T(8,128)(2,1)S(1)}, u32[]{:S(2)}, u32[]{:S(2)}) collective-permute-start(bf16[4,256,384]{2,1,0:T(8,128)(2,1)} %constant_dynamic-slice_fusion.9), channel_id=1, source_target_pairs={{0,4},{4,0},{8,12},{12,8},{16,20},{20,16},{24,28},{28,24},{1,5},{5... | collective-permute-start | bytes 2359304 | tf_op jit(solution)/shard_map/cond/branch_1_fun/ppermute | solution.py:83
  53.1 0.6 copy-start.22
  53.2 2.0 collective-permute-start.27
  55.2 4.2 %collective-permute-start.28 = (f32[2,24,256]{2,0,1:T(2,128)S(1)}, f32[2,24,256]{2,0,1:T(2,128)S(1)}, u32[]{:S(2)}, u32[]{:S(2)}) collective-permute-start(f32[2,24,256]{2,0,1:T(2,128)S(1)} %pad_maximum_fusion.9), channel_id=1, source_target_pairs={{0,16},{4,20},{8,24},{12,28},{16,0},{20,4},{24,8},{28,12},{1,17},{... | collective-permute-start | bytes 147464 | tf_op jit(solution)/shard_map/cond/branch_1_fun/ppermute | solution.py:83
  57.0 4.1 %collective-permute-start.33 = (f32[2,24,256]{2,0,1:T(2,128)S(1)}, f32[2,24,256]{2,0,1:T(2,128)S(1)}, u32[]{:S(2)}, u32[]{:S(2)}) collective-permute-start(f32[2,24,256]{2,0,1:T(2,128)S(1)} %pad_maximum_fusion.9), channel_id=1, source_target_pairs={{0,8},{4,12},{8,0},{12,4},{16,24},{20,28},{24,16},{28,20},{1,9},{5... | collective-permute-start | bytes 147464 | tf_op jit(solution)/shard_map/cond/branch_1_fun/ppermute | solution.py:83
  62.0 1.4 copy-start.7
  69.9 93.8 %collective-permute-start.42 = (bf16[3,4,256,384]{3,2,1,0:T(8,128)(2,1)}, bf16[3,4,256,384]{3,2,1,0:T(8,128)(2,1)S(1)}, u32[]{:S(2)}, u32[]{:S(2)}) collective-permute-start(bf16[3,4,256,384]{3,2,1,0:T(8,128)(2,1)} %get-tuple-element.56), channel_id=1, source_target_pairs={{0,16},{4,20},{8,24},{12,28},{16,0},{20,4},{24,8},{28,12},{1,17},{... | collective-permute-start | bytes 7077896 | tf_op jit(solution)/shard_map/cond/branch_1_fun/ppermute | solution.py:83
  70.7 0.9 copy-start.14
  78.1 90.2 %collective-permute-start.38 = (bf16[3,4,256,384]{3,2,1,0:T(8,128)(2,1)}, bf16[3,4,256,384]{3,2,1,0:T(8,128)(2,1)}, u32[]{:S(2)}, u32[]{:S(2)}) collective-permute-start(bf16[3,4,256,384]{3,2,1,0:T(8,128)(2,1)} %get-tuple-element.54), channel_id=1, source_target_pairs={{0,8},{4,12},{8,0},{12,4},{16,24},{20,28},{24,16},{28,20},{1,9},{5... | collective-permute-start | bytes 7077896 | tf_op jit(solution)/shard_map/cond/branch_1_fun/ppermute | solution.py:83
  79.9 67.6 %collective-permute-start.31 = (bf16[4,256,384]{2,1,0:T(8,128)(2,1)}, bf16[4,256,384]{2,1,0:T(8,128)(2,1)}, u32[]{:S(2)}, u32[]{:S(2)}) collective-permute-start(bf16[4,256,384]{2,1,0:T(8,128)(2,1)} %get-tuple-element.136), channel_id=1, source_target_pairs={{0,8},{4,12},{8,0},{12,4},{16,24},{20,28},{24,16},{28,20},{1,9},{5... | collective-permute-start | bytes 2359304 | tf_op jit(solution)/shard_map/cond/branch_1_fun/ppermute | solution.py:83
  80.1 69.2 %collective-permute-start.25 = (bf16[4,256,384]{2,1,0:T(8,128)(2,1)}, bf16[4,256,384]{2,1,0:T(8,128)(2,1)S(1)}, u32[]{:S(2)}, u32[]{:S(2)}) collective-permute-start(bf16[4,256,384]{2,1,0:T(8,128)(2,1)} %get-tuple-element.137), channel_id=1, source_target_pairs={{0,16},{4,20},{8,24},{12,28},{16,0},{20,4},{24,8},{28,12},{1,17},{... | collective-permute-start | bytes 2359304 | tf_op jit(solution)/shard_map/cond/branch_1_fun/ppermute | solution.py:83
  149.3 2.6 %collective-permute-start.32 = (bf16[2,256,384]{2,1,0:T(8,128)(2,1)}, bf16[2,256,384]{2,1,0:T(8,128)(2,1)}, u32[]{:S(2)}, u32[]{:S(2)}) collective-permute-start(bf16[2,256,384]{2,1,0:T(8,128)(2,1)} %constant_dynamic-slice_fusion.10), channel_id=1, source_target_pairs={{0,4},{4,0},{8,12},{12,8},{16,20},{20,16},{24,28},{28,24},{1,5},{5... | collective-permute-start | bytes 1179656 | tf_op jit(solution)/shard_map/cond/branch_1_fun/ppermute | solution.py:83
  149.3 6.6 %copy-start.13 = (bf16[4,256,384]{2,1,0:T(8,128)(2,1)}, bf16[4,256,384]{2,1,0:T(8,128)(2,1)S(1)}, u32[]{:S(2)}) copy-start(bf16[4,256,384]{2,1,0:T(8,128)(2,1)S(1)} %collective-permute-done.25.near) | copy-start | bytes 2359300 | tf_op jit(solution)/shard_map/cond
  150.2 7.1 %collective-permute-start.26 = (bf16[2,256,384]{2,1,0:T(8,128)(2,1)}, bf16[2,256,384]{2,1,0:T(8,128)(2,1)S(1)}, u32[]{:S(2)}, u32[]{:S(2)}) collective-permute-start(bf16[2,256,384]{2,1,0:T(8,128)(2,1)} %constant_dynamic-slice_fusion.11), channel_id=1, source_target_pairs={{0,4},{4,0},{8,12},{12,8},{16,20},{20,16},{24,28},{28,24},{1,5},{5... | collective-permute-start | bytes 1179656 | tf_op jit(solution)/shard_map/cond/branch_1_fun/ppermute | solution.py:83
  155.9 28.2 %collective-permute-start.34 = (bf16[3,2,256,384]{3,2,1,0:T(8,128)(2,1)}, bf16[3,2,256,384]{3,2,1,0:T(8,128)(2,1)}, u32[]{:S(2)}, u32[]{:S(2)}) collective-permute-start(bf16[3,2,256,384]{3,2,1,0:T(8,128)(2,1)} %get-tuple-element.52), channel_id=1, source_target_pairs={{0,16},{4,20},{8,24},{12,28},{16,0},{20,4},{24,8},{28,12},{1,17},{... | collective-permute-start | bytes 3538952 | tf_op jit(solution)/shard_map/cond/branch_1_fun/ppermute | solution.py:83
  157.3 0.7 copy-start.18
  162.1 27.9 %collective-permute-start.29 = (bf16[3,2,256,384]{3,2,1,0:T(8,128)(2,1)}, bf16[3,2,256,384]{3,2,1,0:T(8,128)(2,1)}, u32[]{:S(2)}, u32[]{:S(2)}) collective-permute-start(bf16[3,2,256,384]{3,2,1,0:T(8,128)(2,1)} %get-tuple-element.50), channel_id=1, source_target_pairs={{0,8},{4,12},{8,0},{12,4},{16,24},{20,28},{24,16},{28,20},{1,9},{5... | collective-permute-start | bytes 3538952 | tf_op jit(solution)/shard_map/cond/branch_1_fun/ppermute | solution.py:83
  163.6 1.5 copy-start.10
  168.3 52.2 %collective-permute-start.43 = (bf16[2,4,256,384]{3,2,1,0:T(8,128)(2,1)}, bf16[2,4,256,384]{3,2,1,0:T(8,128)(2,1)}, u32[]{:S(2)}, u32[]{:S(2)}) collective-permute-start(bf16[2,4,256,384]{3,2,1,0:T(8,128)(2,1)} %give.19), channel_id=1, source_target_pairs={{0,4},{4,0},{8,12},{12,8},{16,20},{20,16},{24,28},{28,24},{1,5},{5... | collective-permute-start | bytes 4718600 | tf_op jit(solution)/shard_map/cond/branch_1_fun/ppermute | solution.py:83
  168.3 3.7 %copy-start.23 = (f32[24,256]{1,0:T(8,128)S(1)}, f32[24,256]{1,0:T(8,128)}, u32[]{:S(2)}) copy-start(f32[24,256]{1,0:T(8,128)} %copy-done.22) | copy-start | bytes 73732 | tf_op jit(solution)/shard_map/cond
  171.5 54.4 %collective-permute-start.39 = (bf16[2,4,256,384]{3,2,1,0:T(8,128)(2,1)}, bf16[2,4,256,384]{3,2,1,0:T(8,128)(2,1)}, u32[]{:S(2)}, u32[]{:S(2)}) collective-permute-start(bf16[2,4,256,384]{3,2,1,0:T(8,128)(2,1)} %give.18), channel_id=1, source_target_pairs={{0,4},{4,0},{8,12},{12,8},{16,20},{20,16},{24,28},{28,24},{1,5},{5... | collective-permute-start | bytes 4718600 | tf_op jit(solution)/shard_map/cond/branch_1_fun/ppermute | solution.py:83
  174.9 3.2 %copy-start.3 = (bf16[24,256,384]{2,1,0:T(8,128)(2,1)}, bf16[24,256,384]{2,1,0:T(8,128)(2,1)S(1)}, u32[]{:S(2)}) copy-start(bf16[24,256,384]{2,1,0:T(8,128)(2,1)S(1)} %fusion.79.own) | copy-start | bytes 14155780 | tf_op jit(solution)/shard_map/cond
  186.8 52.2 %collective-permute-start.35 = (bf16[2,2,256,384]{3,2,1,0:T(8,128)(2,1)}, bf16[2,2,256,384]{3,2,1,0:T(8,128)(2,1)}, u32[]{:S(2)}, u32[]{:S(2)}) collective-permute-start(bf16[2,2,256,384]{3,2,1,0:T(8,128)(2,1)} %give.17), channel_id=1, source_target_pairs={{0,4},{4,0},{8,12},{12,8},{16,20},{20,16},{24,28},{28,24},{1,5},{5... | collective-permute-start | bytes 2359304 | tf_op jit(solution)/shard_map/cond/branch_1_fun/ppermute | solution.py:83
  192.7 49.8 %collective-permute-start.30 = (bf16[2,2,256,384]{3,2,1,0:T(8,128)(2,1)}, bf16[2,2,256,384]{3,2,1,0:T(8,128)(2,1)}, u32[]{:S(2)}, u32[]{:S(2)}) collective-permute-start(bf16[2,2,256,384]{3,2,1,0:T(8,128)(2,1)} %give.16), channel_id=1, source_target_pairs={{0,4},{4,0},{8,12},{12,8},{16,20},{20,16},{24,28},{28,24},{1,5},{5... | collective-permute-start | bytes 2359304 | tf_op jit(solution)/shard_map/cond/branch_1_fun/ppermute | solution.py:83

commit v2 on v0

--- a/solution.py
+++ b/solution.py
@@ -1,10 +1,18 @@
+import functools
+
 import jax
 import jax.numpy as jnp
 from jax import lax
+from jax.experimental import pallas as pl
+from jax.experimental.pallas import tpu as pltpu
 from jax.sharding import PartitionSpec as P
+
 
 HMAX = 12
 ROUNDS = 2
+CORE = 1
+AXIS_X = 2
+AXIS_Y = 4
 
 
 def padded_2(cells, sides, width):
@@ -31,7 +39,7 @@
     return (product * (1.0 / windows)).astype(jnp.bfloat16)
 
 
-def body(spectra, half_width, partner):
+def whitening_scale(spectra, half_width):
     bins, chans, columns = spectra.shape
     windows = columns // 2
     raw = spectra.astype(jnp.float32)
@@ -48,8 +56,17 @@
         inside = (abs(offset) <= half_width).astype(jnp.float32)[None, :]
         total = total + padded[HMAX + offset : HMAX + offset + bins] * inside
         count = count + present[HMAX + offset : HMAX + offset + bins] * inside
-    scale = lax.rsqrt(total / (2.0 * windows * count) + 1e-06)
-    white = (raw * scale[:, :, None]).astype(jnp.bfloat16)
+    return lax.rsqrt(total / (2.0 * windows * count) + 1e-06)
+
+
+def whitened(raw, scale):
+    return (raw.astype(jnp.float32) * scale[..., None]).astype(jnp.bfloat16)
+
+
+def general_body(spectra, half_width, partner):
+    bins, chans, columns = spectra.shape
+    windows = columns // 2
+    white = whitened(spectra, whitening_scale(spectra, half_width))
     blocks = lax.axis_size("chan")
     piece = chans // blocks
     sectioned = white.reshape(bins, blocks, piece, columns)
@@ -62,8 +79,437 @@
     return jnp.stack(results)
 
 
+MIB = 1 << 20
+
+
+def swap(values, offset):
+    return lax.ppermute(values, "chan", [(i, i ^ offset) for i in range(lax.axis_size("chan"))])
+
+
+SIDES = ((AXIS_X, AXIS_Y), (AXIS_Y, AXIS_X))
+NEEDS, OFFSETS, HALF, LISTS = 0, 2, 4, 8
+SEND, TAKE, THEIRS, LIST = 0, 4, 6, 8
+
+
+def line_of(first):
+    return (0, CORE, first, first | CORE)
+
+
+def route_kernel(devices, device_ref, partner_ref, out_ref):
+    def needed(sender, first, second):
+        receiver = sender ^ second
+        wanted = [
+            partner_ref[r, who] for r in range(ROUNDS) for who in (receiver, receiver ^ CORE)
+        ]
+        need = []
+        for place in line_of(first):
+            hit = (sender ^ wanted[0]) == place
+            for want in wanted[1:]:
+                hit = hit | ((sender ^ want) == place)
+            need.append(hit.astype(jnp.int32))
+        return need
+
+    def slots(need):
+        slot = [jnp.int32(0)]
+        for flag in need[:-1]:
+            slot.append(slot[-1] + flag)
+        return slot
+
+    device = device_ref[0]
+    for place in range(LISTS + 2 * LIST):
+        out_ref[place] = 0
+    for r in range(ROUNDS):
+        out_ref[OFFSETS + r] = device ^ partner_ref[r, device]
+    out_ref[HALF] = device & CORE
+    for side, (first, second) in enumerate(SIDES):
+        most = jnp.int32(0)
+        for chip in range(0, devices, 2):
+            need = needed(jnp.int32(chip), first, second)
+            most = jnp.maximum(most, need[0] + need[1] + need[2] + need[3])
+        out_ref[NEEDS + side] = most
+        base = LISTS + side * LIST
+        need = needed(device, first, second)
+        slot = slots(need)
+        for s in range(4):
+            value = jnp.int32(0)
+            for place in range(4):
+                value = value + place * need[place] * (slot[place] == s).astype(jnp.int32)
+            out_ref[base + SEND + s] = value
+        mine = slots(needed(device ^ second, first, second))
+        theirs = slots(needed(device ^ CORE ^ second, first, second))
+        for r in range(ROUNDS):
+            offset = device ^ partner_ref[r, device]
+            take, other = jnp.int32(0), jnp.int32(0)
+            for place, bits in enumerate(line_of(first)):
+                near = (offset == bits).astype(jnp.int32) * place
+                take += near + (offset == (bits | second)).astype(jnp.int32) * (4 + mine[place])
+                other += near + (offset == ((bits ^ CORE) | second)).astype(jnp.int32) * (
+                    4 + theirs[place]
+                )
+            out_ref[base + TAKE + r] = take
+            out_ref[base + THEIRS + r] = other
+
+
+def routes(device, partner):
+    smem = pl.BlockSpec(memory_space=pltpu.SMEM)
+    return pl.pallas_call(
+        functools.partial(route_kernel, partner.shape[1]),
+        out_shape=jax.ShapeDtypeStruct((LISTS + 2 * LIST,), jnp.int32),
+        in_specs=[smem, smem],
+        out_specs=smem,
+        name="route",
+    )(device.reshape(1), partner)
+
+
+def column(row):
+    return jnp.transpose(jnp.broadcast_to(row, (8, row.shape[1])))[:, :1]
+
+
+def multiply(both, other, out_ref, at, bin_at):
+    chans, columns = other.shape
+    product = lax.dot_general(
+        both, other, (((1,), (1,)), ((), ())), preferred_element_type=jnp.float32
+    )
+    product = (product * (1.0 / (columns // 2))).astype(jnp.bfloat16)
+    out_ref[at, bin_at, :, :chans] = product[:chans]
+    out_ref[at, bin_at, :, chans:] = product[chans:]
+
+
+def own_kernel(raw, scale, both_ref, out_ref):
+    step, chans, columns = raw.shape
+    first = pl.program_id(0) * step
+
+    for b in range(step):
+        white = raw[b].astype(jnp.float32) * column(scale[pl.ds(first + b, 1), :])
+        lane = lax.broadcasted_iota(jnp.int32, (chans, columns), 1)
+        turned = pltpu.roll(jnp.where(lane < columns // 2, -white, white), columns // 2, 1)
+        white, turned = white.astype(jnp.bfloat16), turned.astype(jnp.bfloat16)
+        both_ref[b, :chans] = white
+        both_ref[b, chans:] = turned
+        multiply(jnp.concatenate([white, turned]), white, out_ref, 0, b)
+
+
+def own_products(spectra, scale):
+    bins, chans, columns = spectra.shape
+    step = 3
+    return pl.pallas_call(
+        own_kernel,
+        out_shape=(
+            jax.ShapeDtypeStruct((bins, 2 * chans, columns), jnp.bfloat16),
+            jax.ShapeDtypeStruct((1 + ROUNDS, bins, chans, 2 * chans), jnp.bfloat16),
+        ),
+        grid=(bins // step,),
+        in_specs=[
+            pl.BlockSpec((step, chans, columns), lambda i: (i, 0, 0)),
+            pl.BlockSpec((bins, chans), lambda i: (0, 0)),
+        ],
+        out_specs=[
+            pl.BlockSpec((step, 2 * chans, columns), lambda i: (i, 0, 0)),
+            pl.BlockSpec((1, step, chans, 2 * chans), lambda i: (0, i, 0, 0)),
+        ],
+        cost_estimate=pl.CostEstimate(
+            flops=4 * bins * chans * chans * columns,
+            bytes_accessed=2 * bins * chans * (3 * columns + 2 * chans),
+            transcendentals=0,
+        ),
+        compiler_params=pltpu.CompilerParams(vmem_limit_bytes=16 * MIB),
+        name="own_products",
+    )(spectra, scale)
+
+
+def send_kernel(side, start, route, own, sister, near, far, out_ref, held, arrived, left):
+    slots, part = held.shape[:2]
+    base = LISTS + side * LIST + SEND
+    at = route[HALF] * part
+    sources = (
+        own.at[pl.ds(start + at, part)],
+        sister.at[pl.ds(start + at, part)],
+        near.at[pl.ds(at, part)],
+        far.at[pl.ds(at, part)],
+    )
+    for s in range(slots):
+        for place, source in enumerate(sources):
+
+            @pl.when(route[base + s] == place)
+            def _():
+                pltpu.make_async_copy(source, held.at[s], arrived.at[s]).start()
+
+    for s in range(slots):
+        pltpu.make_async_copy(sources[0], held.at[s], arrived.at[s]).wait()
+        pltpu.make_async_copy(held.at[s], out_ref.at[s], left.at[s]).start()
+    for s in range(slots):
+        pltpu.make_async_copy(held.at[s], out_ref.at[s], left.at[s]).wait()
+
+
+def sends(side, slots, start, part, route, own, sister, near, far):
+    chans, columns = own.shape[1:]
+    anywhere = pl.BlockSpec(memory_space=pl.ANY)
+    smem = pl.BlockSpec(memory_space=pltpu.SMEM)
+    return pl.pallas_call(
+        functools.partial(send_kernel, side, start),
+        out_shape=jax.ShapeDtypeStruct((slots, part, chans, columns), jnp.bfloat16),
+        in_specs=[smem] + [anywhere] * 4,
+        out_specs=anywhere,
+        scratch_shapes=[
+            pltpu.VMEM((slots, part, chans, columns), jnp.bfloat16),
+            pltpu.SemaphoreType.DMA((slots,)),
+            pltpu.SemaphoreType.DMA((slots,)),
+        ],
+        cost_estimate=pl.CostEstimate(
+            flops=0, bytes_accessed=4 * slots * part * chans * columns, transcendentals=0
+        ),
+        compiler_params=pltpu.CompilerParams(vmem_limit_bytes=6 * MIB),
+        name="send",
+    )(route, own, sister, near, far)
+
+
+def pair_kernel(parts, offset, which, raw, inside, unroll, route, both, sister, *refs):
+    out_ref, held, done, done_out, owned, scale, owned_in, held_in, scale_in = refs[-9:]
+    if raw:
+        scales, refs = refs[0], refs[1:]
+    half = route[HALF] if which == TAKE else 1 - route[HALF]
+    total = sum(parts)
+    sides = []
+    for side, part in enumerate(parts):
+        if part:
+            sides.append((side, part, *refs[:3]))
+            refs = refs[3:]
+
+    def place_of(side, r):
+        return route[LISTS + side * LIST + which + r]
+
+    def bin_of(j):
+        return jnp.where(j < parts[0], half * parts[0] + j, parts[0] + half * parts[1] + j)
+
+    if raw:
+        for r in range(ROUNDS):
+            source = scales.at[route[OFFSETS + r]]
+            pltpu.make_async_copy(source, scale.at[r], scale_in.at[r]).start()
+    if not inside:
+        for side, part, near, far, got in sides:
+            for local in range(part):
+                j = local + (parts[0] if side else 0)
+                at = half * part + local
+                start = 2 * parts[0] if side else 0
+                pltpu.make_async_copy(both.at[offset + start + at], owned.at[j], owned_in.at[j]).start()
+                for r in range(ROUNDS):
+                    place = place_of(side, r)
+                    for chosen, source in (
+                        (place <= 1, sister.at[start + at]),
+                        (place == 2, near.at[at]),
+                        (place == 3, far.at[at]),
+                    ):
+
+                        @pl.when(chosen)
+                        def _():
+                            pltpu.make_async_copy(source, held.at[r, j], held_in.at[r, j]).start()
+
+    if raw:
+        for r in range(ROUNDS):
+            pltpu.make_async_copy(scales.at[0], scale.at[r], scale_in.at[r]).wait()
+
+    def ready(j):
+        for side, part, near, far, got in sides:
+
+            @pl.when((j >= parts[0]) == (side == 1))
+            def _():
+                local = j - (parts[0] if side else 0)
+                at = half * part + local
+                for r in range(ROUNDS):
+                    place = place_of(side, r)
+
+                    @pl.when(place >= 4)
+                    def _():
+                        held[r, j] = got[place - 4, local]
+
+                    if inside:
+                        for chosen, source, where in (
+                            (place <= 1, sister, bin_of(j)),
+                            (place == 2, near, at),
+                            (place == 3, far, at),
+                        ):
+
+                            @pl.when(chosen)
+                            def _():
+                                held[r, j] = source[where]
+
+                    else:
+
+                        @pl.when(place < 4)
+                        def _():
+                            pltpu.make_async_copy(
+                                sister.at[0], held.at[r, j], held_in.at[r, j]
+                            ).wait()
+
+        if not inside:
+            pltpu.make_async_copy(both.at[0], owned.at[j], owned_in.at[j]).wait()
+
+    def compute(j):
+        own = both[bin_of(j)] if inside else owned[j]
+        for r in range(ROUNDS):
+            other = held[r, j]
+            if raw:
+                rows = column(scale[r, pl.ds(offset + bin_of(j), 1), :])
+                other = (other.astype(jnp.float32) * rows).astype(jnp.bfloat16)
+            multiply(own, other, done, j, r)
+
+    def leave(j):
+        target = out_ref.at[pl.ds(1, ROUNDS), offset + bin_of(j)]
+        return pltpu.make_async_copy(done.at[j], target, done_out.at[j])
+
+    def step(i, carry):
+        for k in range(unroll):
+            ready(i * unroll + k)
+        for k in range(unroll):
+            compute(i * unroll + k)
+            leave(i * unroll + k).start()
+        return carry
+
+    lax.fori_loop(0, total // unroll, step, 0)
+    for j in range(total):
+        leave(j).wait()
+
+
+def pair_products(
+    which, parts, offset, inside, unroll, route, both, sister, scales, pieces, result
+):
+    chans, columns = sister.shape[1:]
+    anywhere = pl.BlockSpec(memory_space=pl.ANY)
+    within = pl.BlockSpec(memory_space=pltpu.VMEM)
+    place = within if inside else anywhere
+    raw = scales is not None
+    operands = [route, both, sister]
+    in_specs = [pl.BlockSpec(memory_space=pltpu.SMEM), place, place]
+    if raw:
+        operands.append(scales)
+        in_specs.append(anywhere)
+    for piece in pieces:
+        operands += list(piece)
+        in_specs += [place, place, within]
+    total = sum(parts)
+    fetched = 1 if inside else total
+    bins = scales.shape[1] if raw else 8
+    return pl.pallas_call(
+        lambda *refs: pair_kernel(
+            parts, offset, which, raw, inside, unroll, *refs[: len(operands)], *refs[len(operands) + 1 :]
+        ),
+        out_shape=jax.ShapeDtypeStruct(result.shape, result.dtype),
+        in_specs=in_specs + [anywhere],
+        out_specs=anywhere,
+        scratch_shapes=[
+            pltpu.VMEM((ROUNDS, total, chans, columns), jnp.bfloat16),
+            pltpu.VMEM((total, ROUNDS, chans, 2 * chans), jnp.bfloat16),
+            pltpu.SemaphoreType.DMA((total,)),
+            pltpu.VMEM((fetched, 2 * chans, columns), jnp.bfloat16),
+            pltpu.VMEM((ROUNDS, bins, chans), jnp.float32),
+            pltpu.SemaphoreType.DMA((total,)),
+            pltpu.SemaphoreType.DMA((ROUNDS, total)),
+            pltpu.SemaphoreType.DMA((ROUNDS,)),
+        ],
+        input_output_aliases={len(operands): 0},
+        cost_estimate=pl.CostEstimate(
+            flops=8 * total * chans * chans * columns,
+            bytes_accessed=8 * total * chans * (columns + chans),
+            transcendentals=0,
+        ),
+        compiler_params=pltpu.CompilerParams(vmem_limit_bytes=(16 if inside else 30) * MIB),
+    )(*operands, result)
+
+
+def exchange(slots, pairs, spectra, half_width, route):
+    ends = [0]
+    for parts in pairs:
+        ends.append(ends[-1] + 2 * sum(parts))
+
+    def piece_of(values, p, side):
+        start = 2 * pairs[p][0] if side else 0
+        return values[start : start + 2 * pairs[p][side]]
+
+    def near_of(values, p):
+        near = [None, None]
+        for side, (first, second) in enumerate(SIDES):
+            if pairs[p][side]:
+                near[side] = swap(piece_of(values, p, side), first)
+        return near
+
+    near = [near_of(spectra, 0)]
+    owns = [spectra]
+    sisters = [swap(owns[0], CORE)]
+    scale = whitening_scale(spectra, half_width)
+    for p in range(1, len(pairs)):
+        owns.append(whitened(spectra[ends[p] : ends[p + 1]], scale[ends[p] : ends[p + 1]]))
+        near.append(near_of(owns[p], p))
+        sisters.append(swap(owns[p], CORE))
+    couple = jnp.stack([scale, swap(scale, CORE)])
+    scales = [couple]
+    for offset in (AXIS_X, AXIS_Y, AXIS_X | AXIS_Y):
+        scales.append(swap(couple, offset))
+    scales = jnp.concatenate(scales)
+    both, result = own_products(spectra, scale)
+    far, got = [], []
+    for p, parts in enumerate(pairs):
+        far.append([None, None])
+        got.append([None, None])
+        for side, (first, second) in enumerate(SIDES):
+            part = parts[side]
+            if part:
+                far[p][side] = swap(near[p][side], CORE)
+                sent = sends(
+                    side,
+                    slots,
+                    2 * parts[0] if side else 0,
+                    part,
+                    route,
+                    owns[p],
+                    sisters[p],
+                    near[p][side],
+                    far[p][side],
+                )
+                got[p][side] = swap(sent, second)
+    for p, parts in enumerate(pairs):
+        used = [side for side in (0, 1) if parts[side]]
+        shared = {}
+        for side in used:
+            shared[side] = swap(got[p][side], CORE)
+        owned = both[ends[p] : ends[p + 1]] if p else both
+        for which, table in ((TAKE, {side: got[p][side] for side in used}), (THEIRS, shared)):
+            pieces = [(near[p][side], far[p][side], table[side]) for side in used]
+            result = pair_products(
+                which,
+                parts,
+                ends[p],
+                p > 0,
+                UNROLL[p],
+                route,
+                owned,
+                sisters[p],
+                None if p else scales,
+                pieces,
+                result,
+            )
+    return result
+
+
+PAIRS = ((4, 4), (2, 2))
+UNROLL = (1, 1)
+CASES = [(2, PAIRS), (3, PAIRS), (4, PAIRS)]
+
+
+def paired_body(spectra, half_width, partner):
+    device = lax.axis_index("chan").astype(jnp.int32)
+    route = routes(device, partner)
+    most = jnp.maximum(route[NEEDS], route[NEEDS + 1])
+    choices = [functools.partial(exchange, slots, pairs) for slots, pairs in CASES]
+    return lax.switch(jnp.clip(most - 2, 0, 2), choices, spectra, half_width, route)
+
+
 def solution(mesh):
     placed = (P("band", "chan", None), P("chan"), P())
+    paired = mesh.shape["chan"] == 8
     return jax.shard_map(
-        body, mesh=mesh, in_specs=placed, out_specs=P(None, "band", "chan", None), check_vma=False
+        paired_body if paired else general_body,
+        mesh=mesh,
+        in_specs=placed,
+        out_specs=P(None, "band", "chan", None),
+        check_vma=False,
     )

time: 253 us -> 217 us (0.86)
  Pallas kernels: 0 us -> 48.3 us
  other arithmetic: 47.6 us -> 1.57 us
  matrix products: 25.6 us -> 0 us
  local copies, waits for them, and re-layouts: 25.3 us -> 3.8 us
  waiting for transfers between devices: 133 us -> 141 us
    ppermute x0 -> x22, waiting for transfers between devices: none -> 141 us  [swap(): lax.ppermute(values, 'chan', [(i, i ^ offset) for i in range(lax.axis_siz...]
    all_to_all x3 -> x0, waiting for transfers between devices: 129 us -> none  [the longest x2 74.5 us: body(): lax.all_to_all(chosen, 'chan', split_axis=1, concat_axis=1, tiled=True)]
    pallas_call x0 -> x10, Pallas kernels: none -> 48.3 us  [the longest x4 30.7 us: pair_products(): pl.pallas_call(lambda *refs: pair_kernel(parts, offset, which, raw, insid...]
    dot_general x3 -> x0, matrix products: 25.6 us -> none  [pair_block(): jnp.einsum('fcw,fdw->fcd', own, right, preferred_element_type=jnp.float32)]
    another operation x1, other arithmetic: 16.5 us -> 0.01 us  [exchange(): couple = jnp.stack([scale, swap(scale, CORE)])]
    ppermute x0 -> x22, starting transfers between devices: none -> 15.1 us  [swap(): lax.ppermute(values, 'chan', [(i, i ^ offset) for i in range(lax.axis_siz...]
    neg x3 -> x0, other arithmetic: 14.4 us -> none  [pair_block(): -other[:, :, windows:]]
    all_to_all x3 -> x0, starting transfers between devices: 14.3 us -> none  [the longest x2 9.53 us: body(): lax.all_to_all(chosen, 'chan', split_axis=1, concat_axis=1, tiled=True)]
  transfers between devices with their start and end apart: 5 -> 24, of which waited for: 4 -> 9; matrix products, arithmetic and copies ran while one was open for 13% -> 2% of each run, Pallas kernels for 0% -> 16%
where the time goes in v2:
time: 217 us; the launch traced here: 216 us
  waiting for transfers between devices  141 us (65%)
  Pallas kernels  48.3 us (22%)
  starting transfers between devices  19.8 us (9%)
  local copies, waits for them, and re-layouts  3.8 us (2%)
    ppermute x22, waiting for transfers between devices, swap(): lax.ppermute(values, 'chan', [(i, i ^ offset) for i in range(lax.axis_siz...  141 us
    pallas_call x4, Pallas kernels, pair_products(): pl.pallas_call(lambda *refs: pair_kernel(parts, offset, which, raw, insid...  30.7 us
    ppermute x22, starting transfers between devices, swap(): lax.ppermute(values, 'chan', [(i, i ^ offset) for i in range(lax.axis_siz...  15.1 us
    pallas_call x1, Pallas kernels, own_products(): pl.pallas_call(own_kernel, out_shape=(jax.ShapeDtypeStruct((bins, 2 * cha...  8.95 us
    pallas_call x4, Pallas kernels, sends(): pl.pallas_call(functools.partial(send_kernel, side, start), out_shape=jax...  7.14 us
  transfers between devices with their start and end apart: 24, of which 9 were waited for; matrix products, arithmetic and copies ran while one was open for 2% of the time, Pallas kernels for 16%

profile of v2, /device:TPU:0, one launch (start us, length us, event | category | flops | bytes accessed | tf_op | source)
XLA Modules:
  0.0 216.4 jit_solution(5139028675145771977)
XLA Ops:
  0.0 1.5 route.1
  1.6 0.6 fusion.237
  3.4 212.8 %conditional.1 = (bf16[3,24,256,512]{3,2,1,0:T(8,128)(2,1)}) conditional(s32[]{:T(128)} %bitcast.7, (bf16[24,256,384]{2,1,0:T(8,128)(2,1)}, s32[256]{0:T(256)}, s32[24]{0:T(128)S(1)}) %tuple.14, (bf16[24,256,384]{2,1,0:T(8,128)(2,1)}, s32[256]{0:T(256)}, s32[24]{0:T(128)S(1)}) %tuple.14, (bf16[24,256,384]{2,1,0:T(8,128)(2,1)}, ...), branch_computations={%region_0.2_spmd, %region_2.4_spmd, %region_4.6_spmd} | conditional | flops 7257975808 | bytes 363224512 | solution.py:503
  3.5 0.0 copy-start.8
  3.5 0.6 collective-permute-start.35
  4.0 2.5 %fusion.227 = (bf16[8,256,384]{2,1,0:T(8,128)(2,1)S(1)}, bf16[8,256,384]{2,1,0:T(8,128)(2,1)S(1)}) fusion(bf16[24,256,384]{2,1,0:T(8,128)(2,1)} %get-tuple-element.50.raw.own), kind=kLoop, calls=%fused_computation.428 | loop fusion | bytes 6291456 | tf_op jit(solution)/shard_map/cond/branch_1_fun/slice | solution.py:426
  6.6 2.4 %collective-permute-start.40 = (bf16[8,256,384]{2,1,0:T(8,128)(2,1)S(1)}, bf16[8,256,384]{2,1,0:T(8,128)(2,1)S(1)}, u32[]{:S(2)}, u32[]{:S(2)}) collective-permute-start(bf16[8,256,384]{2,1,0:T(8,128)(2,1)S(1)} %get-tuple-element.106), channel_id=1, source_target_pairs={{0,8},{4,12},{8,0},{12,4},{16,24},{20,28},{24,16},{28,20},{1,9},{5... | collective-permute-start | bytes 4718600 | tf_op jit(solution)/shard_map/cond/branch_1_fun/ppermute | solution.py:86
  9.0 1.5 collective-permute-start.44
  10.5 33.7 %collective-permute-done.40.near.refs_4_ = bf16[8,256,384]{2,1,0:T(8,128)(2,1)S(1)} collective-permute-done((bf16[8,256,384]{2,1,0:T(8,128)(2,1)S(1)}, bf16[8,256,384]{2,1,0:T(8,128)(2,1)S(1)}, u32[]{:S(2)}, u32[]{:S(2)}) %collective-permute-start.40) | collective-permute-done | bytes 1572896 | tf_op jit(solution)/shard_map/cond/branch_1_fun/ppermute | solution.py:86
  44.2 0.1 collective-permute-start.41
  44.3 1.4 collective-permute-done.44.near.refs_7_
  45.7 0.0 collective-permute-start.45
  45.7 1.0 multiply_reduce_fusion.1
  46.7 3.5 %collective-permute-start.24 = (f32[12,256]{1,0:T(8,128)S(1)}, f32[12,256]{1,0:T(8,128)S(1)}, u32[]{:S(2)}, u32[]{:S(2)}) collective-permute-start(f32[12,256]{1,0:T(8,128)S(1)} %get-tuple-element.109), channel_id=1, source_target_pairs={{0,1},{1,2},{2,3},{4,5},{5,6},{6,7},{8,9},{9,10},{10,11},{12,13},{... | collective-permute-start | bytes 36872 | tf_op jit(solution)/shard_map/cond/branch_1_fun/ppermute | solution.py:26
  50.2 1.3 collective-permute-start.25
  51.5 0.1 fusion.230
  51.7 0.0 collective-permute-done.41.far.refs_5_
  51.7 0.0 collective-permute-done.35.sister.refs_2_
  51.7 0.0 slice-start.4
  51.7 2.5 %send.18 = bf16[3,4,256,384]{3,2,1,0:T(8,128)(2,1)S(1)} custom-call(s32[24]{0:T(128)S(1)} %get-tuple-element.32.route.refs_0_, bf16[24,256,384]{2,1,0:T(8,128)(2,1)} %get-tuple-element.50.raw.own, bf16[24,256,384]{2,1,0:T(8,128)(2,1)} %collective-permute-done.35.sister.refs_2_, bf16[8,256,384]{2,1,0:T(8,128)(2,1)S(1)} %collective-permute-done.40.near.refs_4_, ...), custom_call_target="tpu_custom_call" | custom-call | bytes 4718592 | tf_op jit(solution)/shard_map/cond/branch_1_fun/send/pallas_call | solution.py:248
  54.3 1.5 collective-permute-start.42
  55.8 0.0 collective-permute-done.45.far.refs_8_
  55.8 1.0 send.19
  56.8 2.1 collective-permute-start.46
  58.9 0.1 fusion.231
  59.0 0.0 collective-permute-done.24
  59.0 0.0 collective-permute-done.25
  59.0 0.2 constant_dynamic-update-slice_fusion.9
  59.2 0.3 multiply_convert_fusion.1.own
  59.5 0.2 fusion.228
  59.7 0.1 collective-permute-start.27
  59.8 0.3 collective-permute-start.26
  60.0 1.2 collective-permute-start.31
  61.3 66.4 %collective-permute-done.27.near.refs_3_ = bf16[4,256,384]{2,1,0:T(8,128)(2,1)S(1)} collective-permute-done((bf16[4,256,384]{2,1,0:T(8,128)(2,1)S(1)}, bf16[4,256,384]{2,1,0:T(8,128)(2,1)S(1)}, u32[]{:S(2)}, u32[]{:S(2)}) %collective-permute-start.27) | collective-permute-done | bytes 786464 | tf_op jit(solution)/shard_map/cond/branch_1_fun/ppermute | solution.py:86
  127.7 0.0 collective-permute-start.28
  127.7 0.0 collective-permute-done.31.near.refs_6_
  127.7 0.5 collective-permute-start.32
  128.2 0.0 collective-permute-done.42.refs_6_
  128.2 0.1 collective-permute-start.43
  128.3 0.0 collective-permute-done.46.refs_9_
  128.3 0.4 collective-permute-start.47
  128.7 1.3 collective-permute-done.28.far.refs_4_
  130.0 0.0 collective-permute-done.26.sister.refs_2_
  130.0 1.8 send.16
  131.8 0.8 collective-permute-start.29
  132.6 1.8 send.17
  134.4 0.4 collective-permute-start.33
  134.8 25.1 %collective-permute-done.29.refs_5_ = bf16[3,2,256,384]{3,2,1,0:T(8,128)(2,1)S(1)} collective-permute-done((bf16[3,2,256,384]{3,2,1,0:T(8,128)(2,1)S(1)}, bf16[3,2,256,384]{3,2,1,0:T(8,128)(2,1)S(1)}, u32[]{:S(2)}, u32[]{:S(2)}) %collective-permute-start.29) | collective-permute-done | bytes 1179680 | tf_op jit(solution)/shard_map/cond/branch_1_fun/ppermute | solution.py:86
  159.9 0.0 collective-permute-start.30
  159.9 2.5 %collective-permute-done.33.refs_8_ = bf16[3,2,256,384]{3,2,1,0:T(8,128)(2,1)} collective-permute-done((bf16[3,2,256,384]{3,2,1,0:T(8,128)(2,1)S(1)}, bf16[3,2,256,384]{3,2,1,0:T(8,128)(2,1)}, u32[]{:S(2)}, u32[]{:S(2)}) %collective-permute-start.33) | collective-permute-done | bytes 1179680 | tf_op jit(solution)/shard_map/cond/branch_1_fun/ppermute | solution.py:86
  162.4 0.0 collective-permute-start.34
  162.4 9.0 %own_products.4 = (bf16[24,512,384]{2,1,0:T(8,128)(2,1)S(1)}, bf16[3,24,256,512]{3,2,1,0:T(8,128)(2,1)}) custom-call(bf16[24,256,384]{2,1,0:T(8,128)(2,1)S(1)} %bitcast.22, f32[24,256]{1,0:T(8,128)S(1)} %get-tuple-element.58.scale), custom_call_target="tpu_custom_call" | custom-call | flops 2415919104 | bytes 20447232 | tf_op jit(solution)/shard_map/cond/branch_1_fun/own_products/pallas_call | solution.py:195
  171.3 0.3 slice.608.refs_1_
  171.6 0.0 collective-permute-done.36
  171.7 0.3 collective-permute-start.37
  172.0 3.9 %collective-permute-done.37 = f32[2,24,256]{2,1,0:T(8,128)S(1)} collective-permute-done((f32[2,24,256]{2,1,0:T(8,128)S(1)}, f32[2,24,256]{2,1,0:T(8,128)S(1)}, u32[]{:S(2)}, u32[]{:S(2)}) %collective-permute-start.37) | collective-permute-done | bytes 49184 | tf_op jit(solution)/shard_map/cond/branch_1_fun/ppermute | solution.py:86
  175.9 1.3 collective-permute-start.38
  177.2 2.8 %collective-permute-done.38 = f32[2,24,256]{2,1,0:T(8,128)S(1)} collective-permute-done((f32[2,24,256]{2,1,0:T(8,128)S(1)}, f32[2,24,256]{2,1,0:T(8,128)S(1)}, u32[]{:S(2)}, u32[]{:S(2)}) %collective-permute-start.38) | collective-permute-done | bytes 49184 | tf_op jit(solution)/shard_map/cond/branch_1_fun/ppermute | solution.py:86
  180.0 1.4 collective-permute-start.39
  181.3 3.6 %collective-permute-done.39 = f32[2,24,256]{2,1,0:T(8,128)S(1)} collective-permute-done((f32[2,24,256]{2,1,0:T(8,128)S(1)}, f32[2,24,256]{2,1,0:T(8,128)S(1)}, u32[]{:S(2)}, u32[]{:S(2)}) %collective-permute-start.39) | collective-permute-done | bytes 49184 | tf_op jit(solution)/shard_map/cond/branch_1_fun/ppermute | solution.py:86
  185.0 10.7 %branch_1_fun.4.refs_10_ = bf16[3,24,256,512]{3,2,1,0:T(8,128)(2,1)} custom-call(s32[24]{0:T(128)S(1)} %get-tuple-element.32.route.refs_0_, bf16[24,512,384]{2,1,0:T(8,128)(2,1)} %copy-done.1, bf16[24,256,384]{2,1,0:T(8,128)(2,1)} %collective-permute-done.35.sister.refs_2_, ...), custom_call_target="tpu_custom_call", output_to_operand_aliasing={{}: (10, {})} | custom-call | flops 1610612736 | bytes 10485760 | tf_op jit(solution)/shard_map/cond/branch_1_fun/pallas_call | solution.py:392
  195.7 10.7 %branch_1_fun.5.refs_9_ = bf16[3,24,256,512]{3,2,1,0:T(8,128)(2,1)} custom-call(s32[24]{0:T(128)S(1)} %get-tuple-element.32.route.refs_0_, bf16[24,512,384]{2,1,0:T(8,128)(2,1)} %copy-done.1, bf16[24,256,384]{2,1,0:T(8,128)(2,1)} %collective-permute-done.35.sister.refs_2_, ...), custom_call_target="tpu_custom_call", output_to_operand_aliasing={{}: (10, {})} | custom-call | flops 1610612736 | bytes 10485760 | tf_op jit(solution)/shard_map/cond/branch_1_fun/pallas_call | solution.py:392
  206.4 4.5 %branch_1_fun.6.refs_9_ = bf16[3,24,256,512]{3,2,1,0:T(8,128)(2,1)} custom-call(s32[24]{0:T(128)S(1)} %get-tuple-element.32.route.refs_0_, bf16[8,512,384]{2,1,0:T(8,128)(2,1)S(1)} %slice.608.refs_1_, bf16[8,256,384]{2,1,0:T(8,128)(2,1)S(1)} %collective-permute-done.26.sister.refs_2_, ...), custom_call_target="tpu_custom_call", output_to_operand_aliasing={{}: (9, {})} | custom-call | flops 805306368 | bytes 5242880 | tf_op jit(solution)/shard_map/cond/branch_1_fun/pallas_call | solution.py:392
  210.9 4.8 %branch_1_fun.7 = bf16[3,24,256,512]{3,2,1,0:T(8,128)(2,1)} custom-call(s32[24]{0:T(128)S(1)} %get-tuple-element.32.route.refs_0_, bf16[8,512,384]{2,1,0:T(8,128)(2,1)S(1)} %slice.608.refs_1_, bf16[8,256,384]{2,1,0:T(8,128)(2,1)S(1)} %collective-permute-done.26.sister.refs_2_, ...), custom_call_target="tpu_custom_call", output_to_operand_aliasing={{}: (9, {})} | custom-call | flops 805306368 | bytes 5242880 | tf_op jit(solution)/shard_map/cond/branch_1_fun/pallas_call | solution.py:392
  (24 shorter events, 0.1 us)
Async XLA Ops:
  3.5 42.3 %copy-start.8 = (bf16[24,256,384]{2,1,0:T(8,128)(2,1)S(1)}, bf16[24,256,384]{2,1,0:T(8,128)(2,1)}, u32[]{:S(2)}) copy-start(bf16[24,256,384]{2,1,0:T(8,128)(2,1)} %get-tuple-element.50.raw.own) | copy-start | bytes 14155780 | tf_op jit(solution)/shard_map/cond
  3.5 48.2 %collective-permute-start.35 = (bf16[24,256,384]{2,1,0:T(8,128)(2,1)}, bf16[24,256,384]{2,1,0:T(8,128)(2,1)}, u32[]{:S(2)}, u32[]{:S(2)}) collective-permute-start(bf16[24,256,384]{2,1,0:T(8,128)(2,1)} %get-tuple-element.50.raw.own), channel_id=1, source_target_pairs={{0,4},{4,0},{8,12},{12,8},{16,20},{20,16},{24,28},{28,24},{1,5},{5... | collective-permute-start | bytes 14155784 | tf_op jit(solution)/shard_map/cond/branch_1_fun/ppermute | solution.py:86
  6.6 37.6 %collective-permute-start.40 = (bf16[8,256,384]{2,1,0:T(8,128)(2,1)S(1)}, bf16[8,256,384]{2,1,0:T(8,128)(2,1)S(1)}, u32[]{:S(2)}, u32[]{:S(2)}) collective-permute-start(bf16[8,256,384]{2,1,0:T(8,128)(2,1)S(1)} %get-tuple-element.106), channel_id=1, source_target_pairs={{0,8},{4,12},{8,0},{12,4},{16,24},{20,28},{24,16},{28,20},{1,9},{5... | collective-permute-start | bytes 4718600 | tf_op jit(solution)/shard_map/cond/branch_1_fun/ppermute | solution.py:86
  9.0 42.7 %copy-start.11 = (s32[256]{0:T(256)S(1)}, s32[256]{0:T(256)}, u32[]{:S(2)}) copy-start(s32[256]{0:T(256)} %get-tuple-element.53) | copy-start | bytes 3076 | tf_op jit(solution)/shard_map/cond
  9.0 36.7 %collective-permute-start.44 = (bf16[8,256,384]{2,1,0:T(8,128)(2,1)S(1)}, bf16[8,256,384]{2,1,0:T(8,128)(2,1)S(1)}, u32[]{:S(2)}, u32[]{:S(2)}) collective-permute-start(bf16[8,256,384]{2,1,0:T(8,128)(2,1)S(1)} %get-tuple-element.105), channel_id=1, source_target_pairs={{0,16},{4,20},{8,24},{12,28},{16,0},{20,4},{24,8},{28,12},{1,17},{... | collective-permute-start | bytes 4718600 | tf_op jit(solution)/shard_map/cond/branch_1_fun/ppermute | solution.py:86
  44.2 7.5 %collective-permute-start.41 = (bf16[8,256,384]{2,1,0:T(8,128)(2,1)S(1)}, bf16[8,256,384]{2,1,0:T(8,128)(2,1)}, u32[]{:S(2)}, u32[]{:S(2)}) collective-permute-start(bf16[8,256,384]{2,1,0:T(8,128)(2,1)S(1)} %collective-permute-done.40.near.refs_4_), channel_id=1, source_target_pairs={{0,4},{4,0},{8,12},{12,8},{16,20},{20,16},{24,28},{28,24},{1,5},{5... | collective-permute-start | bytes 4718600 | tf_op jit(solution)/shard_map/cond/branch_1_fun/ppermute | solution.py:86
  45.7 10.0 %collective-permute-start.45 = (bf16[8,256,384]{2,1,0:T(8,128)(2,1)S(1)}, bf16[8,256,384]{2,1,0:T(8,128)(2,1)}, u32[]{:S(2)}, u32[]{:S(2)}) collective-permute-start(bf16[8,256,384]{2,1,0:T(8,128)(2,1)S(1)} %collective-permute-done.44.near.refs_7_), channel_id=1, source_target_pairs={{0,4},{4,0},{8,12},{12,8},{16,20},{20,16},{24,28},{28,24},{1,5},{5... | collective-permute-start | bytes 4718600 | tf_op jit(solution)/shard_map/cond/branch_1_fun/ppermute | solution.py:86
  46.7 12.2 %collective-permute-start.24 = (f32[12,256]{1,0:T(8,128)S(1)}, f32[12,256]{1,0:T(8,128)S(1)}, u32[]{:S(2)}, u32[]{:S(2)}) collective-permute-start(f32[12,256]{1,0:T(8,128)S(1)} %get-tuple-element.109), channel_id=1, source_target_pairs={{0,1},{1,2},{2,3},{4,5},{5,6},{6,7},{8,9},{9,10},{10,11},{12,13},{... | collective-permute-start | bytes 36872 | tf_op jit(solution)/shard_map/cond/branch_1_fun/ppermute | solution.py:26
  50.2 8.7 %collective-permute-start.25 = (f32[12,256]{1,0:T(8,128)S(1)}, f32[12,256]{1,0:T(8,128)S(1)}, u32[]{:S(2)}, u32[]{:S(2)}) collective-permute-start(f32[12,256]{1,0:T(8,128)S(1)} %get-tuple-element.110), channel_id=1, source_target_pairs={{1,0},{2,1},{3,2},{5,4},{6,5},{7,6},{9,8},{10,9},{11,10},{13,12},{... | collective-permute-start | bytes 36872 | tf_op jit(solution)/shard_map/cond/branch_1_fun/ppermute | solution.py:28
  51.7 4.1 %slice-start.4 = ((s8[4718592]{0:T(1024)(128)(4,1)}), s8[4194304]{0:T(1024)(128)(4,1)S(1)}, s32[]{:S(2)}) async-start(s8[4718592]{0:T(1024)(128)(4,1)} %bitcast.21), calls=%async_computation.4 | async-start | bytes 8388608 | tf_op jit(solution)/shard_map/cond
  51.7 4.1 %slice-start.5 = ((s8[4718592]{0:T(1024)(128)(4,1)}), s8[524288]{0:T(1024)(128)(4,1)S(1)}, s32[]{:S(2)}) async-start(s8[4718592]{0:T(1024)(128)(4,1)} %bitcast.21), calls=%async_computation.5 | async-start | bytes 1048576 | tf_op jit(solution)/shard_map/cond
  54.3 74.0 %collective-permute-start.42 = (bf16[3,4,256,384]{3,2,1,0:T(8,128)(2,1)S(1)}, bf16[3,4,256,384]{3,2,1,0:T(8,128)(2,1)}, u32[]{:S(2)}, u32[]{:S(2)}) collective-permute-start(bf16[3,4,256,384]{3,2,1,0:T(8,128)(2,1)S(1)} %send.18), channel_id=1, source_target_pairs={{0,16},{4,20},{8,24},{12,28},{16,0},{20,4},{24,8},{28,12},{1,17},{... | collective-permute-start | bytes 7077896 | tf_op jit(solution)/shard_map/cond/branch_1_fun/ppermute | solution.py:86
  56.8 71.5 %collective-permute-start.46 = (bf16[3,4,256,384]{3,2,1,0:T(8,128)(2,1)S(1)}, bf16[3,4,256,384]{3,2,1,0:T(8,128)(2,1)}, u32[]{:S(2)}, u32[]{:S(2)}) collective-permute-start(bf16[3,4,256,384]{3,2,1,0:T(8,128)(2,1)S(1)} %send.19), channel_id=1, source_target_pairs={{0,8},{4,12},{8,0},{12,4},{16,24},{20,28},{24,16},{28,20},{1,9},{5... | collective-permute-start | bytes 7077896 | tf_op jit(solution)/shard_map/cond/branch_1_fun/ppermute | solution.py:86
  59.7 68.0 %collective-permute-start.27 = (bf16[4,256,384]{2,1,0:T(8,128)(2,1)S(1)}, bf16[4,256,384]{2,1,0:T(8,128)(2,1)S(1)}, u32[]{:S(2)}, u32[]{:S(2)}) collective-permute-start(bf16[4,256,384]{2,1,0:T(8,128)(2,1)S(1)} %get-tuple-element.108), channel_id=1, source_target_pairs={{0,8},{4,12},{8,0},{12,4},{16,24},{20,28},{24,16},{28,20},{1,9},{5... | collective-permute-start | bytes 2359304 | tf_op jit(solution)/shard_map/cond/branch_1_fun/ppermute | solution.py:86
  59.8 70.2 %collective-permute-start.26 = (bf16[8,256,384]{2,1,0:T(8,128)(2,1)S(1)}, bf16[8,256,384]{2,1,0:T(8,128)(2,1)S(1)}, u32[]{:S(2)}, u32[]{:S(2)}) collective-permute-start(bf16[8,256,384]{2,1,0:T(8,128)(2,1)S(1)} %multiply_convert_fusion.1.own), channel_id=1, source_target_pairs={{0,4},{4,0},{8,12},{12,8},{16,20},{20,16},{24,28},{28,24},{1,5},{5... | collective-permute-start | bytes 4718600 | tf_op jit(solution)/shard_map/cond/branch_1_fun/ppermute | solution.py:86
  60.0 67.7 %collective-permute-start.31 = (bf16[4,256,384]{2,1,0:T(8,128)(2,1)S(1)}, bf16[4,256,384]{2,1,0:T(8,128)(2,1)S(1)}, u32[]{:S(2)}, u32[]{:S(2)}) collective-permute-start(bf16[4,256,384]{2,1,0:T(8,128)(2,1)S(1)} %get-tuple-element.107), channel_id=1, source_target_pairs={{0,16},{4,20},{8,24},{12,28},{16,0},{20,4},{24,8},{28,12},{1,17},{... | collective-permute-start | bytes 2359304 | tf_op jit(solution)/shard_map/cond/branch_1_fun/ppermute | solution.py:86
  127.7 2.3 %collective-permute-start.28 = (bf16[4,256,384]{2,1,0:T(8,128)(2,1)S(1)}, bf16[4,256,384]{2,1,0:T(8,128)(2,1)S(1)}, u32[]{:S(2)}, u32[]{:S(2)}) collective-permute-start(bf16[4,256,384]{2,1,0:T(8,128)(2,1)S(1)} %collective-permute-done.27.near.refs_3_), channel_id=1, source_target_pairs={{0,4},{4,0},{8,12},{12,8},{16,20},{20,16},{24,28},{28,24},{1,5},{5... | collective-permute-start | bytes 2359304 | tf_op jit(solution)/shard_map/cond/branch_1_fun/ppermute | solution.py:86
  127.7 4.9 %collective-permute-start.32 = (bf16[4,256,384]{2,1,0:T(8,128)(2,1)S(1)}, bf16[4,256,384]{2,1,0:T(8,128)(2,1)S(1)}, u32[]{:S(2)}, u32[]{:S(2)}) collective-permute-start(bf16[4,256,384]{2,1,0:T(8,128)(2,1)S(1)} %collective-permute-done.31.near.refs_6_), channel_id=1, source_target_pairs={{0,4},{4,0},{8,12},{12,8},{16,20},{20,16},{24,28},{28,24},{1,5},{5... | collective-permute-start | bytes 2359304 | tf_op jit(solution)/shard_map/cond/branch_1_fun/ppermute | solution.py:86
  128.2 67.5 %collective-permute-start.43 = (bf16[3,4,256,384]{3,2,1,0:T(8,128)(2,1)}, bf16[3,4,256,384]{3,2,1,0:T(8,128)(2,1)}, u32[]{:S(2)}, u32[]{:S(2)}) collective-permute-start(bf16[3,4,256,384]{3,2,1,0:T(8,128)(2,1)} %collective-permute-done.42.refs_6_), channel_id=1, source_target_pairs={{0,4},{4,0},{8,12},{12,8},{16,20},{20,16},{24,28},{28,24},{1,5},{5... | collective-permute-start | bytes 7077896 | tf_op jit(solution)/shard_map/cond/branch_1_fun/ppermute | solution.py:86
  128.3 67.4 %collective-permute-start.47 = (bf16[3,4,256,384]{3,2,1,0:T(8,128)(2,1)}, bf16[3,4,256,384]{3,2,1,0:T(8,128)(2,1)}, u32[]{:S(2)}, u32[]{:S(2)}) collective-permute-start(bf16[3,4,256,384]{3,2,1,0:T(8,128)(2,1)} %collective-permute-done.46.refs_9_), channel_id=1, source_target_pairs={{0,4},{4,0},{8,12},{12,8},{16,20},{20,16},{24,28},{28,24},{1,5},{5... | collective-permute-start | bytes 7077896 | tf_op jit(solution)/shard_map/cond/branch_1_fun/ppermute | solution.py:86
  131.8 28.1 %collective-permute-start.29 = (bf16[3,2,256,384]{3,2,1,0:T(8,128)(2,1)S(1)}, bf16[3,2,256,384]{3,2,1,0:T(8,128)(2,1)S(1)}, u32[]{:S(2)}, u32[]{:S(2)}) collective-permute-start(bf16[3,2,256,384]{3,2,1,0:T(8,128)(2,1)S(1)} %send.16), channel_id=1, source_target_pairs={{0,16},{4,20},{8,24},{12,28},{16,0},{20,4},{24,8},{28,12},{1,17},{... | collective-permute-start | bytes 3538952 | tf_op jit(solution)/shard_map/cond/branch_1_fun/ppermute | solution.py:86
  134.4 27.9 %collective-permute-start.33 = (bf16[3,2,256,384]{3,2,1,0:T(8,128)(2,1)S(1)}, bf16[3,2,256,384]{3,2,1,0:T(8,128)(2,1)}, u32[]{:S(2)}, u32[]{:S(2)}) collective-permute-start(bf16[3,2,256,384]{3,2,1,0:T(8,128)(2,1)S(1)} %send.17), channel_id=1, source_target_pairs={{0,8},{4,12},{8,0},{12,4},{16,24},{20,28},{24,16},{28,20},{1,9},{5... | collective-permute-start | bytes 3538952 | tf_op jit(solution)/shard_map/cond/branch_1_fun/ppermute | solution.py:86
  134.8 36.8 %collective-permute-start.36 = (f32[24,256]{1,0:T(8,128)S(1)}, f32[24,256]{1,0:T(8,128)S(1)}, u32[]{:S(2)}, u32[]{:S(2)}) collective-permute-start(f32[24,256]{1,0:T(8,128)S(1)} %get-tuple-element.58.scale), channel_id=1, source_target_pairs={{0,4},{4,0},{8,12},{12,8},{16,20},{20,16},{24,28},{28,24},{1,5},{5... | collective-permute-start | bytes 73736 | tf_op jit(solution)/shard_map/cond/branch_1_fun/ppermute | solution.py:86
  159.9 51.0 %collective-permute-start.30 = (bf16[3,2,256,384]{3,2,1,0:T(8,128)(2,1)S(1)}, bf16[3,2,256,384]{3,2,1,0:T(8,128)(2,1)}, u32[]{:S(2)}, u32[]{:S(2)}) collective-permute-start(bf16[3,2,256,384]{3,2,1,0:T(8,128)(2,1)S(1)} %collective-permute-done.29.refs_5_), channel_id=1, source_target_pairs={{0,4},{4,0},{8,12},{12,8},{16,20},{20,16},{24,28},{28,24},{1,5},{5... | collective-permute-start | bytes 3538952 | tf_op jit(solution)/shard_map/cond/branch_1_fun/ppermute | solution.py:86
  162.4 48.5 %collective-permute-start.34 = (bf16[3,2,256,384]{3,2,1,0:T(8,128)(2,1)}, bf16[3,2,256,384]{3,2,1,0:T(8,128)(2,1)}, u32[]{:S(2)}, u32[]{:S(2)}) collective-permute-start(bf16[3,2,256,384]{3,2,1,0:T(8,128)(2,1)} %collective-permute-done.33.refs_8_), channel_id=1, source_target_pairs={{0,4},{4,0},{8,12},{12,8},{16,20},{20,16},{24,28},{28,24},{1,5},{5... | collective-permute-start | bytes 3538952 | tf_op jit(solution)/shard_map/cond/branch_1_fun/ppermute | solution.py:86
  171.3 13.7 %copy-start.1 = (bf16[24,512,384]{2,1,0:T(8,128)(2,1)}, bf16[24,512,384]{2,1,0:T(8,128)(2,1)S(1)}, u32[]{:S(2)}) copy-start(bf16[24,512,384]{2,1,0:T(8,128)(2,1)S(1)} %get-tuple-element.35.refs_1_) | copy-start | bytes 28311556 | tf_op jit(solution)/shard_map/cond
  171.7 4.2 %collective-permute-start.37 = (f32[2,24,256]{2,1,0:T(8,128)S(1)}, f32[2,24,256]{2,1,0:T(8,128)S(1)}, u32[]{:S(2)}, u32[]{:S(2)}) collective-permute-start(f32[2,24,256]{2,1,0:T(8,128)S(1)} %pad_maximum_fusion.3), channel_id=1, source_target_pairs={{0,8},{4,12},{8,0},{12,4},{16,24},{20,28},{24,16},{28,20},{1,9},{5... | collective-permute-start | bytes 147464 | tf_op jit(solution)/shard_map/cond/branch_1_fun/ppermute | solution.py:86
  175.9 4.1 %collective-permute-start.38 = (f32[2,24,256]{2,1,0:T(8,128)S(1)}, f32[2,24,256]{2,1,0:T(8,128)S(1)}, u32[]{:S(2)}, u32[]{:S(2)}) collective-permute-start(f32[2,24,256]{2,1,0:T(8,128)S(1)} %pad_maximum_fusion.3), channel_id=1, source_target_pairs={{0,16},{4,20},{8,24},{12,28},{16,0},{20,4},{24,8},{28,12},{1,17},{... | collective-permute-start | bytes 147464 | tf_op jit(solution)/shard_map/cond/branch_1_fun/ppermute | solution.py:86
  180.0 5.0 %collective-permute-start.39 = (f32[2,24,256]{2,1,0:T(8,128)S(1)}, f32[2,24,256]{2,1,0:T(8,128)S(1)}, u32[]{:S(2)}, u32[]{:S(2)}) collective-permute-start(f32[2,24,256]{2,1,0:T(8,128)S(1)} %pad_maximum_fusion.3), channel_id=1, source_target_pairs={{0,24},{4,28},{8,16},{12,20},{16,8},{20,12},{24,0},{28,4},{1,25},{... | collective-permute-start | bytes 147464 | tf_op jit(solution)/shard_map/cond/branch_1_fun/ppermute | solution.py:86

commit v3 on v2

--- a/solution.py
+++ b/solution.py
@@ -87,7 +87,7 @@
 
 
 SIDES = ((AXIS_X, AXIS_Y), (AXIS_Y, AXIS_X))
-NEEDS, OFFSETS, HALF, LISTS = 0, 2, 4, 8
+OFFSETS, HALF, LISTS = 0, 2, 8
 SEND, TAKE, THEIRS, LIST = 0, 4, 6, 8
 
 
@@ -95,7 +95,7 @@
     return (0, CORE, first, first | CORE)
 
 
-def route_kernel(devices, device_ref, partner_ref, out_ref):
+def route_kernel(devices, device_ref, partner_ref, out_ref, case_ref):
     def needed(sender, first, second):
         receiver = sender ^ second
         wanted = [
@@ -121,12 +121,11 @@
     for r in range(ROUNDS):
         out_ref[OFFSETS + r] = device ^ partner_ref[r, device]
     out_ref[HALF] = device & CORE
+    most = jnp.int32(0)
     for side, (first, second) in enumerate(SIDES):
-        most = jnp.int32(0)
         for chip in range(0, devices, 2):
             need = needed(jnp.int32(chip), first, second)
             most = jnp.maximum(most, need[0] + need[1] + need[2] + need[3])
-        out_ref[NEEDS + side] = most
         base = LISTS + side * LIST
         need = needed(device, first, second)
         slot = slots(need)
@@ -148,17 +147,7 @@
                 )
             out_ref[base + TAKE + r] = take
             out_ref[base + THEIRS + r] = other
-
-
-def routes(device, partner):
-    smem = pl.BlockSpec(memory_space=pltpu.SMEM)
-    return pl.pallas_call(
-        functools.partial(route_kernel, partner.shape[1]),
-        out_shape=jax.ShapeDtypeStruct((LISTS + 2 * LIST,), jnp.int32),
-        in_specs=[smem, smem],
-        out_specs=smem,
-        name="route",
-    )(device.reshape(1), partner)
+    case_ref[0] = jnp.clip(most - 2, 0, 2)
 
 
 def column(row):
@@ -215,6 +204,55 @@
         compiler_params=pltpu.CompilerParams(vmem_limit_bytes=16 * MIB),
         name="own_products",
     )(spectra, scale)
+
+
+def start_kernel(devices, chunk, device_ref, partner_ref, spectra, *refs):
+    out_ref, case_ref, *outs, held, arrived, left = refs
+    copies = []
+    begin = 0
+    for piece in outs:
+        for local in range(0, piece.shape[0], chunk):
+            n = len(copies)
+            into = pltpu.make_async_copy(
+                spectra.at[pl.ds(begin + local, chunk)], held.at[n], arrived.at[n]
+            )
+            onto = pltpu.make_async_copy(held.at[n], piece.at[pl.ds(local, chunk)], left.at[n])
+            copies.append((into, onto))
+        begin += piece.shape[0]
+    for into, onto in copies:
+        into.start()
+    route_kernel(devices, device_ref, partner_ref, out_ref, case_ref)
+    for into, onto in copies:
+        into.wait()
+        onto.start()
+    for into, onto in copies:
+        onto.wait()
+
+
+def starts_of(device, partner, spectra, parts):
+    chans, columns = spectra.shape[1:]
+    chunk = 2
+    count = 2 * sum(parts) // chunk
+    anywhere = pl.BlockSpec(memory_space=pl.ANY)
+    smem = pl.BlockSpec(memory_space=pltpu.SMEM)
+    route, case, *pieces = pl.pallas_call(
+        functools.partial(start_kernel, partner.shape[1], chunk),
+        out_shape=(
+            jax.ShapeDtypeStruct((LISTS + 2 * LIST,), jnp.int32),
+            jax.ShapeDtypeStruct((1,), jnp.int32),
+            *(jax.ShapeDtypeStruct((2 * part, chans, columns), spectra.dtype) for part in parts),
+        ),
+        in_specs=[smem, smem, anywhere],
+        out_specs=(smem, smem) + (anywhere,) * len(parts),
+        scratch_shapes=[
+            pltpu.VMEM((count, chunk, chans, columns), spectra.dtype),
+            pltpu.SemaphoreType.DMA((count,)),
+            pltpu.SemaphoreType.DMA((count,)),
+        ],
+        compiler_params=pltpu.CompilerParams(vmem_limit_bytes=6 * MIB),
+        name="start",
+    )(device.reshape(1), partner, spectra)
+    return route, case, pieces
 
 
 def send_kernel(side, start, route, own, sister, near, far, out_ref, held, arrived, left):
@@ -412,11 +450,11 @@
             bytes_accessed=8 * total * chans * (columns + chans),
             transcendentals=0,
         ),
-        compiler_params=pltpu.CompilerParams(vmem_limit_bytes=(16 if inside else 30) * MIB),
+        compiler_params=pltpu.CompilerParams(vmem_limit_bytes=(16 if inside else 20) * MIB),
     )(*operands, result)
 
 
-def exchange(slots, pairs, spectra, half_width, route):
+def exchange(slots, pairs, spectra, half_width, route, *pieces):
     ends = [0]
     for parts in pairs:
         ends.append(ends[-1] + 2 * sum(parts))
@@ -425,20 +463,20 @@
         start = 2 * pairs[p][0] if side else 0
         return values[start : start + 2 * pairs[p][side]]
 
-    def near_of(values, p):
+    def near_of(pieces, p):
         near = [None, None]
         for side, (first, second) in enumerate(SIDES):
             if pairs[p][side]:
-                near[side] = swap(piece_of(values, p, side), first)
+                near[side] = swap(pieces[side], first)
         return near
 
-    near = [near_of(spectra, 0)]
+    near = [near_of(pieces, 0)]
     owns = [spectra]
     sisters = [swap(owns[0], CORE)]
     scale = whitening_scale(spectra, half_width)
     for p in range(1, len(pairs)):
         owns.append(whitened(spectra[ends[p] : ends[p + 1]], scale[ends[p] : ends[p + 1]]))
-        near.append(near_of(owns[p], p))
+        near.append(near_of([piece_of(owns[p], p, side) for side in (0, 1)], p))
         sisters.append(swap(owns[p], CORE))
     couple = jnp.stack([scale, swap(scale, CORE)])
     scales = [couple]
@@ -491,16 +529,15 @@
 
 
 PAIRS = ((4, 4), (2, 2))
-UNROLL = (1, 1)
+UNROLL = (1, 2)
 CASES = [(2, PAIRS), (3, PAIRS), (4, PAIRS)]
 
 
 def paired_body(spectra, half_width, partner):
     device = lax.axis_index("chan").astype(jnp.int32)
-    route = routes(device, partner)
-    most = jnp.maximum(route[NEEDS], route[NEEDS + 1])
+    route, case, pieces = starts_of(device, partner, spectra, PAIRS[0])
     choices = [functools.partial(exchange, slots, pairs) for slots, pairs in CASES]
-    return lax.switch(jnp.clip(most - 2, 0, 2), choices, spectra, half_width, route)
+    return lax.switch(case.reshape(()), choices, spectra, half_width, route, *pieces)
 
 
 def solution(mesh):

time: 217 us -> 222 us (1.023)
  Pallas kernels: 48.3 us -> 52.2 us
  other arithmetic: 1.57 us -> 5.32 us
    cond x13 -> x7, local copies, waits for them, and re-layouts: 0.04 us -> 3.17 us
    pallas_call x1, Pallas kernels: 1.54 us -> 4.07 us  [starts_of(): pl.pallas_call(functools.partial(start_kernel, partner.shape[1], chunk),...]
    slice x2 -> x1, local copies, waits for them, and re-layouts: 2.69 us -> 0.16 us  [piece_of(): return values[start:start + 2 * pairs[p][side]]]
    reduce_sum x1, other arithmetic: 1.01 us -> 3.35 us  [whitening_scale(): power = jnp.sum(raw * raw, axis=2)]
  transfers between devices with their start and end apart: 24 -> 24, of which waited for: 9 -> 9; matrix products, arithmetic and copies ran while one was open for 2% -> 3% of each run, Pallas kernels for 16% -> 16%
where the time goes in v3:
time: 222 us; the launch traced here: 221 us
  waiting for transfers between devices  139 us (63%)
  Pallas kernels  52.2 us (24%)
  starting transfers between devices  19 us (9%)
  other arithmetic  5.32 us (2%)
  local copies, waits for them, and re-layouts  4.52 us (2%)
    ppermute x22, waiting for transfers between devices, swap(): lax.ppermute(values, 'chan', [(i, i ^ offset) for i in range(lax.axis_siz...  139 us
    pallas_call x4, Pallas kernels, pair_products(): pl.pallas_call(lambda *refs: pair_kernel(parts, offset, which, raw, insid...  28.7 us
    ppermute x22, starting transfers between devices, swap(): lax.ppermute(values, 'chan', [(i, i ^ offset) for i in range(lax.axis_siz...  14.2 us
    pallas_call x1, Pallas kernels, own_products(): pl.pallas_call(own_kernel, out_shape=(jax.ShapeDtypeStruct((bins, 2 * cha...  11.2 us
    pallas_call x4, Pallas kernels, sends(): pl.pallas_call(functools.partial(send_kernel, side, start), out_shape=jax...  8.33 us
  transfers between devices with their start and end apart: 24, of which 9 were waited for; matrix products, arithmetic and copies ran while one was open for 3% of the time, Pallas kernels for 16%

profile of v3, /device:TPU:0, one launch (start us, length us, event | category | flops | bytes accessed | tf_op | source)
XLA Modules:
  0.0 221.4 jit_solution(15770640360861649829)
XLA Ops:
  0.0 0.7 copy-done.7
  0.7 4.1 %start.1 = (s32[24]{0:T(128)S(1)}, s32[1]{0:T(128)}, bf16[8,256,384]{2,1,0:T(8,128)(2,1)S(1)}, bf16[8,256,384]{2,1,0:T(8,128)(2,1)S(1)}) custom-call(s32[1]{0:T(128)} %bitcast.6.device_ref, s32[2,8]{1,0:T(2,128)S(1)} %copy-done.7, bf16[24,256,384]{2,1,0:T(8,128)(2,1)} %spectra.1), custom_call_target="tpu_custom_call" | custom-call | tf_op jit(solution)/shard_map/start/pallas_call | solution.py:238
  5.4 215.8 %conditional.1 = (bf16[3,24,256,512]{3,2,1,0:T(8,128)(2,1)}) conditional(s32[]{:T(128)} %bitcast.7, (bf16[24,256,384]{2,1,0:T(8,128)(2,1)}, s32[256]{0:T(256)S(1)}, s32[24]{0:T(128)S(1)}, bf16[8,256,384]{2,1,0:T(8,128)(2,1)S(1)}, bf16[8,256,384]{2,1,0:T(8,128)(2,1)S(1)}) %tuple.135, (bf16[24,256,384]{2,1,0:T(8,128)(2,1)}, ...), branch_computations={%region_0.0_spmd, %region_2.0_spmd, %region_4.0_spmd} | conditional | flops 7257975808 | bytes 286149952 | solution.py:540
  5.6 0.6 collective-permute-start.35
  6.2 2.6 %collective-permute-start.40 = (bf16[8,256,384]{2,1,0:T(8,128)(2,1)S(1)}, bf16[8,256,384]{2,1,0:T(8,128)(2,1)S(1)}, u32[]{:S(2)}, u32[]{:S(2)}) collective-permute-start(bf16[8,256,384]{2,1,0:T(8,128)(2,1)S(1)} %get-tuple-element.50), channel_id=1, source_target_pairs={{0,8},{4,12},{8,0},{12,4},{16,24},{20,28},{24,16},{28,20},{1,9},{5... | collective-permute-start | bytes 4718600 | tf_op jit(solution)/shard_map/cond/branch_1_fun/ppermute | solution.py:86
  8.7 1.5 collective-permute-start.44
  10.3 33.5 %collective-permute-done.40.near.refs_4_ = bf16[8,256,384]{2,1,0:T(8,128)(2,1)S(1)} collective-permute-done((bf16[8,256,384]{2,1,0:T(8,128)(2,1)S(1)}, bf16[8,256,384]{2,1,0:T(8,128)(2,1)S(1)}, u32[]{:S(2)}, u32[]{:S(2)}) %collective-permute-start.40) | collective-permute-done | bytes 1572896 | tf_op jit(solution)/shard_map/cond/branch_1_fun/ppermute | solution.py:86
  43.7 0.0 collective-permute-start.41
  43.7 1.5 collective-permute-done.44.near.refs_7_
  45.2 0.0 collective-permute-start.45
  45.2 3.3 %multiply_reduce_fusion.1 = f32[24,256]{1,0:T(8,128)S(1)} fusion(bf16[24,256,384]{2,1,0:T(8,128)(2,1)} %get-tuple-element.47.raw.own), kind=kLoop, calls=%fused_computation.141 | loop fusion | flops 7071744 | bytes 4743168 | tf_op jit(solution)/shard_map/cond/branch_1_fun/reduce_sum | solution.py:46
  48.5 3.5 %collective-permute-start.24 = (f32[12,256]{1,0:T(8,128)S(1)}, f32[12,256]{1,0:T(8,128)S(1)}, u32[]{:S(2)}, u32[]{:S(2)}) collective-permute-start(f32[12,256]{1,0:T(8,128)S(1)} %get-tuple-element.125), channel_id=1, source_target_pairs={{0,1},{1,2},{2,3},{4,5},{5,6},{6,7},{8,9},{9,10},{10,11},{12,13},{... | collective-permute-start | bytes 36872 | tf_op jit(solution)/shard_map/cond/branch_1_fun/ppermute | solution.py:26
  52.0 1.3 collective-permute-start.25
  53.4 0.1 fusion.228
  53.5 0.0 collective-permute-done.41.far.refs_5_
  53.5 0.0 collective-permute-done.35.sister.refs_2_
  53.5 2.3 %send.18 = bf16[3,4,256,384]{3,2,1,0:T(8,128)(2,1)S(1)} custom-call(s32[24]{0:T(128)S(1)} %get-tuple-element.46.route.refs_0_, bf16[24,256,384]{2,1,0:T(8,128)(2,1)} %get-tuple-element.47.raw.own, bf16[24,256,384]{2,1,0:T(8,128)(2,1)} %collective-permute-done.35.sister.refs_2_, bf16[8,256,384]{2,1,0:T(8,128)(2,1)S(1)} %collective-permute-done.40.near.refs_4_, ...), custom_call_target="tpu_custom_call" | custom-call | bytes 4718592 | tf_op jit(solution)/shard_map/cond/branch_1_fun/send/pallas_call | solution.py:286
  55.8 1.3 collective-permute-start.42
  57.1 0.0 collective-permute-done.45.far.refs_8_
  57.1 2.4 %send.19 = bf16[3,4,256,384]{3,2,1,0:T(8,128)(2,1)S(1)} custom-call(s32[24]{0:T(128)S(1)} %get-tuple-element.46.route.refs_0_, bf16[24,256,384]{2,1,0:T(8,128)(2,1)} %get-tuple-element.47.raw.own, bf16[24,256,384]{2,1,0:T(8,128)(2,1)} %collective-permute-done.35.sister.refs_2_, bf16[8,256,384]{2,1,0:T(8,128)(2,1)S(1)} %collective-permute-done.44.near.refs_7_, ...), custom_call_target="tpu_custom_call" | custom-call | bytes 4718592 | tf_op jit(solution)/shard_map/cond/branch_1_fun/send/pallas_call | solution.py:286
  59.5 1.1 collective-permute-start.46
  60.6 0.1 fusion.229
  60.7 0.0 collective-permute-done.24
  60.7 0.0 collective-permute-done.25
  60.7 0.2 constant_dynamic-update-slice_fusion.9
  60.9 1.8 multiply_convert_fusion.1.own
  62.6 0.2 fusion.226
  62.8 1.1 collective-permute-start.27
  63.9 0.0 collective-permute-start.26
  63.9 0.5 collective-permute-start.31
  64.4 65.1 %collective-permute-done.27.near.refs_3_ = bf16[4,256,384]{2,1,0:T(8,128)(2,1)S(1)} collective-permute-done((bf16[4,256,384]{2,1,0:T(8,128)(2,1)S(1)}, bf16[4,256,384]{2,1,0:T(8,128)(2,1)S(1)}, u32[]{:S(2)}, u32[]{:S(2)}) %collective-permute-start.27) | collective-permute-done | bytes 786464 | tf_op jit(solution)/shard_map/cond/branch_1_fun/ppermute | solution.py:86
  129.4 0.0 collective-permute-start.28
  129.4 0.0 collective-permute-done.31.near.refs_6_
  129.5 0.5 collective-permute-start.32
  130.0 0.0 collective-permute-done.42.refs_6_
  130.0 0.1 collective-permute-start.43
  130.0 0.0 collective-permute-done.46.refs_9_
  130.0 0.4 collective-permute-start.47
  130.5 1.3 collective-permute-done.28.far.refs_4_
  131.7 1.8 send.16
  133.6 0.8 collective-permute-start.29
  134.3 0.0 collective-permute-done.32.far.refs_7_
  134.3 1.8 send.17
  136.1 0.6 collective-permute-start.33
  136.8 24.9 %collective-permute-done.29.refs_5_ = bf16[3,2,256,384]{3,2,1,0:T(8,128)(2,1)S(1)} collective-permute-done((bf16[3,2,256,384]{3,2,1,0:T(8,128)(2,1)S(1)}, bf16[3,2,256,384]{3,2,1,0:T(8,128)(2,1)S(1)}, u32[]{:S(2)}, u32[]{:S(2)}) %collective-permute-start.29) | collective-permute-done | bytes 1179680 | tf_op jit(solution)/shard_map/cond/branch_1_fun/ppermute | solution.py:86
  161.6 2.4 %collective-permute-done.33.refs_8_ = bf16[3,2,256,384]{3,2,1,0:T(8,128)(2,1)} collective-permute-done((bf16[3,2,256,384]{3,2,1,0:T(8,128)(2,1)S(1)}, bf16[3,2,256,384]{3,2,1,0:T(8,128)(2,1)}, u32[]{:S(2)}, u32[]{:S(2)}) %collective-permute-start.33) | collective-permute-done | bytes 1179680 | tf_op jit(solution)/shard_map/cond/branch_1_fun/ppermute | solution.py:86
  164.0 0.0 collective-permute-start.34
  164.1 11.2 %own_products.4 = (bf16[24,512,384]{2,1,0:T(8,128)(2,1)S(1)}, bf16[3,24,256,512]{3,2,1,0:T(8,128)(2,1)}) custom-call(bf16[24,256,384]{2,1,0:T(8,128)(2,1)} %get-tuple-element.47.raw.own, f32[24,256]{1,0:T(8,128)S(1)} %get-tuple-element.78.scale), custom_call_target="tpu_custom_call" | custom-call | flops 2415919104 | bytes 20447232 | tf_op jit(solution)/shard_map/cond/branch_1_fun/own_products/pallas_call | solution.py:184
  175.2 0.3 slice.590.refs_1_
  175.5 0.0 collective-permute-done.36
  175.6 0.6 collective-permute-start.37
  176.2 3.6 %collective-permute-done.37 = f32[2,24,256]{2,1,0:T(8,128)S(1)} collective-permute-done((f32[2,24,256]{2,1,0:T(8,128)S(1)}, f32[2,24,256]{2,1,0:T(8,128)S(1)}, u32[]{:S(2)}, u32[]{:S(2)}) %collective-permute-start.37) | collective-permute-done | bytes 49184 | tf_op jit(solution)/shard_map/cond/branch_1_fun/ppermute | solution.py:86
  179.8 1.3 collective-permute-start.38
  181.1 2.8 %collective-permute-done.38 = f32[2,24,256]{2,1,0:T(8,128)S(1)} collective-permute-done((f32[2,24,256]{2,1,0:T(8,128)S(1)}, f32[2,24,256]{2,1,0:T(8,128)S(1)}, u32[]{:S(2)}, u32[]{:S(2)}) %collective-permute-start.38) | collective-permute-done | bytes 49184 | tf_op jit(solution)/shard_map/cond/branch_1_fun/ppermute | solution.py:86
  183.9 1.3 collective-permute-start.39
  185.2 3.7 %collective-permute-done.39 = f32[2,24,256]{2,1,0:T(8,128)S(1)} collective-permute-done((f32[2,24,256]{2,1,0:T(8,128)S(1)}, f32[2,24,256]{2,1,0:T(8,128)S(1)}, u32[]{:S(2)}, u32[]{:S(2)}) %collective-permute-start.39) | collective-permute-done | bytes 49184 | tf_op jit(solution)/shard_map/cond/branch_1_fun/ppermute | solution.py:86
  188.9 9.5 %branch_1_fun.4.refs_10_ = bf16[3,24,256,512]{3,2,1,0:T(8,128)(2,1)} custom-call(s32[24]{0:T(128)S(1)} %get-tuple-element.46.route.refs_0_, bf16[24,512,384]{2,1,0:T(8,128)(2,1)S(1)} %get-tuple-element.49.refs_1_, bf16[24,256,384]{2,1,0:T(8,128)(2,1)} %collective-permute-done.35.sister.refs_2_, ...), custom_call_target="tpu_custom_call", output_to_operand_aliasing={{}: (10, {})} | custom-call | flops 1610612736 | bytes 10485760 | tf_op jit(solution)/shard_map/cond/branch_1_fun/pallas_call | solution.py:430
  198.4 1.5 copy-done.5
  199.9 0.0 collective-permute-done.47.refs_9_
  199.9 1.7 copy-done.6
  201.6 10.6 %branch_1_fun.5.refs_9_ = bf16[3,24,256,512]{3,2,1,0:T(8,128)(2,1)} custom-call(s32[24]{0:T(128)S(1)} %get-tuple-element.46.route.refs_0_, bf16[24,512,384]{2,1,0:T(8,128)(2,1)S(1)} %get-tuple-element.49.refs_1_, bf16[24,256,384]{2,1,0:T(8,128)(2,1)} %collective-permute-done.35.sister.refs_2_, ...), custom_call_target="tpu_custom_call", output_to_operand_aliasing={{}: (10, {})} | custom-call | flops 1610612736 | bytes 10485760 | tf_op jit(solution)/shard_map/cond/branch_1_fun/pallas_call | solution.py:430
  212.2 4.1 %branch_1_fun.6.refs_9_ = bf16[3,24,256,512]{3,2,1,0:T(8,128)(2,1)} custom-call(s32[24]{0:T(128)S(1)} %get-tuple-element.46.route.refs_0_, bf16[8,512,384]{2,1,0:T(8,128)(2,1)S(1)} %slice.590.refs_1_, bf16[8,256,384]{2,1,0:T(8,128)(2,1)S(1)} %collective-permute-done.26.sister.refs_2_, ...), custom_call_target="tpu_custom_call", output_to_operand_aliasing={{}: (9, {})} | custom-call | flops 805306368 | bytes 5242880 | tf_op jit(solution)/shard_map/cond/branch_1_fun/pallas_call | solution.py:430
  216.3 0.0 collective-permute-done.34.refs_8_
  216.3 4.4 %branch_1_fun.7 = bf16[3,24,256,512]{3,2,1,0:T(8,128)(2,1)} custom-call(s32[24]{0:T(128)S(1)} %get-tuple-element.46.route.refs_0_, bf16[8,512,384]{2,1,0:T(8,128)(2,1)S(1)} %slice.590.refs_1_, bf16[8,256,384]{2,1,0:T(8,128)(2,1)S(1)} %collective-permute-done.26.sister.refs_2_, ...), custom_call_target="tpu_custom_call", output_to_operand_aliasing={{}: (9, {})} | custom-call | flops 805306368 | bytes 5242880 | tf_op jit(solution)/shard_map/cond/branch_1_fun/pallas_call | solution.py:430
  (19 shorter events, 0.1 us)
Async XLA Ops:
  0.0 5.4 %copy-start.8 = (s32[256]{0:T(256)S(1)}, s32[256]{0:T(256)}, u32[]{:S(2)}) copy-start(s32[256]{0:T(256)} %param.7) | copy-start | bytes 3076
  0.0 0.7 copy-start.7
  5.6 47.9 %collective-permute-start.35 = (bf16[24,256,384]{2,1,0:T(8,128)(2,1)}, bf16[24,256,384]{2,1,0:T(8,128)(2,1)}, u32[]{:S(2)}, u32[]{:S(2)}) collective-permute-start(bf16[24,256,384]{2,1,0:T(8,128)(2,1)} %get-tuple-element.47.raw.own), channel_id=1, source_target_pairs={{0,4},{4,0},{8,12},{12,8},{16,20},{20,16},{24,28},{28,24},{1,5},{5... | collective-permute-start | bytes 14155784 | tf_op jit(solution)/shard_map/cond/branch_1_fun/ppermute | solution.py:86
  6.2 37.5 %collective-permute-start.40 = (bf16[8,256,384]{2,1,0:T(8,128)(2,1)S(1)}, bf16[8,256,384]{2,1,0:T(8,128)(2,1)S(1)}, u32[]{:S(2)}, u32[]{:S(2)}) collective-permute-start(bf16[8,256,384]{2,1,0:T(8,128)(2,1)S(1)} %get-tuple-element.50), channel_id=1, source_target_pairs={{0,8},{4,12},{8,0},{12,4},{16,24},{20,28},{24,16},{28,20},{1,9},{5... | collective-permute-start | bytes 4718600 | tf_op jit(solution)/shard_map/cond/branch_1_fun/ppermute | solution.py:86
  8.7 36.4 %collective-permute-start.44 = (bf16[8,256,384]{2,1,0:T(8,128)(2,1)S(1)}, bf16[8,256,384]{2,1,0:T(8,128)(2,1)S(1)}, u32[]{:S(2)}, u32[]{:S(2)}) collective-permute-start(bf16[8,256,384]{2,1,0:T(8,128)(2,1)S(1)} %get-tuple-element.51), channel_id=1, source_target_pairs={{0,16},{4,20},{8,24},{12,28},{16,0},{20,4},{24,8},{28,12},{1,17},{... | collective-permute-start | bytes 4718600 | tf_op jit(solution)/shard_map/cond/branch_1_fun/ppermute | solution.py:86
  43.7 9.7 %collective-permute-start.41 = (bf16[8,256,384]{2,1,0:T(8,128)(2,1)S(1)}, bf16[8,256,384]{2,1,0:T(8,128)(2,1)}, u32[]{:S(2)}, u32[]{:S(2)}) collective-permute-start(bf16[8,256,384]{2,1,0:T(8,128)(2,1)S(1)} %collective-permute-done.40.near.refs_4_), channel_id=1, source_target_pairs={{0,4},{4,0},{8,12},{12,8},{16,20},{20,16},{24,28},{28,24},{1,5},{5... | collective-permute-start | bytes 4718600 | tf_op jit(solution)/shard_map/cond/branch_1_fun/ppermute | solution.py:86
  45.2 11.9 %collective-permute-start.45 = (bf16[8,256,384]{2,1,0:T(8,128)(2,1)S(1)}, bf16[8,256,384]{2,1,0:T(8,128)(2,1)}, u32[]{:S(2)}, u32[]{:S(2)}) collective-permute-start(bf16[8,256,384]{2,1,0:T(8,128)(2,1)S(1)} %collective-permute-done.44.near.refs_7_), channel_id=1, source_target_pairs={{0,4},{4,0},{8,12},{12,8},{16,20},{20,16},{24,28},{28,24},{1,5},{5... | collective-permute-start | bytes 4718600 | tf_op jit(solution)/shard_map/cond/branch_1_fun/ppermute | solution.py:86
  48.5 12.1 %collective-permute-start.24 = (f32[12,256]{1,0:T(8,128)S(1)}, f32[12,256]{1,0:T(8,128)S(1)}, u32[]{:S(2)}, u32[]{:S(2)}) collective-permute-start(f32[12,256]{1,0:T(8,128)S(1)} %get-tuple-element.125), channel_id=1, source_target_pairs={{0,1},{1,2},{2,3},{4,5},{5,6},{6,7},{8,9},{9,10},{10,11},{12,13},{... | collective-permute-start | bytes 36872 | tf_op jit(solution)/shard_map/cond/branch_1_fun/ppermute | solution.py:26
  52.0 8.6 %collective-permute-start.25 = (f32[12,256]{1,0:T(8,128)S(1)}, f32[12,256]{1,0:T(8,128)S(1)}, u32[]{:S(2)}, u32[]{:S(2)}) collective-permute-start(f32[12,256]{1,0:T(8,128)S(1)} %get-tuple-element.126), channel_id=1, source_target_pairs={{1,0},{2,1},{3,2},{5,4},{6,5},{7,6},{9,8},{10,9},{11,10},{13,12},{... | collective-permute-start | bytes 36872 | tf_op jit(solution)/shard_map/cond/branch_1_fun/ppermute | solution.py:28
  55.8 74.1 %collective-permute-start.42 = (bf16[3,4,256,384]{3,2,1,0:T(8,128)(2,1)S(1)}, bf16[3,4,256,384]{3,2,1,0:T(8,128)(2,1)S(1)}, u32[]{:S(2)}, u32[]{:S(2)}) collective-permute-start(bf16[3,4,256,384]{3,2,1,0:T(8,128)(2,1)S(1)} %send.18), channel_id=1, source_target_pairs={{0,16},{4,20},{8,24},{12,28},{16,0},{20,4},{24,8},{28,12},{1,17},{... | collective-permute-start | bytes 7077896 | tf_op jit(solution)/shard_map/cond/branch_1_fun/ppermute | solution.py:86
  59.5 70.5 %collective-permute-start.46 = (bf16[3,4,256,384]{3,2,1,0:T(8,128)(2,1)S(1)}, bf16[3,4,256,384]{3,2,1,0:T(8,128)(2,1)S(1)}, u32[]{:S(2)}, u32[]{:S(2)}) collective-permute-start(bf16[3,4,256,384]{3,2,1,0:T(8,128)(2,1)S(1)} %send.19), channel_id=1, source_target_pairs={{0,8},{4,12},{8,0},{12,4},{16,24},{20,28},{24,16},{28,20},{1,9},{5... | collective-permute-start | bytes 7077896 | tf_op jit(solution)/shard_map/cond/branch_1_fun/ppermute | solution.py:86
  62.8 66.6 %collective-permute-start.27 = (bf16[4,256,384]{2,1,0:T(8,128)(2,1)S(1)}, bf16[4,256,384]{2,1,0:T(8,128)(2,1)S(1)}, u32[]{:S(2)}, u32[]{:S(2)}) collective-permute-start(bf16[4,256,384]{2,1,0:T(8,128)(2,1)S(1)} %get-tuple-element.124), channel_id=1, source_target_pairs={{0,8},{4,12},{8,0},{12,4},{16,24},{20,28},{24,16},{28,20},{1,9},{5... | collective-permute-start | bytes 2359304 | tf_op jit(solution)/shard_map/cond/branch_1_fun/ppermute | solution.py:86
  63.9 67.8 %collective-permute-start.26 = (bf16[8,256,384]{2,1,0:T(8,128)(2,1)S(1)}, bf16[8,256,384]{2,1,0:T(8,128)(2,1)S(1)}, u32[]{:S(2)}, u32[]{:S(2)}) collective-permute-start(bf16[8,256,384]{2,1,0:T(8,128)(2,1)S(1)} %multiply_convert_fusion.1.own), channel_id=1, source_target_pairs={{0,4},{4,0},{8,12},{12,8},{16,20},{20,16},{24,28},{28,24},{1,5},{5... | collective-permute-start | bytes 4718600 | tf_op jit(solution)/shard_map/cond/branch_1_fun/ppermute | solution.py:86
  63.9 65.6 %collective-permute-start.31 = (bf16[4,256,384]{2,1,0:T(8,128)(2,1)S(1)}, bf16[4,256,384]{2,1,0:T(8,128)(2,1)S(1)}, u32[]{:S(2)}, u32[]{:S(2)}) collective-permute-start(bf16[4,256,384]{2,1,0:T(8,128)(2,1)S(1)} %get-tuple-element.123), channel_id=1, source_target_pairs={{0,16},{4,20},{8,24},{12,28},{16,0},{20,4},{24,8},{28,12},{1,17},{... | collective-permute-start | bytes 2359304 | tf_op jit(solution)/shard_map/cond/branch_1_fun/ppermute | solution.py:86
  129.4 2.3 %collective-permute-start.28 = (bf16[4,256,384]{2,1,0:T(8,128)(2,1)S(1)}, bf16[4,256,384]{2,1,0:T(8,128)(2,1)S(1)}, u32[]{:S(2)}, u32[]{:S(2)}) collective-permute-start(bf16[4,256,384]{2,1,0:T(8,128)(2,1)S(1)} %collective-permute-done.27.near.refs_3_), channel_id=1, source_target_pairs={{0,4},{4,0},{8,12},{12,8},{16,20},{20,16},{24,28},{28,24},{1,5},{5... | collective-permute-start | bytes 2359304 | tf_op jit(solution)/shard_map/cond/branch_1_fun/ppermute | solution.py:86
  129.5 4.9 %collective-permute-start.32 = (bf16[4,256,384]{2,1,0:T(8,128)(2,1)S(1)}, bf16[4,256,384]{2,1,0:T(8,128)(2,1)S(1)}, u32[]{:S(2)}, u32[]{:S(2)}) collective-permute-start(bf16[4,256,384]{2,1,0:T(8,128)(2,1)S(1)} %collective-permute-done.31.near.refs_6_), channel_id=1, source_target_pairs={{0,4},{4,0},{8,12},{12,8},{16,20},{20,16},{24,28},{28,24},{1,5},{5... | collective-permute-start | bytes 2359304 | tf_op jit(solution)/shard_map/cond/branch_1_fun/ppermute | solution.py:86
  130.0 68.4 %collective-permute-start.43 = (bf16[3,4,256,384]{3,2,1,0:T(8,128)(2,1)S(1)}, bf16[3,4,256,384]{3,2,1,0:T(8,128)(2,1)S(1)}, u32[]{:S(2)}, u32[]{:S(2)}) collective-permute-start(bf16[3,4,256,384]{3,2,1,0:T(8,128)(2,1)S(1)} %collective-permute-done.42.refs_6_), channel_id=1, source_target_pairs={{0,4},{4,0},{8,12},{12,8},{16,20},{20,16},{24,28},{28,24},{1,5},{5... | collective-permute-start | bytes 7077896 | tf_op jit(solution)/shard_map/cond/branch_1_fun/ppermute | solution.py:86
  130.0 69.9 %collective-permute-start.47 = (bf16[3,4,256,384]{3,2,1,0:T(8,128)(2,1)S(1)}, bf16[3,4,256,384]{3,2,1,0:T(8,128)(2,1)}, u32[]{:S(2)}, u32[]{:S(2)}) collective-permute-start(bf16[3,4,256,384]{3,2,1,0:T(8,128)(2,1)S(1)} %collective-permute-done.46.refs_9_), channel_id=1, source_target_pairs={{0,4},{4,0},{8,12},{12,8},{16,20},{20,16},{24,28},{28,24},{1,5},{5... | collective-permute-start | bytes 7077896 | tf_op jit(solution)/shard_map/cond/branch_1_fun/ppermute | solution.py:86
  133.6 28.1 %collective-permute-start.29 = (bf16[3,2,256,384]{3,2,1,0:T(8,128)(2,1)S(1)}, bf16[3,2,256,384]{3,2,1,0:T(8,128)(2,1)S(1)}, u32[]{:S(2)}, u32[]{:S(2)}) collective-permute-start(bf16[3,2,256,384]{3,2,1,0:T(8,128)(2,1)S(1)} %send.16), channel_id=1, source_target_pairs={{0,16},{4,20},{8,24},{12,28},{16,0},{20,4},{24,8},{28,12},{1,17},{... | collective-permute-start | bytes 3538952 | tf_op jit(solution)/shard_map/cond/branch_1_fun/ppermute | solution.py:86
  136.1 27.9 %collective-permute-start.33 = (bf16[3,2,256,384]{3,2,1,0:T(8,128)(2,1)S(1)}, bf16[3,2,256,384]{3,2,1,0:T(8,128)(2,1)}, u32[]{:S(2)}, u32[]{:S(2)}) collective-permute-start(bf16[3,2,256,384]{3,2,1,0:T(8,128)(2,1)S(1)} %send.17), channel_id=1, source_target_pairs={{0,8},{4,12},{8,0},{12,4},{16,24},{20,28},{24,16},{28,20},{1,9},{5... | collective-permute-start | bytes 3538952 | tf_op jit(solution)/shard_map/cond/branch_1_fun/ppermute | solution.py:86
  136.8 38.8 %collective-permute-start.36 = (f32[24,256]{1,0:T(8,128)S(1)}, f32[24,256]{1,0:T(8,128)S(1)}, u32[]{:S(2)}, u32[]{:S(2)}) collective-permute-start(f32[24,256]{1,0:T(8,128)S(1)} %get-tuple-element.78.scale), channel_id=1, source_target_pairs={{0,4},{4,0},{8,12},{12,8},{16,20},{20,16},{24,28},{28,24},{1,5},{5... | collective-permute-start | bytes 73736 | tf_op jit(solution)/shard_map/cond/branch_1_fun/ppermute | solution.py:86
  161.6 54.7 %collective-permute-start.30 = (bf16[3,2,256,384]{3,2,1,0:T(8,128)(2,1)S(1)}, bf16[3,2,256,384]{3,2,1,0:T(8,128)(2,1)}, u32[]{:S(2)}, u32[]{:S(2)}) collective-permute-start(bf16[3,2,256,384]{3,2,1,0:T(8,128)(2,1)S(1)} %collective-permute-done.29.refs_5_), channel_id=1, source_target_pairs={{0,4},{4,0},{8,12},{12,8},{16,20},{20,16},{24,28},{28,24},{1,5},{5... | collective-permute-start | bytes 3538952 | tf_op jit(solution)/shard_map/cond/branch_1_fun/ppermute | solution.py:86
  164.0 52.3 %collective-permute-start.34 = (bf16[3,2,256,384]{3,2,1,0:T(8,128)(2,1)}, bf16[3,2,256,384]{3,2,1,0:T(8,128)(2,1)}, u32[]{:S(2)}, u32[]{:S(2)}) collective-permute-start(bf16[3,2,256,384]{3,2,1,0:T(8,128)(2,1)} %collective-permute-done.33.refs_8_), channel_id=1, source_target_pairs={{0,4},{4,0},{8,12},{12,8},{16,20},{20,16},{24,28},{28,24},{1,5},{5... | collective-permute-start | bytes 3538952 | tf_op jit(solution)/shard_map/cond/branch_1_fun/ppermute | solution.py:86
  175.6 4.2 %collective-permute-start.37 = (f32[2,24,256]{2,1,0:T(8,128)S(1)}, f32[2,24,256]{2,1,0:T(8,128)S(1)}, u32[]{:S(2)}, u32[]{:S(2)}) collective-permute-start(f32[2,24,256]{2,1,0:T(8,128)S(1)} %pad_maximum_fusion.3), channel_id=1, source_target_pairs={{0,8},{4,12},{8,0},{12,4},{16,24},{20,28},{24,16},{28,20},{1,9},{5... | collective-permute-start | bytes 147464 | tf_op jit(solution)/shard_map/cond/branch_1_fun/ppermute | solution.py:86
  179.8 4.1 %collective-permute-start.38 = (f32[2,24,256]{2,1,0:T(8,128)S(1)}, f32[2,24,256]{2,1,0:T(8,128)S(1)}, u32[]{:S(2)}, u32[]{:S(2)}) collective-permute-start(f32[2,24,256]{2,1,0:T(8,128)S(1)} %pad_maximum_fusion.3), channel_id=1, source_target_pairs={{0,16},{4,20},{8,24},{12,28},{16,0},{20,4},{24,8},{28,12},{1,17},{... | collective-permute-start | bytes 147464 | tf_op jit(solution)/shard_map/cond/branch_1_fun/ppermute | solution.py:86
  183.9 5.0 %collective-permute-start.39 = (f32[2,24,256]{2,1,0:T(8,128)S(1)}, f32[2,24,256]{2,1,0:T(8,128)S(1)}, u32[]{:S(2)}, u32[]{:S(2)}) collective-permute-start(f32[2,24,256]{2,1,0:T(8,128)S(1)} %pad_maximum_fusion.3), channel_id=1, source_target_pairs={{0,24},{4,28},{8,16},{12,20},{16,8},{20,12},{24,0},{28,4},{1,25},{... | collective-permute-start | bytes 147464 | tf_op jit(solution)/shard_map/cond/branch_1_fun/ppermute | solution.py:86
  198.4 1.5 copy-start.5
  199.9 1.7 copy-start.6

commit v4 on v3

--- a/solution.py
+++ b/solution.py
@@ -302,7 +302,7 @@
 
 
 def pair_kernel(parts, offset, which, raw, inside, unroll, route, both, sister, *refs):
-    out_ref, held, done, done_out, owned, scale, owned_in, held_in, scale_in = refs[-9:]
+    out_ref, held, done, done_out, owned, scale, pure, owned_in, held_in, scale_in = refs[-10:]
     if raw:
         scales, refs = refs[0], refs[1:]
     half = route[HALF] if which == TAKE else 1 - route[HALF]
@@ -323,17 +323,18 @@
         for r in range(ROUNDS):
             source = scales.at[route[OFFSETS + r]]
             pltpu.make_async_copy(source, scale.at[r], scale_in.at[r]).start()
-    if not inside:
+
+    def fetch(j):
+        pltpu.make_async_copy(both.at[offset + bin_of(j)], owned.at[j], owned_in.at[j]).start()
         for side, part, near, far, got in sides:
-            for local in range(part):
-                j = local + (parts[0] if side else 0)
-                at = half * part + local
-                start = 2 * parts[0] if side else 0
-                pltpu.make_async_copy(both.at[offset + start + at], owned.at[j], owned_in.at[j]).start()
+
+            @pl.when((j >= parts[0]) == (side == 1))
+            def _():
+                at = half * part + j - (parts[0] if side else 0)
                 for r in range(ROUNDS):
                     place = place_of(side, r)
                     for chosen, source in (
-                        (place <= 1, sister.at[start + at]),
+                        (place <= 1, sister.at[bin_of(j)]),
                         (place == 2, near.at[at]),
                         (place == 3, far.at[at]),
                     ):
@@ -341,6 +342,10 @@
                         @pl.when(chosen)
                         def _():
                             pltpu.make_async_copy(source, held.at[r, j], held_in.at[r, j]).start()
+
+    if not inside:
+        for j in range(AHEAD):
+            fetch(jnp.int32(j))
 
     if raw:
         for r in range(ROUNDS):
@@ -385,17 +390,36 @@
     def compute(j):
         own = both[bin_of(j)] if inside else owned[j]
         for r in range(ROUNDS):
-            other = held[r, j]
-            if raw:
-                rows = column(scale[r, pl.ds(offset + bin_of(j), 1), :])
-                other = (other.astype(jnp.float32) * rows).astype(jnp.bfloat16)
+            other = pure[lax.rem(j, 2), r] if raw else held[r, j]
             multiply(own, other, done, j, r)
+
+    def whiten(j):
+        for r in range(ROUNDS):
+            rows = column(scale[r, pl.ds(offset + bin_of(j), 1), :])
+            white = held[r, j].astype(jnp.float32) * rows
+            pure[lax.rem(j, 2), r] = white.astype(jnp.bfloat16)
 
     def leave(j):
         target = out_ref.at[pl.ds(1, ROUNDS), offset + bin_of(j)]
         return pltpu.make_async_copy(done.at[j], target, done_out.at[j])
 
     def step(i, carry):
+        if not inside:
+
+            @pl.when(i + AHEAD < total)
+            def _():
+                fetch(i + AHEAD)
+
+        if raw:
+
+            @pl.when(i + 1 < total)
+            def _():
+                ready(i + 1)
+
+            compute(i)
+            whiten(jnp.minimum(i + 1, total - 1))
+            leave(i).start()
+            return carry
         for k in range(unroll):
             ready(i * unroll + k)
         for k in range(unroll):
@@ -403,6 +427,9 @@
             leave(i * unroll + k).start()
         return carry
 
+    if raw:
+        ready(jnp.int32(0))
+        whiten(jnp.int32(0))
     lax.fori_loop(0, total // unroll, step, 0)
     for j in range(total):
         leave(j).wait()
@@ -440,6 +467,7 @@
             pltpu.SemaphoreType.DMA((total,)),
             pltpu.VMEM((fetched, 2 * chans, columns), jnp.bfloat16),
             pltpu.VMEM((ROUNDS, bins, chans), jnp.float32),
+            pltpu.VMEM((2, ROUNDS, chans if raw else 8, columns), jnp.bfloat16),
             pltpu.SemaphoreType.DMA((total,)),
             pltpu.SemaphoreType.DMA((ROUNDS, total)),
             pltpu.SemaphoreType.DMA((ROUNDS,)),
@@ -450,7 +478,7 @@
             bytes_accessed=8 * total * chans * (columns + chans),
             transcendentals=0,
         ),
-        compiler_params=pltpu.CompilerParams(vmem_limit_bytes=(16 if inside else 20) * MIB),
+        compiler_params=pltpu.CompilerParams(vmem_limit_bytes=(16 if inside else 21) * MIB),
     )(*operands, result)
 
 
@@ -530,6 +558,7 @@
 
 PAIRS = ((4, 4), (2, 2))
 UNROLL = (1, 2)
+AHEAD = 3
 CASES = [(2, PAIRS), (3, PAIRS), (4, PAIRS)]
 
 

time: 222 us -> 221 us (level)
  transfers between devices with their start and end apart: 24 -> 24, of which waited for: 9 -> 9; matrix products, arithmetic and copies ran while one was open for 3% -> 3% of each run, Pallas kernels for 16% -> 15%
where the time goes in v4:
time: 221 us; the launch traced here: 220 us
  waiting for transfers between devices  139 us (63%)
  Pallas kernels  50.9 us (23%)
  starting transfers between devices  19 us (9%)
  other arithmetic  5.32 us (2%)
  local copies, waits for them, and re-layouts  4.52 us (2%)
    ppermute x22, waiting for transfers between devices, swap(): lax.ppermute(values, 'chan', [(i, i ^ offset) for i in range(lax.axis_siz...  139 us
    pallas_call x4, Pallas kernels, pair_products(): pl.pallas_call(lambda *refs: pair_kernel(parts, offset, which, raw, insid...  27.4 us
    ppermute x22, starting transfers between devices, swap(): lax.ppermute(values, 'chan', [(i, i ^ offset) for i in range(lax.axis_siz...  14.2 us
    pallas_call x1, Pallas kernels, own_products(): pl.pallas_call(own_kernel, out_shape=(jax.ShapeDtypeStruct((bins, 2 * cha...  11.2 us
    pallas_call x4, Pallas kernels, sends(): pl.pallas_call(functools.partial(send_kernel, side, start), out_shape=jax...  8.33 us
  transfers between devices with their start and end apart: 24, of which 9 were waited for; matrix products, arithmetic and copies ran while one was open for 3% of the time, Pallas kernels for 15%

profile of v4, /device:TPU:0, one launch (start us, length us, event | category | flops | bytes accessed | tf_op | source)
XLA Modules:
  0.0 220.2 jit_solution(2561007573405660993)
XLA Ops:
  0.0 0.7 copy-done.7
  0.7 4.1 %start.1 = (s32[24]{0:T(128)S(1)}, s32[1]{0:T(128)}, bf16[8,256,384]{2,1,0:T(8,128)(2,1)S(1)}, bf16[8,256,384]{2,1,0:T(8,128)(2,1)S(1)}) custom-call(s32[1]{0:T(128)} %bitcast.6.device_ref, s32[2,8]{1,0:T(2,128)S(1)} %copy-done.7, bf16[24,256,384]{2,1,0:T(8,128)(2,1)} %spectra.1), custom_call_target="tpu_custom_call" | custom-call | tf_op jit(solution)/shard_map/start/pallas_call | solution.py:238
  5.4 214.5 %conditional.1 = (bf16[3,24,256,512]{3,2,1,0:T(8,128)(2,1)}) conditional(s32[]{:T(128)} %bitcast.7, (bf16[24,256,384]{2,1,0:T(8,128)(2,1)}, s32[256]{0:T(256)S(1)}, s32[24]{0:T(128)S(1)}, bf16[8,256,384]{2,1,0:T(8,128)(2,1)S(1)}, bf16[8,256,384]{2,1,0:T(8,128)(2,1)S(1)}) %tuple.135, (bf16[24,256,384]{2,1,0:T(8,128)(2,1)}, ...), branch_computations={%region_0.0_spmd, %region_2.0_spmd, %region_4.0_spmd} | conditional | flops 7257975808 | bytes 286149952 | solution.py:569
  5.6 0.6 collective-permute-start.35
  6.2 2.6 %collective-permute-start.40 = (bf16[8,256,384]{2,1,0:T(8,128)(2,1)S(1)}, bf16[8,256,384]{2,1,0:T(8,128)(2,1)S(1)}, u32[]{:S(2)}, u32[]{:S(2)}) collective-permute-start(bf16[8,256,384]{2,1,0:T(8,128)(2,1)S(1)} %get-tuple-element.50), channel_id=1, source_target_pairs={{0,8},{4,12},{8,0},{12,4},{16,24},{20,28},{24,16},{28,20},{1,9},{5... | collective-permute-start | bytes 4718600 | tf_op jit(solution)/shard_map/cond/branch_1_fun/ppermute | solution.py:86
  8.7 1.5 collective-permute-start.44
  10.3 33.5 %collective-permute-done.40.near.refs_4_ = bf16[8,256,384]{2,1,0:T(8,128)(2,1)S(1)} collective-permute-done((bf16[8,256,384]{2,1,0:T(8,128)(2,1)S(1)}, bf16[8,256,384]{2,1,0:T(8,128)(2,1)S(1)}, u32[]{:S(2)}, u32[]{:S(2)}) %collective-permute-start.40) | collective-permute-done | bytes 1572896 | tf_op jit(solution)/shard_map/cond/branch_1_fun/ppermute | solution.py:86
  43.7 0.0 collective-permute-start.41
  43.7 1.5 collective-permute-done.44.near.refs_7_
  45.2 0.0 collective-permute-start.45
  45.2 3.3 %multiply_reduce_fusion.1 = f32[24,256]{1,0:T(8,128)S(1)} fusion(bf16[24,256,384]{2,1,0:T(8,128)(2,1)} %get-tuple-element.47.raw.own), kind=kLoop, calls=%fused_computation.141 | loop fusion | flops 7071744 | bytes 4743168 | tf_op jit(solution)/shard_map/cond/branch_1_fun/reduce_sum | solution.py:46
  48.5 3.5 %collective-permute-start.24 = (f32[12,256]{1,0:T(8,128)S(1)}, f32[12,256]{1,0:T(8,128)S(1)}, u32[]{:S(2)}, u32[]{:S(2)}) collective-permute-start(f32[12,256]{1,0:T(8,128)S(1)} %get-tuple-element.125), channel_id=1, source_target_pairs={{0,1},{1,2},{2,3},{4,5},{5,6},{6,7},{8,9},{9,10},{10,11},{12,13},{... | collective-permute-start | bytes 36872 | tf_op jit(solution)/shard_map/cond/branch_1_fun/ppermute | solution.py:26
  52.0 1.3 collective-permute-start.25
  53.4 0.1 fusion.228
  53.5 0.0 collective-permute-done.41.far.refs_5_
  53.5 0.0 collective-permute-done.35.sister.refs_2_
  53.5 2.3 %send.18 = bf16[3,4,256,384]{3,2,1,0:T(8,128)(2,1)S(1)} custom-call(s32[24]{0:T(128)S(1)} %get-tuple-element.46.route.refs_0_, bf16[24,256,384]{2,1,0:T(8,128)(2,1)} %get-tuple-element.47.raw.own, bf16[24,256,384]{2,1,0:T(8,128)(2,1)} %collective-permute-done.35.sister.refs_2_, bf16[8,256,384]{2,1,0:T(8,128)(2,1)S(1)} %collective-permute-done.40.near.refs_4_, ...), custom_call_target="tpu_custom_call" | custom-call | bytes 4718592 | tf_op jit(solution)/shard_map/cond/branch_1_fun/send/pallas_call | solution.py:286
  55.8 1.3 collective-permute-start.42
  57.1 0.0 collective-permute-done.45.far.refs_8_
  57.1 2.4 %send.19 = bf16[3,4,256,384]{3,2,1,0:T(8,128)(2,1)S(1)} custom-call(s32[24]{0:T(128)S(1)} %get-tuple-element.46.route.refs_0_, bf16[24,256,384]{2,1,0:T(8,128)(2,1)} %get-tuple-element.47.raw.own, bf16[24,256,384]{2,1,0:T(8,128)(2,1)} %collective-permute-done.35.sister.refs_2_, bf16[8,256,384]{2,1,0:T(8,128)(2,1)S(1)} %collective-permute-done.44.near.refs_7_, ...), custom_call_target="tpu_custom_call" | custom-call | bytes 4718592 | tf_op jit(solution)/shard_map/cond/branch_1_fun/send/pallas_call | solution.py:286
  59.5 1.1 collective-permute-start.46
  60.6 0.1 fusion.229
  60.7 0.0 collective-permute-done.24
  60.7 0.0 collective-permute-done.25
  60.7 0.2 constant_dynamic-update-slice_fusion.9
  60.9 1.8 multiply_convert_fusion.1.own
  62.6 0.2 fusion.226
  62.8 1.1 collective-permute-start.27
  63.9 0.0 collective-permute-start.26
  63.9 0.5 collective-permute-start.31
  64.4 65.1 %collective-permute-done.27.near.refs_3_ = bf16[4,256,384]{2,1,0:T(8,128)(2,1)S(1)} collective-permute-done((bf16[4,256,384]{2,1,0:T(8,128)(2,1)S(1)}, bf16[4,256,384]{2,1,0:T(8,128)(2,1)S(1)}, u32[]{:S(2)}, u32[]{:S(2)}) %collective-permute-start.27) | collective-permute-done | bytes 786464 | tf_op jit(solution)/shard_map/cond/branch_1_fun/ppermute | solution.py:86
  129.4 0.0 collective-permute-start.28
  129.4 0.0 collective-permute-done.31.near.refs_6_
  129.5 0.5 collective-permute-start.32
  130.0 0.1 collective-permute-start.43
  130.0 0.0 collective-permute-done.46.refs_9_
  130.0 0.4 collective-permute-start.47
  130.5 1.3 collective-permute-done.28.far.refs_4_
  131.7 1.8 send.16
  133.6 0.8 collective-permute-start.29
  134.3 0.0 collective-permute-done.32.far.refs_7_
  134.3 1.8 send.17
  136.1 0.6 collective-permute-start.33
  136.8 25.0 %collective-permute-done.29.refs_5_ = bf16[3,2,256,384]{3,2,1,0:T(8,128)(2,1)} collective-permute-done((bf16[3,2,256,384]{3,2,1,0:T(8,128)(2,1)S(1)}, bf16[3,2,256,384]{3,2,1,0:T(8,128)(2,1)}, u32[]{:S(2)}, u32[]{:S(2)}) %collective-permute-start.29) | collective-permute-done | bytes 1179680 | tf_op jit(solution)/shard_map/cond/branch_1_fun/ppermute | solution.py:86
  161.7 2.3 %collective-permute-done.33.refs_8_ = bf16[3,2,256,384]{3,2,1,0:T(8,128)(2,1)} collective-permute-done((bf16[3,2,256,384]{3,2,1,0:T(8,128)(2,1)S(1)}, bf16[3,2,256,384]{3,2,1,0:T(8,128)(2,1)}, u32[]{:S(2)}, u32[]{:S(2)}) %collective-permute-start.33) | collective-permute-done | bytes 1179680 | tf_op jit(solution)/shard_map/cond/branch_1_fun/ppermute | solution.py:86
  164.0 0.0 collective-permute-start.34
  164.1 11.2 %own_products.4 = (bf16[24,512,384]{2,1,0:T(8,128)(2,1)S(1)}, bf16[3,24,256,512]{3,2,1,0:T(8,128)(2,1)}) custom-call(bf16[24,256,384]{2,1,0:T(8,128)(2,1)} %get-tuple-element.47.raw.own, f32[24,256]{1,0:T(8,128)S(1)} %get-tuple-element.78.scale), custom_call_target="tpu_custom_call" | custom-call | flops 2415919104 | bytes 20447232 | tf_op jit(solution)/shard_map/cond/branch_1_fun/own_products/pallas_call | solution.py:184
  175.2 0.3 slice.590.refs_1_
  175.5 0.0 collective-permute-done.36
  175.6 0.6 collective-permute-start.37
  176.2 3.6 %collective-permute-done.37 = f32[2,24,256]{2,1,0:T(8,128)S(1)} collective-permute-done((f32[2,24,256]{2,1,0:T(8,128)S(1)}, f32[2,24,256]{2,1,0:T(8,128)S(1)}, u32[]{:S(2)}, u32[]{:S(2)}) %collective-permute-start.37) | collective-permute-done | bytes 49184 | tf_op jit(solution)/shard_map/cond/branch_1_fun/ppermute | solution.py:86
  179.8 1.3 collective-permute-start.38
  181.1 2.8 %collective-permute-done.38 = f32[2,24,256]{2,1,0:T(8,128)S(1)} collective-permute-done((f32[2,24,256]{2,1,0:T(8,128)S(1)}, f32[2,24,256]{2,1,0:T(8,128)S(1)}, u32[]{:S(2)}, u32[]{:S(2)}) %collective-permute-start.38) | collective-permute-done | bytes 49184 | tf_op jit(solution)/shard_map/cond/branch_1_fun/ppermute | solution.py:86
  183.9 1.3 collective-permute-start.39
  185.2 3.7 %collective-permute-done.39 = f32[2,24,256]{2,1,0:T(8,128)S(1)} collective-permute-done((f32[2,24,256]{2,1,0:T(8,128)S(1)}, f32[2,24,256]{2,1,0:T(8,128)S(1)}, u32[]{:S(2)}, u32[]{:S(2)}) %collective-permute-start.39) | collective-permute-done | bytes 49184 | tf_op jit(solution)/shard_map/cond/branch_1_fun/ppermute | solution.py:86
  188.9 8.7 %branch_1_fun.4.refs_10_ = bf16[3,24,256,512]{3,2,1,0:T(8,128)(2,1)} custom-call(s32[24]{0:T(128)S(1)} %get-tuple-element.46.route.refs_0_, bf16[24,512,384]{2,1,0:T(8,128)(2,1)S(1)} %get-tuple-element.49.refs_1_, bf16[24,256,384]{2,1,0:T(8,128)(2,1)} %collective-permute-done.35.sister.refs_2_, ...), custom_call_target="tpu_custom_call", output_to_operand_aliasing={{}: (10, {})} | custom-call | flops 1610612736 | bytes 10485760 | tf_op jit(solution)/shard_map/cond/branch_1_fun/pallas_call | solution.py:457
  197.6 0.0 collective-permute-done.43.refs_6_
  197.6 1.5 copy-done.5
  199.1 1.7 copy-done.6
  200.7 9.8 %branch_1_fun.5.refs_9_ = bf16[3,24,256,512]{3,2,1,0:T(8,128)(2,1)} custom-call(s32[24]{0:T(128)S(1)} %get-tuple-element.46.route.refs_0_, bf16[24,512,384]{2,1,0:T(8,128)(2,1)S(1)} %get-tuple-element.49.refs_1_, bf16[24,256,384]{2,1,0:T(8,128)(2,1)} %collective-permute-done.35.sister.refs_2_, ...), custom_call_target="tpu_custom_call", output_to_operand_aliasing={{}: (10, {})} | custom-call | flops 1610612736 | bytes 10485760 | tf_op jit(solution)/shard_map/cond/branch_1_fun/pallas_call | solution.py:457
  210.6 4.4 %branch_1_fun.6.refs_9_ = bf16[3,24,256,512]{3,2,1,0:T(8,128)(2,1)} custom-call(s32[24]{0:T(128)S(1)} %get-tuple-element.46.route.refs_0_, bf16[8,512,384]{2,1,0:T(8,128)(2,1)S(1)} %slice.590.refs_1_, bf16[8,256,384]{2,1,0:T(8,128)(2,1)S(1)} %collective-permute-done.26.sister.refs_2_, ...), custom_call_target="tpu_custom_call", output_to_operand_aliasing={{}: (9, {})} | custom-call | flops 805306368 | bytes 5242880 | tf_op jit(solution)/shard_map/cond/branch_1_fun/pallas_call | solution.py:457
  215.0 0.0 collective-permute-done.30.refs_5_
  215.0 0.0 collective-permute-done.34.refs_8_
  215.0 4.4 %branch_1_fun.7 = bf16[3,24,256,512]{3,2,1,0:T(8,128)(2,1)} custom-call(s32[24]{0:T(128)S(1)} %get-tuple-element.46.route.refs_0_, bf16[8,512,384]{2,1,0:T(8,128)(2,1)S(1)} %slice.590.refs_1_, bf16[8,256,384]{2,1,0:T(8,128)(2,1)S(1)} %collective-permute-done.26.sister.refs_2_, ...), custom_call_target="tpu_custom_call", output_to_operand_aliasing={{}: (9, {})} | custom-call | flops 805306368 | bytes 5242880 | tf_op jit(solution)/shard_map/cond/branch_1_fun/pallas_call | solution.py:457
  (19 shorter events, 0.1 us)
Async XLA Ops:
  0.0 5.4 %copy-start.8 = (s32[256]{0:T(256)S(1)}, s32[256]{0:T(256)}, u32[]{:S(2)}) copy-start(s32[256]{0:T(256)} %param.7) | copy-start | bytes 3076
  0.0 0.7 copy-start.7
  5.6 47.9 %collective-permute-start.35 = (bf16[24,256,384]{2,1,0:T(8,128)(2,1)}, bf16[24,256,384]{2,1,0:T(8,128)(2,1)}, u32[]{:S(2)}, u32[]{:S(2)}) collective-permute-start(bf16[24,256,384]{2,1,0:T(8,128)(2,1)} %get-tuple-element.47.raw.own), channel_id=1, source_target_pairs={{0,4},{4,0},{8,12},{12,8},{16,20},{20,16},{24,28},{28,24},{1,5},{5... | collective-permute-start | bytes 14155784 | tf_op jit(solution)/shard_map/cond/branch_1_fun/ppermute | solution.py:86
  6.2 37.5 %collective-permute-start.40 = (bf16[8,256,384]{2,1,0:T(8,128)(2,1)S(1)}, bf16[8,256,384]{2,1,0:T(8,128)(2,1)S(1)}, u32[]{:S(2)}, u32[]{:S(2)}) collective-permute-start(bf16[8,256,384]{2,1,0:T(8,128)(2,1)S(1)} %get-tuple-element.50), channel_id=1, source_target_pairs={{0,8},{4,12},{8,0},{12,4},{16,24},{20,28},{24,16},{28,20},{1,9},{5... | collective-permute-start | bytes 4718600 | tf_op jit(solution)/shard_map/cond/branch_1_fun/ppermute | solution.py:86
  8.7 36.4 %collective-permute-start.44 = (bf16[8,256,384]{2,1,0:T(8,128)(2,1)S(1)}, bf16[8,256,384]{2,1,0:T(8,128)(2,1)S(1)}, u32[]{:S(2)}, u32[]{:S(2)}) collective-permute-start(bf16[8,256,384]{2,1,0:T(8,128)(2,1)S(1)} %get-tuple-element.51), channel_id=1, source_target_pairs={{0,16},{4,20},{8,24},{12,28},{16,0},{20,4},{24,8},{28,12},{1,17},{... | collective-permute-start | bytes 4718600 | tf_op jit(solution)/shard_map/cond/branch_1_fun/ppermute | solution.py:86
  43.7 9.7 %collective-permute-start.41 = (bf16[8,256,384]{2,1,0:T(8,128)(2,1)S(1)}, bf16[8,256,384]{2,1,0:T(8,128)(2,1)}, u32[]{:S(2)}, u32[]{:S(2)}) collective-permute-start(bf16[8,256,384]{2,1,0:T(8,128)(2,1)S(1)} %collective-permute-done.40.near.refs_4_), channel_id=1, source_target_pairs={{0,4},{4,0},{8,12},{12,8},{16,20},{20,16},{24,28},{28,24},{1,5},{5... | collective-permute-start | bytes 4718600 | tf_op jit(solution)/shard_map/cond/branch_1_fun/ppermute | solution.py:86
  45.2 11.9 %collective-permute-start.45 = (bf16[8,256,384]{2,1,0:T(8,128)(2,1)S(1)}, bf16[8,256,384]{2,1,0:T(8,128)(2,1)}, u32[]{:S(2)}, u32[]{:S(2)}) collective-permute-start(bf16[8,256,384]{2,1,0:T(8,128)(2,1)S(1)} %collective-permute-done.44.near.refs_7_), channel_id=1, source_target_pairs={{0,4},{4,0},{8,12},{12,8},{16,20},{20,16},{24,28},{28,24},{1,5},{5... | collective-permute-start | bytes 4718600 | tf_op jit(solution)/shard_map/cond/branch_1_fun/ppermute | solution.py:86
  48.5 12.1 %collective-permute-start.24 = (f32[12,256]{1,0:T(8,128)S(1)}, f32[12,256]{1,0:T(8,128)S(1)}, u32[]{:S(2)}, u32[]{:S(2)}) collective-permute-start(f32[12,256]{1,0:T(8,128)S(1)} %get-tuple-element.125), channel_id=1, source_target_pairs={{0,1},{1,2},{2,3},{4,5},{5,6},{6,7},{8,9},{9,10},{10,11},{12,13},{... | collective-permute-start | bytes 36872 | tf_op jit(solution)/shard_map/cond/branch_1_fun/ppermute | solution.py:26
  52.0 8.6 %collective-permute-start.25 = (f32[12,256]{1,0:T(8,128)S(1)}, f32[12,256]{1,0:T(8,128)S(1)}, u32[]{:S(2)}, u32[]{:S(2)}) collective-permute-start(f32[12,256]{1,0:T(8,128)S(1)} %get-tuple-element.126), channel_id=1, source_target_pairs={{1,0},{2,1},{3,2},{5,4},{6,5},{7,6},{9,8},{10,9},{11,10},{13,12},{... | collective-permute-start | bytes 36872 | tf_op jit(solution)/shard_map/cond/branch_1_fun/ppermute | solution.py:28
  55.8 74.1 %collective-permute-start.42 = (bf16[3,4,256,384]{3,2,1,0:T(8,128)(2,1)S(1)}, bf16[3,4,256,384]{3,2,1,0:T(8,128)(2,1)S(1)}, u32[]{:S(2)}, u32[]{:S(2)}) collective-permute-start(bf16[3,4,256,384]{3,2,1,0:T(8,128)(2,1)S(1)} %send.18), channel_id=1, source_target_pairs={{0,16},{4,20},{8,24},{12,28},{16,0},{20,4},{24,8},{28,12},{1,17},{... | collective-permute-start | bytes 7077896 | tf_op jit(solution)/shard_map/cond/branch_1_fun/ppermute | solution.py:86
  59.5 70.5 %collective-permute-start.46 = (bf16[3,4,256,384]{3,2,1,0:T(8,128)(2,1)S(1)}, bf16[3,4,256,384]{3,2,1,0:T(8,128)(2,1)S(1)}, u32[]{:S(2)}, u32[]{:S(2)}) collective-permute-start(bf16[3,4,256,384]{3,2,1,0:T(8,128)(2,1)S(1)} %send.19), channel_id=1, source_target_pairs={{0,8},{4,12},{8,0},{12,4},{16,24},{20,28},{24,16},{28,20},{1,9},{5... | collective-permute-start | bytes 7077896 | tf_op jit(solution)/shard_map/cond/branch_1_fun/ppermute | solution.py:86
  62.8 66.6 %collective-permute-start.27 = (bf16[4,256,384]{2,1,0:T(8,128)(2,1)S(1)}, bf16[4,256,384]{2,1,0:T(8,128)(2,1)S(1)}, u32[]{:S(2)}, u32[]{:S(2)}) collective-permute-start(bf16[4,256,384]{2,1,0:T(8,128)(2,1)S(1)} %get-tuple-element.124), channel_id=1, source_target_pairs={{0,8},{4,12},{8,0},{12,4},{16,24},{20,28},{24,16},{28,20},{1,9},{5... | collective-permute-start | bytes 2359304 | tf_op jit(solution)/shard_map/cond/branch_1_fun/ppermute | solution.py:86
  63.9 67.8 %collective-permute-start.26 = (bf16[8,256,384]{2,1,0:T(8,128)(2,1)S(1)}, bf16[8,256,384]{2,1,0:T(8,128)(2,1)S(1)}, u32[]{:S(2)}, u32[]{:S(2)}) collective-permute-start(bf16[8,256,384]{2,1,0:T(8,128)(2,1)S(1)} %multiply_convert_fusion.1.own), channel_id=1, source_target_pairs={{0,4},{4,0},{8,12},{12,8},{16,20},{20,16},{24,28},{28,24},{1,5},{5... | collective-permute-start | bytes 4718600 | tf_op jit(solution)/shard_map/cond/branch_1_fun/ppermute | solution.py:86
  63.9 65.6 %collective-permute-start.31 = (bf16[4,256,384]{2,1,0:T(8,128)(2,1)S(1)}, bf16[4,256,384]{2,1,0:T(8,128)(2,1)S(1)}, u32[]{:S(2)}, u32[]{:S(2)}) collective-permute-start(bf16[4,256,384]{2,1,0:T(8,128)(2,1)S(1)} %get-tuple-element.123), channel_id=1, source_target_pairs={{0,16},{4,20},{8,24},{12,28},{16,0},{20,4},{24,8},{28,12},{1,17},{... | collective-permute-start | bytes 2359304 | tf_op jit(solution)/shard_map/cond/branch_1_fun/ppermute | solution.py:86
  129.4 2.3 %collective-permute-start.28 = (bf16[4,256,384]{2,1,0:T(8,128)(2,1)S(1)}, bf16[4,256,384]{2,1,0:T(8,128)(2,1)S(1)}, u32[]{:S(2)}, u32[]{:S(2)}) collective-permute-start(bf16[4,256,384]{2,1,0:T(8,128)(2,1)S(1)} %collective-permute-done.27.near.refs_3_), channel_id=1, source_target_pairs={{0,4},{4,0},{8,12},{12,8},{16,20},{20,16},{24,28},{28,24},{1,5},{5... | collective-permute-start | bytes 2359304 | tf_op jit(solution)/shard_map/cond/branch_1_fun/ppermute | solution.py:86
  129.5 4.9 %collective-permute-start.32 = (bf16[4,256,384]{2,1,0:T(8,128)(2,1)S(1)}, bf16[4,256,384]{2,1,0:T(8,128)(2,1)S(1)}, u32[]{:S(2)}, u32[]{:S(2)}) collective-permute-start(bf16[4,256,384]{2,1,0:T(8,128)(2,1)S(1)} %collective-permute-done.31.near.refs_6_), channel_id=1, source_target_pairs={{0,4},{4,0},{8,12},{12,8},{16,20},{20,16},{24,28},{28,24},{1,5},{5... | collective-permute-start | bytes 2359304 | tf_op jit(solution)/shard_map/cond/branch_1_fun/ppermute | solution.py:86
  130.0 67.6 %collective-permute-start.43 = (bf16[3,4,256,384]{3,2,1,0:T(8,128)(2,1)S(1)}, bf16[3,4,256,384]{3,2,1,0:T(8,128)(2,1)S(1)}, u32[]{:S(2)}, u32[]{:S(2)}) collective-permute-start(bf16[3,4,256,384]{3,2,1,0:T(8,128)(2,1)S(1)} %collective-permute-done.42.refs_6_), channel_id=1, source_target_pairs={{0,4},{4,0},{8,12},{12,8},{16,20},{20,16},{24,28},{28,24},{1,5},{5... | collective-permute-start | bytes 7077896 | tf_op jit(solution)/shard_map/cond/branch_1_fun/ppermute | solution.py:86
  130.0 69.0 %collective-permute-start.47 = (bf16[3,4,256,384]{3,2,1,0:T(8,128)(2,1)S(1)}, bf16[3,4,256,384]{3,2,1,0:T(8,128)(2,1)}, u32[]{:S(2)}, u32[]{:S(2)}) collective-permute-start(bf16[3,4,256,384]{3,2,1,0:T(8,128)(2,1)S(1)} %collective-permute-done.46.refs_9_), channel_id=1, source_target_pairs={{0,4},{4,0},{8,12},{12,8},{16,20},{20,16},{24,28},{28,24},{1,5},{5... | collective-permute-start | bytes 7077896 | tf_op jit(solution)/shard_map/cond/branch_1_fun/ppermute | solution.py:86
  133.6 28.2 %collective-permute-start.29 = (bf16[3,2,256,384]{3,2,1,0:T(8,128)(2,1)S(1)}, bf16[3,2,256,384]{3,2,1,0:T(8,128)(2,1)}, u32[]{:S(2)}, u32[]{:S(2)}) collective-permute-start(bf16[3,2,256,384]{3,2,1,0:T(8,128)(2,1)S(1)} %send.16), channel_id=1, source_target_pairs={{0,16},{4,20},{8,24},{12,28},{16,0},{20,4},{24,8},{28,12},{1,17},{... | collective-permute-start | bytes 3538952 | tf_op jit(solution)/shard_map/cond/branch_1_fun/ppermute | solution.py:86
  136.1 27.9 %collective-permute-start.33 = (bf16[3,2,256,384]{3,2,1,0:T(8,128)(2,1)S(1)}, bf16[3,2,256,384]{3,2,1,0:T(8,128)(2,1)}, u32[]{:S(2)}, u32[]{:S(2)}) collective-permute-start(bf16[3,2,256,384]{3,2,1,0:T(8,128)(2,1)S(1)} %send.17), channel_id=1, source_target_pairs={{0,8},{4,12},{8,0},{12,4},{16,24},{20,28},{24,16},{28,20},{1,9},{5... | collective-permute-start | bytes 3538952 | tf_op jit(solution)/shard_map/cond/branch_1_fun/ppermute | solution.py:86
  136.8 38.8 %collective-permute-start.36 = (f32[24,256]{1,0:T(8,128)S(1)}, f32[24,256]{1,0:T(8,128)S(1)}, u32[]{:S(2)}, u32[]{:S(2)}) collective-permute-start(f32[24,256]{1,0:T(8,128)S(1)} %get-tuple-element.78.scale), channel_id=1, source_target_pairs={{0,4},{4,0},{8,12},{12,8},{16,20},{20,16},{24,28},{28,24},{1,5},{5... | collective-permute-start | bytes 73736 | tf_op jit(solution)/shard_map/cond/branch_1_fun/ppermute | solution.py:86
  161.7 53.3 %collective-permute-start.30 = (bf16[3,2,256,384]{3,2,1,0:T(8,128)(2,1)}, bf16[3,2,256,384]{3,2,1,0:T(8,128)(2,1)}, u32[]{:S(2)}, u32[]{:S(2)}) collective-permute-start(bf16[3,2,256,384]{3,2,1,0:T(8,128)(2,1)} %collective-permute-done.29.refs_5_), channel_id=1, source_target_pairs={{0,4},{4,0},{8,12},{12,8},{16,20},{20,16},{24,28},{28,24},{1,5},{5... | collective-permute-start | bytes 3538952 | tf_op jit(solution)/shard_map/cond/branch_1_fun/ppermute | solution.py:86
  164.0 51.0 %collective-permute-start.34 = (bf16[3,2,256,384]{3,2,1,0:T(8,128)(2,1)}, bf16[3,2,256,384]{3,2,1,0:T(8,128)(2,1)}, u32[]{:S(2)}, u32[]{:S(2)}) collective-permute-start(bf16[3,2,256,384]{3,2,1,0:T(8,128)(2,1)} %collective-permute-done.33.refs_8_), channel_id=1, source_target_pairs={{0,4},{4,0},{8,12},{12,8},{16,20},{20,16},{24,28},{28,24},{1,5},{5... | collective-permute-start | bytes 3538952 | tf_op jit(solution)/shard_map/cond/branch_1_fun/ppermute | solution.py:86
  175.6 4.2 %collective-permute-start.37 = (f32[2,24,256]{2,1,0:T(8,128)S(1)}, f32[2,24,256]{2,1,0:T(8,128)S(1)}, u32[]{:S(2)}, u32[]{:S(2)}) collective-permute-start(f32[2,24,256]{2,1,0:T(8,128)S(1)} %pad_maximum_fusion.3), channel_id=1, source_target_pairs={{0,8},{4,12},{8,0},{12,4},{16,24},{20,28},{24,16},{28,20},{1,9},{5... | collective-permute-start | bytes 147464 | tf_op jit(solution)/shard_map/cond/branch_1_fun/ppermute | solution.py:86
  179.8 4.1 %collective-permute-start.38 = (f32[2,24,256]{2,1,0:T(8,128)S(1)}, f32[2,24,256]{2,1,0:T(8,128)S(1)}, u32[]{:S(2)}, u32[]{:S(2)}) collective-permute-start(f32[2,24,256]{2,1,0:T(8,128)S(1)} %pad_maximum_fusion.3), channel_id=1, source_target_pairs={{0,16},{4,20},{8,24},{12,28},{16,0},{20,4},{24,8},{28,12},{1,17},{... | collective-permute-start | bytes 147464 | tf_op jit(solution)/shard_map/cond/branch_1_fun/ppermute | solution.py:86
  183.9 5.0 %collective-permute-start.39 = (f32[2,24,256]{2,1,0:T(8,128)S(1)}, f32[2,24,256]{2,1,0:T(8,128)S(1)}, u32[]{:S(2)}, u32[]{:S(2)}) collective-permute-start(f32[2,24,256]{2,1,0:T(8,128)S(1)} %pad_maximum_fusion.3), channel_id=1, source_target_pairs={{0,24},{4,28},{8,16},{12,20},{16,8},{20,12},{24,0},{28,4},{1,25},{... | collective-permute-start | bytes 147464 | tf_op jit(solution)/shard_map/cond/branch_1_fun/ppermute | solution.py:86
  197.6 1.5 copy-start.5
  199.1 1.7 copy-start.6

commit v5 on v4

--- a/solution.py
+++ b/solution.py
@@ -221,8 +221,9 @@
         begin += piece.shape[0]
     for into, onto in copies:
         into.start()
-    route_kernel(devices, device_ref, partner_ref, out_ref, case_ref)
-    for into, onto in copies:
+    for n, (into, onto) in enumerate(copies):
+        if n == len(copies) // 2:
+            route_kernel(devices, device_ref, partner_ref, out_ref, case_ref)
         into.wait()
         onto.start()
     for into, onto in copies:
@@ -231,7 +232,7 @@
 
 def starts_of(device, partner, spectra, parts):
     chans, columns = spectra.shape[1:]
-    chunk = 2
+    chunk = 1
     count = 2 * sum(parts) // chunk
     anywhere = pl.BlockSpec(memory_space=pl.ANY)
     smem = pl.BlockSpec(memory_space=pltpu.SMEM)

time: 221 us -> 224 us (1.014)
  Pallas kernels: 50.9 us -> 54 us
    pallas_call x1, Pallas kernels: 4.07 us -> 7.1 us  [starts_of(): pl.pallas_call(functools.partial(start_kernel, partner.shape[1], chunk),...]
where the time goes in v5:
time: 224 us; the launch traced here: 223 us
  waiting for transfers between devices  139 us (62%)
  Pallas kernels  54 us (24%)
  starting transfers between devices  19 us (8%)
  other arithmetic  5.32 us (2%)
  local copies, waits for them, and re-layouts  4.52 us (2%)
    ppermute x22, waiting for transfers between devices, swap(): lax.ppermute(values, 'chan', [(i, i ^ offset) for i in range(lax.axis_siz...  139 us
    pallas_call x4, Pallas kernels, pair_products(): pl.pallas_call(lambda *refs: pair_kernel(parts, offset, which, raw, insid...  27.4 us
    ppermute x22, starting transfers between devices, swap(): lax.ppermute(values, 'chan', [(i, i ^ offset) for i in range(lax.axis_siz...  14.2 us
    pallas_call x1, Pallas kernels, own_products(): pl.pallas_call(own_kernel, out_shape=(jax.ShapeDtypeStruct((bins, 2 * cha...  11.2 us
    pallas_call x4, Pallas kernels, sends(): pl.pallas_call(functools.partial(send_kernel, side, start), out_shape=jax...  8.33 us
    pallas_call x1, Pallas kernels, starts_of(): pl.pallas_call(functools.partial(start_kernel, partner.shape[1], chunk),...  7.1 us
  transfers between devices with their start and end apart: 24, of which 9 were waited for; matrix products, arithmetic and copies ran while one was open for 3% of the time, Pallas kernels for 15%

profile of v5, /device:TPU:0, one launch (start us, length us, event | category | flops | bytes accessed | tf_op | source)
XLA Modules:
  0.0 223.2 jit_solution(15261860064321910172)
XLA Ops:
  0.0 0.7 copy-done.7
  0.7 7.1 %start.1 = (s32[24]{0:T(128)S(1)}, s32[1]{0:T(128)}, bf16[8,256,384]{2,1,0:T(8,128)(2,1)S(1)}, bf16[8,256,384]{2,1,0:T(8,128)(2,1)S(1)}) custom-call(s32[1]{0:T(128)} %bitcast.6.device_ref, s32[2,8]{1,0:T(2,128)S(1)} %copy-done.7, bf16[24,256,384]{2,1,0:T(8,128)(2,1)} %spectra.1), custom_call_target="tpu_custom_call" | custom-call | tf_op jit(solution)/shard_map/start/pallas_call | solution.py:239
  8.4 214.5 %conditional.1 = (bf16[3,24,256,512]{3,2,1,0:T(8,128)(2,1)}) conditional(s32[]{:T(128)} %bitcast.7, (bf16[24,256,384]{2,1,0:T(8,128)(2,1)}, s32[256]{0:T(256)S(1)}, s32[24]{0:T(128)S(1)}, bf16[8,256,384]{2,1,0:T(8,128)(2,1)S(1)}, bf16[8,256,384]{2,1,0:T(8,128)(2,1)S(1)}) %tuple.135, (bf16[24,256,384]{2,1,0:T(8,128)(2,1)}, ...), branch_computations={%region_0.0_spmd, %region_2.0_spmd, %region_4.0_spmd} | conditional | flops 7257975808 | bytes 286149952 | solution.py:570
  8.7 0.6 collective-permute-start.35
  9.2 2.6 %collective-permute-start.40 = (bf16[8,256,384]{2,1,0:T(8,128)(2,1)S(1)}, bf16[8,256,384]{2,1,0:T(8,128)(2,1)S(1)}, u32[]{:S(2)}, u32[]{:S(2)}) collective-permute-start(bf16[8,256,384]{2,1,0:T(8,128)(2,1)S(1)} %get-tuple-element.50), channel_id=1, source_target_pairs={{0,8},{4,12},{8,0},{12,4},{16,24},{20,28},{24,16},{28,20},{1,9},{5... | collective-permute-start | bytes 4718600 | tf_op jit(solution)/shard_map/cond/branch_1_fun/ppermute | solution.py:86
  11.8 1.5 collective-permute-start.44
  13.3 33.5 %collective-permute-done.40.near.refs_4_ = bf16[8,256,384]{2,1,0:T(8,128)(2,1)S(1)} collective-permute-done((bf16[8,256,384]{2,1,0:T(8,128)(2,1)S(1)}, bf16[8,256,384]{2,1,0:T(8,128)(2,1)S(1)}, u32[]{:S(2)}, u32[]{:S(2)}) %collective-permute-start.40) | collective-permute-done | bytes 1572896 | tf_op jit(solution)/shard_map/cond/branch_1_fun/ppermute | solution.py:86
  46.8 0.0 collective-permute-start.41
  46.8 1.5 collective-permute-done.44.near.refs_7_
  48.2 0.0 collective-permute-start.45
  48.2 3.3 %multiply_reduce_fusion.1 = f32[24,256]{1,0:T(8,128)S(1)} fusion(bf16[24,256,384]{2,1,0:T(8,128)(2,1)} %get-tuple-element.47.raw.own), kind=kLoop, calls=%fused_computation.141 | loop fusion | flops 7071744 | bytes 4743168 | tf_op jit(solution)/shard_map/cond/branch_1_fun/reduce_sum | solution.py:46
  51.6 3.5 %collective-permute-start.24 = (f32[12,256]{1,0:T(8,128)S(1)}, f32[12,256]{1,0:T(8,128)S(1)}, u32[]{:S(2)}, u32[]{:S(2)}) collective-permute-start(f32[12,256]{1,0:T(8,128)S(1)} %get-tuple-element.125), channel_id=1, source_target_pairs={{0,1},{1,2},{2,3},{4,5},{5,6},{6,7},{8,9},{9,10},{10,11},{12,13},{... | collective-permute-start | bytes 36872 | tf_op jit(solution)/shard_map/cond/branch_1_fun/ppermute | solution.py:26
  55.1 1.3 collective-permute-start.25
  56.4 0.1 fusion.228
  56.5 0.0 collective-permute-done.41.far.refs_5_
  56.5 0.0 collective-permute-done.35.sister.refs_2_
  56.5 2.3 %send.18 = bf16[3,4,256,384]{3,2,1,0:T(8,128)(2,1)S(1)} custom-call(s32[24]{0:T(128)S(1)} %get-tuple-element.46.route.refs_0_, bf16[24,256,384]{2,1,0:T(8,128)(2,1)} %get-tuple-element.47.raw.own, bf16[24,256,384]{2,1,0:T(8,128)(2,1)} %collective-permute-done.35.sister.refs_2_, bf16[8,256,384]{2,1,0:T(8,128)(2,1)S(1)} %collective-permute-done.40.near.refs_4_, ...), custom_call_target="tpu_custom_call" | custom-call | bytes 4718592 | tf_op jit(solution)/shard_map/cond/branch_1_fun/send/pallas_call | solution.py:287
  58.8 1.3 collective-permute-start.42
  60.1 0.0 collective-permute-done.45.far.refs_8_
  60.2 2.4 %send.19 = bf16[3,4,256,384]{3,2,1,0:T(8,128)(2,1)S(1)} custom-call(s32[24]{0:T(128)S(1)} %get-tuple-element.46.route.refs_0_, bf16[24,256,384]{2,1,0:T(8,128)(2,1)} %get-tuple-element.47.raw.own, bf16[24,256,384]{2,1,0:T(8,128)(2,1)} %collective-permute-done.35.sister.refs_2_, bf16[8,256,384]{2,1,0:T(8,128)(2,1)S(1)} %collective-permute-done.44.near.refs_7_, ...), custom_call_target="tpu_custom_call" | custom-call | bytes 4718592 | tf_op jit(solution)/shard_map/cond/branch_1_fun/send/pallas_call | solution.py:287
  62.5 1.1 collective-permute-start.46
  63.6 0.1 fusion.229
  63.7 0.2 constant_dynamic-update-slice_fusion.9
  63.9 1.8 multiply_convert_fusion.1.own
  65.7 0.2 fusion.226
  65.8 1.1 collective-permute-start.27
  66.9 0.0 collective-permute-start.26
  66.9 0.5 collective-permute-start.31
  67.4 65.1 %collective-permute-done.27.near.refs_3_ = bf16[4,256,384]{2,1,0:T(8,128)(2,1)S(1)} collective-permute-done((bf16[4,256,384]{2,1,0:T(8,128)(2,1)S(1)}, bf16[4,256,384]{2,1,0:T(8,128)(2,1)S(1)}, u32[]{:S(2)}, u32[]{:S(2)}) %collective-permute-start.27) | collective-permute-done | bytes 786464 | tf_op jit(solution)/shard_map/cond/branch_1_fun/ppermute | solution.py:86
  132.5 0.0 collective-permute-start.28
  132.5 0.0 collective-permute-done.31.near.refs_6_
  132.5 0.5 collective-permute-start.32
  133.0 0.0 collective-permute-done.42.refs_6_
  133.0 0.1 collective-permute-start.43
  133.1 0.0 collective-permute-done.46.refs_9_
  133.1 0.4 collective-permute-start.47
  133.5 1.3 collective-permute-done.28.far.refs_4_
  134.8 0.0 collective-permute-done.26.sister.refs_2_
  134.8 1.8 send.16
  136.6 0.8 collective-permute-start.29
  137.4 1.8 send.17
  139.2 0.6 collective-permute-start.33
  139.8 0.0 collective-permute-start.36
  139.8 25.0 %collective-permute-done.29.refs_5_ = bf16[3,2,256,384]{3,2,1,0:T(8,128)(2,1)} collective-permute-done((bf16[3,2,256,384]{3,2,1,0:T(8,128)(2,1)S(1)}, bf16[3,2,256,384]{3,2,1,0:T(8,128)(2,1)}, u32[]{:S(2)}, u32[]{:S(2)}) %collective-permute-start.29) | collective-permute-done | bytes 1179680 | tf_op jit(solution)/shard_map/cond/branch_1_fun/ppermute | solution.py:86
  164.8 0.0 collective-permute-start.30
  164.8 2.3 %collective-permute-done.33.refs_8_ = bf16[3,2,256,384]{3,2,1,0:T(8,128)(2,1)} collective-permute-done((bf16[3,2,256,384]{3,2,1,0:T(8,128)(2,1)S(1)}, bf16[3,2,256,384]{3,2,1,0:T(8,128)(2,1)}, u32[]{:S(2)}, u32[]{:S(2)}) %collective-permute-start.33) | collective-permute-done | bytes 1179680 | tf_op jit(solution)/shard_map/cond/branch_1_fun/ppermute | solution.py:86
  167.1 11.2 %own_products.4 = (bf16[24,512,384]{2,1,0:T(8,128)(2,1)S(1)}, bf16[3,24,256,512]{3,2,1,0:T(8,128)(2,1)}) custom-call(bf16[24,256,384]{2,1,0:T(8,128)(2,1)} %get-tuple-element.47.raw.own, f32[24,256]{1,0:T(8,128)S(1)} %get-tuple-element.78.scale), custom_call_target="tpu_custom_call" | custom-call | flops 2415919104 | bytes 20447232 | tf_op jit(solution)/shard_map/cond/branch_1_fun/own_products/pallas_call | solution.py:184
  178.2 0.3 slice.590.refs_1_
  178.6 0.0 collective-permute-done.36
  178.6 0.6 collective-permute-start.37
  179.2 3.6 %collective-permute-done.37 = f32[2,24,256]{2,1,0:T(8,128)S(1)} collective-permute-done((f32[2,24,256]{2,1,0:T(8,128)S(1)}, f32[2,24,256]{2,1,0:T(8,128)S(1)}, u32[]{:S(2)}, u32[]{:S(2)}) %collective-permute-start.37) | collective-permute-done | bytes 49184 | tf_op jit(solution)/shard_map/cond/branch_1_fun/ppermute | solution.py:86
  182.8 1.3 collective-permute-start.38
  184.1 2.8 %collective-permute-done.38 = f32[2,24,256]{2,1,0:T(8,128)S(1)} collective-permute-done((f32[2,24,256]{2,1,0:T(8,128)S(1)}, f32[2,24,256]{2,1,0:T(8,128)S(1)}, u32[]{:S(2)}, u32[]{:S(2)}) %collective-permute-start.38) | collective-permute-done | bytes 49184 | tf_op jit(solution)/shard_map/cond/branch_1_fun/ppermute | solution.py:86
  186.9 1.3 collective-permute-start.39
  188.2 3.7 %collective-permute-done.39 = f32[2,24,256]{2,1,0:T(8,128)S(1)} collective-permute-done((f32[2,24,256]{2,1,0:T(8,128)S(1)}, f32[2,24,256]{2,1,0:T(8,128)S(1)}, u32[]{:S(2)}, u32[]{:S(2)}) %collective-permute-start.39) | collective-permute-done | bytes 49184 | tf_op jit(solution)/shard_map/cond/branch_1_fun/ppermute | solution.py:86
  191.9 8.7 %branch_1_fun.4.refs_10_ = bf16[3,24,256,512]{3,2,1,0:T(8,128)(2,1)} custom-call(s32[24]{0:T(128)S(1)} %get-tuple-element.46.route.refs_0_, bf16[24,512,384]{2,1,0:T(8,128)(2,1)S(1)} %get-tuple-element.49.refs_1_, bf16[24,256,384]{2,1,0:T(8,128)(2,1)} %collective-permute-done.35.sister.refs_2_, ...), custom_call_target="tpu_custom_call", output_to_operand_aliasing={{}: (10, {})} | custom-call | flops 1610612736 | bytes 10485760 | tf_op jit(solution)/shard_map/cond/branch_1_fun/pallas_call | solution.py:458
  200.6 0.0 collective-permute-done.43.refs_6_
  200.6 1.5 copy-done.5
  202.1 1.7 copy-done.6
  203.8 9.8 %branch_1_fun.5.refs_9_ = bf16[3,24,256,512]{3,2,1,0:T(8,128)(2,1)} custom-call(s32[24]{0:T(128)S(1)} %get-tuple-element.46.route.refs_0_, bf16[24,512,384]{2,1,0:T(8,128)(2,1)S(1)} %get-tuple-element.49.refs_1_, bf16[24,256,384]{2,1,0:T(8,128)(2,1)} %collective-permute-done.35.sister.refs_2_, ...), custom_call_target="tpu_custom_call", output_to_operand_aliasing={{}: (10, {})} | custom-call | flops 1610612736 | bytes 10485760 | tf_op jit(solution)/shard_map/cond/branch_1_fun/pallas_call | solution.py:458
  213.6 4.4 %branch_1_fun.6.refs_9_ = bf16[3,24,256,512]{3,2,1,0:T(8,128)(2,1)} custom-call(s32[24]{0:T(128)S(1)} %get-tuple-element.46.route.refs_0_, bf16[8,512,384]{2,1,0:T(8,128)(2,1)S(1)} %slice.590.refs_1_, bf16[8,256,384]{2,1,0:T(8,128)(2,1)S(1)} %collective-permute-done.26.sister.refs_2_, ...), custom_call_target="tpu_custom_call", output_to_operand_aliasing={{}: (9, {})} | custom-call | flops 805306368 | bytes 5242880 | tf_op jit(solution)/shard_map/cond/branch_1_fun/pallas_call | solution.py:458
  218.0 0.0 collective-permute-done.30.refs_5_
  218.1 0.0 collective-permute-done.34.refs_8_
  218.1 4.4 %branch_1_fun.7 = bf16[3,24,256,512]{3,2,1,0:T(8,128)(2,1)} custom-call(s32[24]{0:T(128)S(1)} %get-tuple-element.46.route.refs_0_, bf16[8,512,384]{2,1,0:T(8,128)(2,1)S(1)} %slice.590.refs_1_, bf16[8,256,384]{2,1,0:T(8,128)(2,1)S(1)} %collective-permute-done.26.sister.refs_2_, ...), custom_call_target="tpu_custom_call", output_to_operand_aliasing={{}: (9, {})} | custom-call | flops 805306368 | bytes 5242880 | tf_op jit(solution)/shard_map/cond/branch_1_fun/pallas_call | solution.py:458
  (19 shorter events, 0.1 us)
Async XLA Ops:
  0.0 8.4 %copy-start.8 = (s32[256]{0:T(256)S(1)}, s32[256]{0:T(256)}, u32[]{:S(2)}) copy-start(s32[256]{0:T(256)} %param.7) | copy-start | bytes 3076
  0.0 0.7 copy-start.7
  8.7 47.9 %collective-permute-start.35 = (bf16[24,256,384]{2,1,0:T(8,128)(2,1)}, bf16[24,256,384]{2,1,0:T(8,128)(2,1)}, u32[]{:S(2)}, u32[]{:S(2)}) collective-permute-start(bf16[24,256,384]{2,1,0:T(8,128)(2,1)} %get-tuple-element.47.raw.own), channel_id=1, source_target_pairs={{0,4},{4,0},{8,12},{12,8},{16,20},{20,16},{24,28},{28,24},{1,5},{5... | collective-permute-start | bytes 14155784 | tf_op jit(solution)/shard_map/cond/branch_1_fun/ppermute | solution.py:86
  9.2 37.5 %collective-permute-start.40 = (bf16[8,256,384]{2,1,0:T(8,128)(2,1)S(1)}, bf16[8,256,384]{2,1,0:T(8,128)(2,1)S(1)}, u32[]{:S(2)}, u32[]{:S(2)}) collective-permute-start(bf16[8,256,384]{2,1,0:T(8,128)(2,1)S(1)} %get-tuple-element.50), channel_id=1, source_target_pairs={{0,8},{4,12},{8,0},{12,4},{16,24},{20,28},{24,16},{28,20},{1,9},{5... | collective-permute-start | bytes 4718600 | tf_op jit(solution)/shard_map/cond/branch_1_fun/ppermute | solution.py:86
  11.8 36.4 %collective-permute-start.44 = (bf16[8,256,384]{2,1,0:T(8,128)(2,1)S(1)}, bf16[8,256,384]{2,1,0:T(8,128)(2,1)S(1)}, u32[]{:S(2)}, u32[]{:S(2)}) collective-permute-start(bf16[8,256,384]{2,1,0:T(8,128)(2,1)S(1)} %get-tuple-element.51), channel_id=1, source_target_pairs={{0,16},{4,20},{8,24},{12,28},{16,0},{20,4},{24,8},{28,12},{1,17},{... | collective-permute-start | bytes 4718600 | tf_op jit(solution)/shard_map/cond/branch_1_fun/ppermute | solution.py:86
  46.8 9.7 %collective-permute-start.41 = (bf16[8,256,384]{2,1,0:T(8,128)(2,1)S(1)}, bf16[8,256,384]{2,1,0:T(8,128)(2,1)}, u32[]{:S(2)}, u32[]{:S(2)}) collective-permute-start(bf16[8,256,384]{2,1,0:T(8,128)(2,1)S(1)} %collective-permute-done.40.near.refs_4_), channel_id=1, source_target_pairs={{0,4},{4,0},{8,12},{12,8},{16,20},{20,16},{24,28},{28,24},{1,5},{5... | collective-permute-start | bytes 4718600 | tf_op jit(solution)/shard_map/cond/branch_1_fun/ppermute | solution.py:86
  48.2 11.9 %collective-permute-start.45 = (bf16[8,256,384]{2,1,0:T(8,128)(2,1)S(1)}, bf16[8,256,384]{2,1,0:T(8,128)(2,1)}, u32[]{:S(2)}, u32[]{:S(2)}) collective-permute-start(bf16[8,256,384]{2,1,0:T(8,128)(2,1)S(1)} %collective-permute-done.44.near.refs_7_), channel_id=1, source_target_pairs={{0,4},{4,0},{8,12},{12,8},{16,20},{20,16},{24,28},{28,24},{1,5},{5... | collective-permute-start | bytes 4718600 | tf_op jit(solution)/shard_map/cond/branch_1_fun/ppermute | solution.py:86
  51.6 12.1 %collective-permute-start.24 = (f32[12,256]{1,0:T(8,128)S(1)}, f32[12,256]{1,0:T(8,128)S(1)}, u32[]{:S(2)}, u32[]{:S(2)}) collective-permute-start(f32[12,256]{1,0:T(8,128)S(1)} %get-tuple-element.125), channel_id=1, source_target_pairs={{0,1},{1,2},{2,3},{4,5},{5,6},{6,7},{8,9},{9,10},{10,11},{12,13},{... | collective-permute-start | bytes 36872 | tf_op jit(solution)/shard_map/cond/branch_1_fun/ppermute | solution.py:26
  55.1 8.6 %collective-permute-start.25 = (f32[12,256]{1,0:T(8,128)S(1)}, f32[12,256]{1,0:T(8,128)S(1)}, u32[]{:S(2)}, u32[]{:S(2)}) collective-permute-start(f32[12,256]{1,0:T(8,128)S(1)} %get-tuple-element.126), channel_id=1, source_target_pairs={{1,0},{2,1},{3,2},{5,4},{6,5},{7,6},{9,8},{10,9},{11,10},{13,12},{... | collective-permute-start | bytes 36872 | tf_op jit(solution)/shard_map/cond/branch_1_fun/ppermute | solution.py:28
  58.8 74.1 %collective-permute-start.42 = (bf16[3,4,256,384]{3,2,1,0:T(8,128)(2,1)S(1)}, bf16[3,4,256,384]{3,2,1,0:T(8,128)(2,1)S(1)}, u32[]{:S(2)}, u32[]{:S(2)}) collective-permute-start(bf16[3,4,256,384]{3,2,1,0:T(8,128)(2,1)S(1)} %send.18), channel_id=1, source_target_pairs={{0,16},{4,20},{8,24},{12,28},{16,0},{20,4},{24,8},{28,12},{1,17},{... | collective-permute-start | bytes 7077896 | tf_op jit(solution)/shard_map/cond/branch_1_fun/ppermute | solution.py:86
  62.5 70.5 %collective-permute-start.46 = (bf16[3,4,256,384]{3,2,1,0:T(8,128)(2,1)S(1)}, bf16[3,4,256,384]{3,2,1,0:T(8,128)(2,1)S(1)}, u32[]{:S(2)}, u32[]{:S(2)}) collective-permute-start(bf16[3,4,256,384]{3,2,1,0:T(8,128)(2,1)S(1)} %send.19), channel_id=1, source_target_pairs={{0,8},{4,12},{8,0},{12,4},{16,24},{20,28},{24,16},{28,20},{1,9},{5... | collective-permute-start | bytes 7077896 | tf_op jit(solution)/shard_map/cond/branch_1_fun/ppermute | solution.py:86
  65.8 66.6 %collective-permute-start.27 = (bf16[4,256,384]{2,1,0:T(8,128)(2,1)S(1)}, bf16[4,256,384]{2,1,0:T(8,128)(2,1)S(1)}, u32[]{:S(2)}, u32[]{:S(2)}) collective-permute-start(bf16[4,256,384]{2,1,0:T(8,128)(2,1)S(1)} %get-tuple-element.124), channel_id=1, source_target_pairs={{0,8},{4,12},{8,0},{12,4},{16,24},{20,28},{24,16},{28,20},{1,9},{5... | collective-permute-start | bytes 2359304 | tf_op jit(solution)/shard_map/cond/branch_1_fun/ppermute | solution.py:86
  66.9 67.8 %collective-permute-start.26 = (bf16[8,256,384]{2,1,0:T(8,128)(2,1)S(1)}, bf16[8,256,384]{2,1,0:T(8,128)(2,1)S(1)}, u32[]{:S(2)}, u32[]{:S(2)}) collective-permute-start(bf16[8,256,384]{2,1,0:T(8,128)(2,1)S(1)} %multiply_convert_fusion.1.own), channel_id=1, source_target_pairs={{0,4},{4,0},{8,12},{12,8},{16,20},{20,16},{24,28},{28,24},{1,5},{5... | collective-permute-start | bytes 4718600 | tf_op jit(solution)/shard_map/cond/branch_1_fun/ppermute | solution.py:86
  66.9 65.6 %collective-permute-start.31 = (bf16[4,256,384]{2,1,0:T(8,128)(2,1)S(1)}, bf16[4,256,384]{2,1,0:T(8,128)(2,1)S(1)}, u32[]{:S(2)}, u32[]{:S(2)}) collective-permute-start(bf16[4,256,384]{2,1,0:T(8,128)(2,1)S(1)} %get-tuple-element.123), channel_id=1, source_target_pairs={{0,16},{4,20},{8,24},{12,28},{16,0},{20,4},{24,8},{28,12},{1,17},{... | collective-permute-start | bytes 2359304 | tf_op jit(solution)/shard_map/cond/branch_1_fun/ppermute | solution.py:86
  132.5 2.3 %collective-permute-start.28 = (bf16[4,256,384]{2,1,0:T(8,128)(2,1)S(1)}, bf16[4,256,384]{2,1,0:T(8,128)(2,1)S(1)}, u32[]{:S(2)}, u32[]{:S(2)}) collective-permute-start(bf16[4,256,384]{2,1,0:T(8,128)(2,1)S(1)} %collective-permute-done.27.near.refs_3_), channel_id=1, source_target_pairs={{0,4},{4,0},{8,12},{12,8},{16,20},{20,16},{24,28},{28,24},{1,5},{5... | collective-permute-start | bytes 2359304 | tf_op jit(solution)/shard_map/cond/branch_1_fun/ppermute | solution.py:86
  132.5 4.9 %collective-permute-start.32 = (bf16[4,256,384]{2,1,0:T(8,128)(2,1)S(1)}, bf16[4,256,384]{2,1,0:T(8,128)(2,1)S(1)}, u32[]{:S(2)}, u32[]{:S(2)}) collective-permute-start(bf16[4,256,384]{2,1,0:T(8,128)(2,1)S(1)} %collective-permute-done.31.near.refs_6_), channel_id=1, source_target_pairs={{0,4},{4,0},{8,12},{12,8},{16,20},{20,16},{24,28},{28,24},{1,5},{5... | collective-permute-start | bytes 2359304 | tf_op jit(solution)/shard_map/cond/branch_1_fun/ppermute | solution.py:86
  133.0 67.6 %collective-permute-start.43 = (bf16[3,4,256,384]{3,2,1,0:T(8,128)(2,1)S(1)}, bf16[3,4,256,384]{3,2,1,0:T(8,128)(2,1)S(1)}, u32[]{:S(2)}, u32[]{:S(2)}) collective-permute-start(bf16[3,4,256,384]{3,2,1,0:T(8,128)(2,1)S(1)} %collective-permute-done.42.refs_6_), channel_id=1, source_target_pairs={{0,4},{4,0},{8,12},{12,8},{16,20},{20,16},{24,28},{28,24},{1,5},{5... | collective-permute-start | bytes 7077896 | tf_op jit(solution)/shard_map/cond/branch_1_fun/ppermute | solution.py:86
  133.1 69.0 %collective-permute-start.47 = (bf16[3,4,256,384]{3,2,1,0:T(8,128)(2,1)S(1)}, bf16[3,4,256,384]{3,2,1,0:T(8,128)(2,1)}, u32[]{:S(2)}, u32[]{:S(2)}) collective-permute-start(bf16[3,4,256,384]{3,2,1,0:T(8,128)(2,1)S(1)} %collective-permute-done.46.refs_9_), channel_id=1, source_target_pairs={{0,4},{4,0},{8,12},{12,8},{16,20},{20,16},{24,28},{28,24},{1,5},{5... | collective-permute-start | bytes 7077896 | tf_op jit(solution)/shard_map/cond/branch_1_fun/ppermute | solution.py:86
  136.6 28.2 %collective-permute-start.29 = (bf16[3,2,256,384]{3,2,1,0:T(8,128)(2,1)S(1)}, bf16[3,2,256,384]{3,2,1,0:T(8,128)(2,1)}, u32[]{:S(2)}, u32[]{:S(2)}) collective-permute-start(bf16[3,2,256,384]{3,2,1,0:T(8,128)(2,1)S(1)} %send.16), channel_id=1, source_target_pairs={{0,16},{4,20},{8,24},{12,28},{16,0},{20,4},{24,8},{28,12},{1,17},{... | collective-permute-start | bytes 3538952 | tf_op jit(solution)/shard_map/cond/branch_1_fun/ppermute | solution.py:86
  139.2 27.9 %collective-permute-start.33 = (bf16[3,2,256,384]{3,2,1,0:T(8,128)(2,1)S(1)}, bf16[3,2,256,384]{3,2,1,0:T(8,128)(2,1)}, u32[]{:S(2)}, u32[]{:S(2)}) collective-permute-start(bf16[3,2,256,384]{3,2,1,0:T(8,128)(2,1)S(1)} %send.17), channel_id=1, source_target_pairs={{0,8},{4,12},{8,0},{12,4},{16,24},{20,28},{24,16},{28,20},{1,9},{5... | collective-permute-start | bytes 3538952 | tf_op jit(solution)/shard_map/cond/branch_1_fun/ppermute | solution.py:86
  139.8 38.8 %collective-permute-start.36 = (f32[24,256]{1,0:T(8,128)S(1)}, f32[24,256]{1,0:T(8,128)S(1)}, u32[]{:S(2)}, u32[]{:S(2)}) collective-permute-start(f32[24,256]{1,0:T(8,128)S(1)} %get-tuple-element.78.scale), channel_id=1, source_target_pairs={{0,4},{4,0},{8,12},{12,8},{16,20},{20,16},{24,28},{28,24},{1,5},{5... | collective-permute-start | bytes 73736 | tf_op jit(solution)/shard_map/cond/branch_1_fun/ppermute | solution.py:86
  164.8 53.3 %collective-permute-start.30 = (bf16[3,2,256,384]{3,2,1,0:T(8,128)(2,1)}, bf16[3,2,256,384]{3,2,1,0:T(8,128)(2,1)}, u32[]{:S(2)}, u32[]{:S(2)}) collective-permute-start(bf16[3,2,256,384]{3,2,1,0:T(8,128)(2,1)} %collective-permute-done.29.refs_5_), channel_id=1, source_target_pairs={{0,4},{4,0},{8,12},{12,8},{16,20},{20,16},{24,28},{28,24},{1,5},{5... | collective-permute-start | bytes 3538952 | tf_op jit(solution)/shard_map/cond/branch_1_fun/ppermute | solution.py:86
  167.1 51.0 %collective-permute-start.34 = (bf16[3,2,256,384]{3,2,1,0:T(8,128)(2,1)}, bf16[3,2,256,384]{3,2,1,0:T(8,128)(2,1)}, u32[]{:S(2)}, u32[]{:S(2)}) collective-permute-start(bf16[3,2,256,384]{3,2,1,0:T(8,128)(2,1)} %collective-permute-done.33.refs_8_), channel_id=1, source_target_pairs={{0,4},{4,0},{8,12},{12,8},{16,20},{20,16},{24,28},{28,24},{1,5},{5... | collective-permute-start | bytes 3538952 | tf_op jit(solution)/shard_map/cond/branch_1_fun/ppermute | solution.py:86
  178.6 4.2 %collective-permute-start.37 = (f32[2,24,256]{2,1,0:T(8,128)S(1)}, f32[2,24,256]{2,1,0:T(8,128)S(1)}, u32[]{:S(2)}, u32[]{:S(2)}) collective-permute-start(f32[2,24,256]{2,1,0:T(8,128)S(1)} %pad_maximum_fusion.3), channel_id=1, source_target_pairs={{0,8},{4,12},{8,0},{12,4},{16,24},{20,28},{24,16},{28,20},{1,9},{5... | collective-permute-start | bytes 147464 | tf_op jit(solution)/shard_map/cond/branch_1_fun/ppermute | solution.py:86
  182.8 4.1 %collective-permute-start.38 = (f32[2,24,256]{2,1,0:T(8,128)S(1)}, f32[2,24,256]{2,1,0:T(8,128)S(1)}, u32[]{:S(2)}, u32[]{:S(2)}) collective-permute-start(f32[2,24,256]{2,1,0:T(8,128)S(1)} %pad_maximum_fusion.3), channel_id=1, source_target_pairs={{0,16},{4,20},{8,24},{12,28},{16,0},{20,4},{24,8},{28,12},{1,17},{... | collective-permute-start | bytes 147464 | tf_op jit(solution)/shard_map/cond/branch_1_fun/ppermute | solution.py:86
  186.9 5.0 %collective-permute-start.39 = (f32[2,24,256]{2,1,0:T(8,128)S(1)}, f32[2,24,256]{2,1,0:T(8,128)S(1)}, u32[]{:S(2)}, u32[]{:S(2)}) collective-permute-start(f32[2,24,256]{2,1,0:T(8,128)S(1)} %pad_maximum_fusion.3), channel_id=1, source_target_pairs={{0,24},{4,28},{8,16},{12,20},{16,8},{20,12},{24,0},{28,4},{1,25},{... | collective-permute-start | bytes 147464 | tf_op jit(solution)/shard_map/cond/branch_1_fun/ppermute | solution.py:86
  200.6 1.5 copy-start.5
  202.1 1.7 copy-start.6
